TPU v7x, 32 devices: a whole 2x2x4 slice. The times are simulated.
32 devices in a mesh: dp: 8 (over z, x), mp: 4 (over y, core).
Axes of the slice: x: 2, y: 2, z: 4, core: 2. Of those that a mesh axis runs over, the one named last changes fastest.
Arguments:
- block_in: bfloat16 [16384, 1024], P('dp', 'mp')
- out_grad: bfloat16 [16384, 1024], P('dp', 'mp')
- lengths: int32 [16], P('dp'), may hold values from 256 to 1024
- group_ids: int32 [16], P('dp'), may hold values from 0 to 7
- time_embed: float32 [8, 1024], replicated, may hold values from -6 to 6
- weights: float32 [1024, 14, 1024], P('dp', None, 'mp')
- first_moments: float32 [1024, 14, 1024], P('dp', None, 'mp')
- second_moments: float32 [1024, 14, 1024], P('dp', None, 'mp'), as said below
- owners: int32 [14, 8], replicated, may hold values from 0 to 7, each once within a row
- left_basis: float32 [14, 1024, 128], P(None, 'dp'), may hold values from -1 to 1, as said below
- right_basis: float32 [14, 1024, 256], P(None, 'mp'), may hold values from -1 to 1, as said below
- biases: float32 [13, 1024], P(None, 'mp'), may hold values from -2.5 to 2.5
- bias_first: float32 [13, 1024], P(None, 'mp')
- bias_second: float32 [13, 1024], P(None, 'mp'), as said below
Outputs:
- block_out: bfloat16 [16384, 1024], P('dp', 'mp')
- input_grad: float32 [16384, 1024], P('dp', 'mp')
- weight_grads: float32 [1024, 14, 1024], P('dp', None, 'mp')
- new_first: float32 [1024, 14, 1024], P('dp', None, 'mp')
- new_second: float32 [1024, 14, 1024], P('dp', None, 'mp')
- new_weights: float32 [1024, 14, 1024], P('dp', None, 'mp')
- new_weights_low: bfloat16 [1024, 14, 1024], P('dp', None, 'mp')
- new_bias_first: float32 [13, 1024], P(None, 'mp')
- new_bias_second: float32 [13, 1024], P(None, 'mp')
- new_biases: float32 [13, 1024], P(None, 'mp')
Inputs may be any that keep to these rules, and one draw needn't show every extreme that they name: Each block left_basis[k, a * 128 to a * 128 + 127, :] is an orthogonal matrix. Each block right_basis[k, c * 256 to c * 256 + 255, :] is an orthogonal matrix. `second_moments`: positive. `bias_second`: positive.
All inputs are finite; a program needn't handle non-finite values.
Results may differ from a plain program's by a relative error of at most 0.02.
The roundings to bfloat16 on the way count: a program that leaves them out, or rounds other values in their place, can miss the bound.
Values may be sent and summed in bfloat16 or wider, within the bound.
No kernel may reach another device: no remote copies, remote signals or barrier semaphores. Data moves between devices by JAX's collectives and lax.ppermute only.
A program may use at most 192 MiB of HBM per device.

v0:
```python
import jax
import jax.numpy as jnp
from jax import lax
from jax.sharding import PartitionSpec as P

D = 1024
HEAD_DIM = 64
LEN = 1024
UTT_DEV = 2
GROUPS = 8
STEP = 10


norm_epsilon = 1e-06
soap_first = 0.95
soap_second = 0.95
soap_epsilon = 1e-08
soap_rate = 0.05
soap_decay = 0.01
vector_first = 0.9
vector_second = 0.999
vector_epsilon = 1e-08
vector_rate = 0.1
masked_score = -1e30


def true_order(gathered, owners):
    block_count = owners.shape[1]
    blocks = gathered.reshape(
        block_count, gathered.shape[0] // block_count, gathered.shape[1], gathered.shape[2]
    )
    picked = [
        jnp.take(blocks[:, :, slot_index, :], owners[slot_index], axis=0)
        for slot_index in range(owners.shape[0])
    ]
    return jnp.stack(picked, axis=2).reshape(gathered.shape)


def stored_order(values, owners):
    block_count = owners.shape[1]
    blocks = values.reshape(
        block_count, values.shape[0] // block_count, values.shape[1], values.shape[2]
    )
    placed = [
        jnp.take(blocks[:, :, slot_index, :], jnp.argsort(owners[slot_index]), axis=0)
        for slot_index in range(owners.shape[0])
    ]
    return jnp.stack(placed, axis=2).reshape(values.shape)


def gather_block(low_weights, owners):
    whole_rows = lax.all_gather(low_weights[:, :8, :], "dp", axis=0, tiled=True)
    return true_order(whole_rows, owners[:8])


def reduce_grads(values):
    return lax.psum_scatter(
        values.astype(jnp.bfloat16), "dp", scatter_dimension=0, tiled=True
    ).astype(jnp.float32)


def branch_total(partial_rows):
    return lax.psum_scatter(
        partial_rows.astype(jnp.bfloat16), "mp", scatter_dimension=1, tiled=True
    ).astype(jnp.float32)


def branch_spread(grad_rows):
    return lax.all_gather(grad_rows, "mp", axis=1, tiled=True)


def gelu_tanh(values):
    return jax.nn.gelu(values, approximate=True)


def rotary_tables():
    half_dim = HEAD_DIM // 2
    places = jnp.arange(LEN, dtype=jnp.float32)
    frequencies = 10000.0 ** (-(jnp.arange(half_dim, dtype=jnp.float32) * 2.0 / HEAD_DIM))
    angles = places[:, None] * frequencies[None, :]
    return (jnp.cos(angles)[:, None, :], jnp.sin(angles)[:, None, :])


def rotate(values, cosine_table, sine_table, direction_sign):
    pair_view = values.reshape(values.shape[0], values.shape[1], values.shape[2] // 2, 2)
    even_part = pair_view[..., 0]
    odd_part = pair_view[..., 1]
    turned = jnp.stack(
        [
            even_part * cosine_table - direction_sign * odd_part * sine_table,
            odd_part * cosine_table + direction_sign * even_part * sine_table,
        ],
        axis=-1,
    )
    return turned.reshape(values.shape)


def modulated(values, shift_row, scale_row):
    totals = lax.psum((jnp.sum(values, axis=1), jnp.sum(values * values, axis=1)), "mp")
    row_mean = totals[0] / D
    spread = totals[1] / D - row_mean * row_mean
    inverse = lax.rsqrt(spread + norm_epsilon)
    normed = (values - row_mean[:, None]) * inverse[:, None]
    low_rows = (normed * (1.0 + scale_row) + shift_row).astype(jnp.bfloat16)
    return (lax.all_gather(low_rows, "mp", axis=1, tiled=True), normed, inverse)


def norm_back(partial_rows, normed, inverse, scale_row):
    grad_hidden = lax.psum_scatter(
        partial_rows.astype(jnp.bfloat16), "mp", scatter_dimension=1, tiled=True
    ).astype(jnp.float32)
    grad_normed = grad_hidden * (1.0 + scale_row)
    totals = lax.psum((jnp.sum(grad_normed, axis=1), jnp.sum(grad_normed * normed, axis=1)), "mp")
    grad_rows = inverse[:, None] * (
        grad_normed - totals[0][:, None] / D - normed * totals[1][:, None] / D
    )
    return (grad_rows, jnp.sum(grad_hidden, axis=0), jnp.sum(grad_hidden * normed, axis=0))


def attend(queries, keys_in, values_in, valid_rows):
    score_scale = HEAD_DIM ** (-0.5)
    block_rows = LEN // 2
    outputs = []
    totals = []
    for offset in range(0, LEN, block_rows):
        scores = (
            jnp.einsum(
                "qhd,khd->hqk",
                queries[offset : offset + block_rows],
                keys_in,
                preferred_element_type=jnp.float32,
            )
            * score_scale
        )
        scores = jnp.where(valid_rows[None, None, :], scores, masked_score)
        row_top = jnp.max(scores, axis=2, keepdims=True)
        row_total = row_top + jnp.log(jnp.sum(jnp.exp(scores - row_top), axis=2, keepdims=True))
        chances = jnp.exp(scores - row_total).astype(jnp.bfloat16)
        outputs.append(
            jnp.einsum("hqk,khd->qhd", chances, values_in, preferred_element_type=jnp.float32)
        )
        totals.append(row_total)
    return (jnp.concatenate(outputs, axis=0).astype(jnp.bfloat16), totals)


def attend_back(queries, keys_in, values_in, valid_rows, totals, grad_mixed):
    score_scale = HEAD_DIM ** (-0.5)
    block_rows = LEN // 2
    grad_keys = jnp.zeros(keys_in.shape, jnp.float32)
    grad_values = jnp.zeros(values_in.shape, jnp.float32)
    grad_queries = []
    for position, offset in enumerate(range(0, LEN, block_rows)):
        query_rows = queries[offset : offset + block_rows]
        grad_rows = grad_mixed[offset : offset + block_rows]
        scores = (
            jnp.einsum("qhd,khd->hqk", query_rows, keys_in, preferred_element_type=jnp.float32)
            * score_scale
        )
        scores = jnp.where(valid_rows[None, None, :], scores, masked_score)
        soft_chances = jnp.exp(scores - totals[position])
        grad_values = grad_values + jnp.einsum(
            "hqk,qhd->khd",
            soft_chances.astype(jnp.bfloat16),
            grad_rows,
            preferred_element_type=jnp.float32,
        )
        grad_chances = jnp.einsum(
            "qhd,khd->hqk", grad_rows, values_in, preferred_element_type=jnp.float32
        )
        inner = jnp.sum(soft_chances * grad_chances, axis=2, keepdims=True)
        grad_scores = (soft_chances * (grad_chances - inner)).astype(jnp.bfloat16)
        grad_queries.append(
            jnp.einsum("hqk,khd->qhd", grad_scores, keys_in, preferred_element_type=jnp.float32)
            * score_scale
        )
        grad_keys = (
            grad_keys
            + jnp.einsum(
                "hqk,qhd->khd", grad_scores, query_rows, preferred_element_type=jnp.float32
            )
            * score_scale
        )
    return (jnp.concatenate(grad_queries, axis=0), grad_keys, grad_values)


def body(
    block_in,
    out_grad,
    lengths,
    group_ids,
    time_embed,
    weights,
    first_moments,
    second_moments,
    owners,
    left_basis,
    right_basis,
    biases,
    bias_first,
    bias_second,
):
    highest = lax.Precision.HIGHEST
    shard_width = weights.shape[2]
    head_count = shard_width // HEAD_DIM
    group_hits = (group_ids[:, None] == jnp.arange(GROUPS, dtype=jnp.int32)[None, :]).astype(
        jnp.float32
    )
    embedded = jnp.dot(group_hits, time_embed, precision=highest)
    condition = jax.nn.silu(embedded).astype(jnp.bfloat16)
    low_weights = weights.astype(jnp.bfloat16)
    mod_whole = lax.all_gather(low_weights[:, 8:, :], "dp", axis=0, tiled=True)
    mod_true = true_order(mod_whole, owners[8:])
    modulation = (
        jnp.einsum("ud,dkc->ukc", condition, mod_true, preferred_element_type=jnp.float32)
        + biases[7:]
    )
    cosine_table, sine_table = rotary_tables()
    outputs = []
    input_rows = []
    mod_grads = []
    weight_total = jnp.zeros((D, 8, shard_width), jnp.float32)
    bias_total = jnp.zeros((7, shard_width), jnp.float32)
    for utterance in range(UTT_DEV):
        block_now = gather_block(low_weights, owners)
        mod_row = modulation[utterance]
        rows_x = block_in[utterance * LEN : (utterance + 1) * LEN].astype(jnp.float32)
        cotangent = out_grad[utterance * LEN : (utterance + 1) * LEN].astype(jnp.float32)
        valid_rows = jnp.arange(LEN, dtype=jnp.int32) < lengths[utterance]
        keep_rows = valid_rows.astype(jnp.float32)[:, None]
        normed_in, first_norm, first_inverse = modulated(rows_x, mod_row[0], mod_row[1])
        projected = (
            jnp.einsum(
                "td,dkc->tkc", normed_in, block_now[:, 0:3, :], preferred_element_type=jnp.float32
            )
            + biases[0:3]
        )
        queries = rotate(
            projected[:, 0, :].reshape(LEN, head_count, HEAD_DIM), cosine_table, sine_table, 1.0
        ).astype(jnp.bfloat16)
        keys_in = rotate(
            projected[:, 1, :].reshape(LEN, head_count, HEAD_DIM), cosine_table, sine_table, 1.0
        ).astype(jnp.bfloat16)
        values_in = projected[:, 2, :].reshape(LEN, head_count, HEAD_DIM).astype(jnp.bfloat16)
        mixed, totals = attend(queries, keys_in, values_in, valid_rows)
        mixed_rows = mixed.reshape(LEN, shard_width)
        attended = (
            branch_total(
                jnp.einsum(
                    "tc,oc->to", mixed_rows, block_now[:, 3, :], preferred_element_type=jnp.float32
                )
            )
            + biases[3]
        ) * keep_rows
        middle = rows_x + mod_row[2] * attended
        normed_mid, second_norm, second_inverse = modulated(middle, mod_row[3], mod_row[4])
        hidden = (
            jnp.einsum(
                "td,dec->tec", normed_mid, block_now[:, 4:6, :], preferred_element_type=jnp.float32
            )
            + biases[4:6]
        )
        active = gelu_tanh(hidden).astype(jnp.bfloat16)
        fed_rows = (
            branch_total(
                jnp.einsum(
                    "tec,oec->to", active, block_now[:, 6:8, :], preferred_element_type=jnp.float32
                )
            )
            + biases[6]
        )
        outputs.append((middle + mod_row[5] * fed_rows).astype(jnp.bfloat16))
        grad_fed = (mod_row[5] * cotangent).astype(jnp.bfloat16)
        grad_fed_whole = branch_spread(grad_fed)
        grad_out_weight = jnp.einsum(
            "to,tec->oec", grad_fed_whole, active, preferred_element_type=jnp.float32
        )
        grad_active = jnp.einsum(
            "to,oec->tec", grad_fed_whole, block_now[:, 6:8, :], preferred_element_type=jnp.float32
        )
        grad_hidden = jax.vjp(gelu_tanh, hidden)[1](grad_active)[0].astype(jnp.bfloat16)
        grad_in_weight = jnp.einsum(
            "td,tec->dec", normed_mid, grad_hidden, preferred_element_type=jnp.float32
        )
        grad_mid_norm, shift_two, scale_two = norm_back(
            jnp.einsum(
                "tec,dec->td", grad_hidden, block_now[:, 4:6, :], preferred_element_type=jnp.float32
            ),
            second_norm,
            second_inverse,
            mod_row[4],
        )
        grad_middle = cotangent + grad_mid_norm
        grad_attended = (mod_row[2] * grad_middle * keep_rows).astype(jnp.bfloat16)
        grad_attended_whole = branch_spread(grad_attended)
        grad_proj_weight = jnp.einsum(
            "to,tc->oc", grad_attended_whole, mixed_rows, preferred_element_type=jnp.float32
        )
        grad_mixed = jnp.einsum(
            "to,oc->tc", grad_attended_whole, block_now[:, 3, :], preferred_element_type=jnp.float32
        ).astype(jnp.bfloat16)
        grad_query_turned, grad_key_turned, grad_values = attend_back(
            queries,
            keys_in,
            values_in,
            valid_rows,
            totals,
            grad_mixed.reshape(LEN, head_count, HEAD_DIM),
        )
        grad_projected = jnp.stack(
            [
                rotate(grad_query_turned, cosine_table, sine_table, -1.0).reshape(LEN, shard_width),
                rotate(grad_key_turned, cosine_table, sine_table, -1.0).reshape(LEN, shard_width),
                grad_values.reshape(LEN, shard_width),
            ],
            axis=1,
        ).astype(jnp.bfloat16)
        grad_qkv_weight = jnp.einsum(
            "td,tkc->dkc", normed_in, grad_projected, preferred_element_type=jnp.float32
        )
        grad_in_norm, shift_one, scale_one = norm_back(
            jnp.einsum(
                "tkc,dkc->td",
                grad_projected,
                block_now[:, 0:3, :],
                preferred_element_type=jnp.float32,
            ),
            first_norm,
            first_inverse,
            mod_row[1],
        )
        input_rows.append(grad_middle + grad_in_norm)
        mod_grads.append(
            jnp.stack(
                [
                    shift_one,
                    scale_one,
                    jnp.sum(grad_middle * attended, axis=0),
                    shift_two,
                    scale_two,
                    jnp.sum(cotangent * fed_rows, axis=0),
                ]
            )
        )
        weight_total = weight_total + jnp.concatenate(
            [grad_qkv_weight, grad_proj_weight[:, None, :], grad_in_weight, grad_out_weight], axis=1
        )
        bias_total = bias_total + jnp.concatenate(
            [
                jnp.sum(grad_projected.astype(jnp.float32), axis=0),
                jnp.sum(grad_attended.astype(jnp.float32), axis=0)[None, :],
                jnp.sum(grad_hidden.astype(jnp.float32), axis=0),
                jnp.sum(grad_fed.astype(jnp.float32), axis=0)[None, :],
            ],
            axis=0,
        )
    grad_mods = jnp.stack(mod_grads)
    grad_mod_weight = jnp.einsum(
        "ud,ukc->dkc", condition.astype(jnp.float32), grad_mods, precision=highest
    )
    reduced = reduce_grads(
        stored_order(jnp.concatenate([weight_total, grad_mod_weight], axis=1), owners)
    )
    bias_local = jnp.concatenate([bias_total, jnp.sum(grad_mods, axis=0)], axis=0)
    bias_grad = lax.psum(bias_local, "dp")
    turned = jnp.einsum("kij,ikc->jkc", left_basis, reduced, precision=highest)
    turned = jnp.einsum("jkc,kce->jke", turned, right_basis, precision=highest)
    first_new = soap_first * first_moments + (1.0 - soap_first) * turned
    second_new = soap_second * second_moments + (1.0 - soap_second) * turned * turned
    direction = (
        first_new
        / (1.0 - soap_first**STEP)
        / (jnp.sqrt(second_new / (1.0 - soap_second**STEP)) + soap_epsilon)
    )
    rotated_back = jnp.einsum("kij,jke->ike", left_basis, direction, precision=highest)
    rotated_back = jnp.einsum("ike,kce->ikc", rotated_back, right_basis, precision=highest)
    new_weights = weights - soap_rate * (rotated_back + soap_decay * weights)
    bias_first_new = vector_first * bias_first + (1.0 - vector_first) * bias_grad
    bias_second_new = vector_second * bias_second + (1.0 - vector_second) * bias_grad * bias_grad
    new_biases = biases - vector_rate * (bias_first_new / (1.0 - vector_first**STEP)) / (
        jnp.sqrt(bias_second_new / (1.0 - vector_second**STEP)) + vector_epsilon
    )
    return (
        jnp.concatenate(outputs, axis=0),
        jnp.concatenate(input_rows, axis=0),
        reduced,
        first_new,
        second_new,
        new_weights,
        new_weights.astype(jnp.bfloat16),
        bias_first_new,
        bias_second_new,
        new_biases,
    )


def solution(mesh):
    return jax.shard_map(
        body,
        mesh=mesh,
        in_specs=(
            P("dp", "mp"),
            P("dp", "mp"),
            P("dp"),
            P("dp"),
            P(),
            P("dp", None, "mp"),
            P("dp", None, "mp"),
            P("dp", None, "mp"),
            P(),
            P(None, "dp", None),
            P(None, "mp", None),
            P(None, "mp"),
            P(None, "mp"),
            P(None, "mp"),
        ),
        out_specs=(
            P("dp", "mp"),
            P("dp", "mp"),
            P("dp", None, "mp"),
            P("dp", None, "mp"),
            P("dp", None, "mp"),
            P("dp", None, "mp"),
            P("dp", None, "mp"),
            P(None, "mp"),
            P(None, "mp"),
            P(None, "mp"),
        ),
        check_vma=False,
    )
```

profile of v0, /device:TPU:0, one launch (start us, length us, event | category | flops | bytes accessed | tf_op | source)
XLA Modules:
  0.0 1065.4 jit_solution(13720281788594007767)
XLA Ops:
  13.4 12.6 %all-reduce.3 = (f32[1024]{0:T(1024)S(1)}, f32[1024]{0:T(1024)S(1)}, f32[1024]{0:T(1024)S(1)}, f32[1024]{0:T(1024)S(1)}) all-reduce(f32[1024]{0:T(1024)S(1)} %get-tuple-element.61, f32[1024]{0:T(1024)S(1)} %get-tuple-element.60, f32[1024]{0:T(1024)S(1)} %get-tuple-element.62, ...), channel_id=1, replica_groups=mesh['dp'=8,'mp'=4] {'mp'}, use_global_device_ids=true, to_apply=%region_3.5 | all-reduce | flops 4096 | bytes 32768 | tf_op jit(solution)/shard_map/psum | solution.py:99
  26.9 47.2 %all-gather.11.cloned.1.call-done = bf16[1024,6,256]{2,0,1:T(8,128)(2,1)} async-done(((bf16[128,6,256]{2,0,1:T(8,128)(2,1)}), bf16[1024,6,256]{2,0,1:T(8,128)(2,1)}) %all-gather.11.cloned.1.call-update) | async-done | bytes 3145744 | tf_op jit(solution)/shard_map/all_gather | solution.py:211
  99.5 48.8 %all-gather.15.cloned.1.call-done = bf16[1024,8,256]{2,0,1:T(8,128)(2,1)} async-done(((bf16[128,8,256]{2,0,1:T(8,128)(2,1)}), bf16[1024,8,256]{2,0,1:T(8,128)(2,1)}) %all-gather.15.cloned.1.call-update) | async-done | bytes 4194320 | tf_op jit(solution)/shard_map/all_gather | solution.py:52
  177.0 19.5 %all-gather.19.cloned.1.call-done = bf16[1024,1024]{1,0:T(8,128)(2,1)} async-done(((bf16[1024,256]{1,0:T(8,128)(2,1)}), bf16[1024,1024]{1,0:T(8,128)(2,1)}) %all-gather.19.cloned.1.call-update) | async-done | bytes 2097168 | tf_op jit(solution)/shard_map/all_gather | solution.py:105
  213.7 9.0 subtract_convert_fusion.4
  274.9 4.3 reduce-scatter.14.cloned.1.call-done
  279.1 34.6 %reduce-scatter.10.cloned.1.call-done = bf16[1024,256]{1,0:T(8,128)(2,1)} async-done(((bf16[1024,1024]{1,0:T(8,128)(2,1)}), bf16[1024,256]{1,0:T(8,128)(2,1)}) %reduce-scatter.10.cloned.1.call-update) | async-done | bytes 524304 | tf_op jit(solution)/shard_map/reduce_scatter | solution.py:63
  316.0 10.1 all-reduce.2
  346.5 6.7 all-gather.21.cloned.1.call-done
  353.2 4.5 fusion.32
  357.7 20.5 %all-gather.27.cloned.1.call-done = bf16[1024,1024]{1,0:T(8,128)(2,1)} async-done(((bf16[1024,256]{1,0:T(8,128)(2,1)}), bf16[1024,1024]{1,0:T(8,128)(2,1)}) %all-gather.27.cloned.1.call-update) | async-done | bytes 2097168 | tf_op jit(solution)/shard_map/all_gather | solution.py:69
  378.2 5.4 convert_reduce_fusion.2
  387.3 16.0 %all-gather.17.cloned.1.call-done = bf16[1024,1024]{1,0:T(8,128)(2,1)} async-done(((bf16[1024,256]{1,0:T(8,128)(2,1)}), bf16[1024,1024]{1,0:T(8,128)(2,1)}) %all-gather.17.cloned.1.call-update) | async-done | bytes 2097168 | tf_op jit(solution)/shard_map/all_gather | solution.py:105
  403.2 4.4 fusion.40
  407.6 19.9 %all-gather.23.cloned.1.call-done = bf16[1024,1024]{1,0:T(8,128)(2,1)} async-done(((bf16[1024,256]{1,0:T(8,128)(2,1)}), bf16[1024,1024]{1,0:T(8,128)(2,1)}) %all-gather.23.cloned.1.call-update) | async-done | bytes 2097168 | tf_op jit(solution)/shard_map/all_gather | solution.py:69
  427.5 5.4 convert_reduce_fusion.3
  437.0 4.8 bitcast_convert_fusion.4
  441.8 4.8 bitcast_convert_fusion.5
  461.5 34.0 %reduce-scatter.18.cloned.1.call-done = bf16[1024,256]{1,0:T(8,128)(2,1)} async-done(((bf16[1024,1024]{1,0:T(8,128)(2,1)}), bf16[1024,256]{1,0:T(8,128)(2,1)}) %reduce-scatter.18.cloned.1.call-update) | async-done | bytes 524304 | tf_op jit(solution)/shard_map/reduce_scatter | solution.py:109
  498.4 10.1 all-reduce.1
  508.5 21.0 %reduce-scatter.16.cloned.1.call-done = bf16[1024,256]{1,0:T(8,128)(2,1)} async-done(((bf16[1024,1024]{1,0:T(8,128)(2,1)}), bf16[1024,256]{1,0:T(8,128)(2,1)}) %reduce-scatter.16.cloned.1.call-update) | async-done | bytes 524304 | tf_op jit(solution)/shard_map/reduce_scatter | solution.py:63
  529.5 34.0 %reduce-scatter.12.cloned.1.call-done = bf16[1024,256]{1,0:T(8,128)(2,1)} async-done(((bf16[1024,1024]{1,0:T(8,128)(2,1)}), bf16[1024,256]{1,0:T(8,128)(2,1)}) %reduce-scatter.12.cloned.1.call-update) | async-done | bytes 524304 | tf_op jit(solution)/shard_map/reduce_scatter | solution.py:63
  563.5 4.2 convert_reduce_fusion.11
  574.2 16.6 %all-gather.29.cloned.1.call-done = bf16[1024,1024]{1,0:T(8,128)(2,1)} async-done(((bf16[1024,256]{1,0:T(8,128)(2,1)}), bf16[1024,1024]{1,0:T(8,128)(2,1)}) %all-gather.29.cloned.1.call-update) | async-done | bytes 2097168 | tf_op jit(solution)/shard_map/all_gather | solution.py:69
  593.9 4.5 fusion.199
  598.5 14.8 %multiply_reduce_fusion = (f32[4,512]{1,0:T(4,128)S(1)}, f32[4,512]{1,0:T(4,128)S(1)}, f32[4,512,1024]{2,1,0:T(8,128)}) fusion(f32[4,512,1024]{2,1,0:T(8,128)} %copy-done.3, f32[4,512]{1,0:T(4,128)S(1)} %log_add_fusion, pred[1024]{0:T(1024)(128)(4,1)S(1)} %iota_compare_fusion, f32[4,512,1024]{2,1,0:T(8,128)} %fusion.199, f32[4,512]{1,0:T(4,128)S(1)} %log_add_fusion.1, ...), kind=kOutput, calls=%fused_computation.31 | convolution fusion | flops 289402880 | bytes 34374656 | tf_op jit(solution)/shard_map/qhd,khd->hqk/dot_general | solution.py:167
  615.5 9.9 multiply_convert_fusion
  635.6 4.5 fusion.197
  640.1 14.1 %multiply_reduce_fusion.2 = (f32[4,512]{1,0:T(4,128)S(1)}, f32[4,512]{1,0:T(4,128)S(1)}, f32[4,512,1024]{2,1,0:T(8,128)}) fusion(f32[4,512,1024]{2,1,0:T(8,128)} %copy-done.2, f32[4,512]{1,0:T(4,128)S(1)} %log_add_fusion.2, pred[1024]{0:T(1024)(128)(4,1)S(1)} %iota_compare_fusion.1, f32[4,512,1024]{2,1,0:T(8,128)} %fusion.197, ...), kind=kOutput, calls=%fused_computation.35 | convolution fusion | flops 289402880 | bytes 34374656 | tf_op jit(solution)/shard_map/qhd,khd->hqk/dot_general | solution.py:167
  656.5 10.1 multiply_convert_fusion.2
  670.7 6.1 fusion.88
  678.9 4.5 fusion.92
  693.3 4.5 fusion.90
  707.5 8.7 subtract_convert_fusion.3
  729.4 4.9 bitcast_convert_fusion
  734.6 5.4 fusion.142
  740.0 6.6 fusion.87
  762.0 5.0 bitcast_convert_fusion.2
  767.4 4.6 fusion.30
  789.0 8.7 maximum_add_fusion
  802.6 10.1 all-reduce
  816.1 4.2 fusion.146
  820.3 6.7 pad_maximum_fusion
  827.1 5.7 slice_bitcast_fusion
  911.8 39.8 %psum.135 = f32[13,256]{1,0:T(8,128)S(1)} all-reduce(f32[13,256]{1,0:T(8,128)S(1)} %pad_maximum_fusion.24), channel_id=1, replica_groups=mesh['dp'=8,'mp'=4] {'dp'}, use_global_device_ids=true, to_apply=%region_87.90 | all-reduce | flops 3328 | bytes 26624 | tf_op jit(solution)/shard_map/psum | solution.py:364
  957.1 85.1 %reduce-scatter.26.cloned.1.call-done = bf16[128,14,256]{2,0,1:T(8,128)(2,1)} async-done(((bf16[1024,14,256]{2,0,1:T(8,128)(2,1)}), bf16[128,14,256]{2,0,1:T(8,128)(2,1)}) %reduce-scatter.26.cloned.1.call-update) | async-done | bytes 917520 | tf_op jit(solution)/shard_map/reduce_scatter | solution.py:57
  1044.5 4.3 fusion.46
  1051.6 5.4 fusion.196
  (660 shorter events, 372.1 us)
Async XLA Ops:
  7.2 1035.0 %copy-start = (f32[14,128,128]{2,1,0:T(8,128)S(1)}, f32[14,128,128]{2,1,0:T(8,128)}, u32[]{:S(2)}) copy-start(f32[14,128,128]{2,1,0:T(8,128)} %param.27) | copy-start | bytes 2752516
  7.2 18.8 %copy-start.78 = (s32[14,8]{0,1:T(8,128)S(1)}, s32[14,8]{0,1:T(8,128)}, u32[]{:S(2)}) copy-start(s32[14,8]{0,1:T(8,128)} %param.26) | copy-start | bytes 1348
  7.2 19.4 %copy-start.130 = (f32[8,1024]{1,0:T(8,128)S(1)}, f32[8,1024]{1,0:T(8,128)}, u32[]{:S(2)}) copy-start(f32[8,1024]{1,0:T(8,128)} %param.22) | copy-start | bytes 98308
  7.2 19.4 %copy-start.131 = (s32[2]{0:T(128)S(1)}, s32[2]{0:T(128)}, u32[]{:S(2)}) copy-start(s32[2]{0:T(128)} %param.21) | copy-start | bytes 28
  7.2 66.9 %all-gather.11.cloned.1.call-start = ((), (), s32[]{:S(2)}) async-start(), calls=%async_computation.9 | async-start | bytes 3538944 | tf_op jit(solution)/shard_map/all_gather | solution.py:211
  10.7 137.6 %all-gather.15.cloned.1.call-start = ((), (), s32[]{:S(2)}) async-start(), calls=%async_computation.11 | async-start | bytes 4718592 | tf_op jit(solution)/shard_map/all_gather | solution.py:52
  12.7 158.9 %all-gather.13.cloned.1.call-start = ((), (), s32[]{:S(2)}) async-start(), calls=%async_computation.10 | async-start | bytes 2621440 | tf_op jit(solution)/shard_map/all_gather | solution.py:105
  26.7 67.5 %copy-start.95 = (f32[1024]{0:T(1024)}, f32[1024]{0:T(1024)S(1)}, u32[]{:S(2)}) copy-start(f32[1024]{0:T(1024)S(1)} %get-tuple-element.293) | copy-start | bytes 12292
  26.7 67.5 %copy-start.97 = (f32[1024]{0:T(1024)}, f32[1024]{0:T(1024)S(1)}, u32[]{:S(2)}) copy-start(f32[1024]{0:T(1024)S(1)} %get-tuple-element.294) | copy-start | bytes 12292
  26.7 67.5 %copy-start.101 = (f32[1024]{0:T(1024)}, f32[1024]{0:T(1024)S(1)}, u32[]{:S(2)}) copy-start(f32[1024]{0:T(1024)S(1)} %get-tuple-element.224) | copy-start | bytes 12292
  26.7 67.5 %copy-start.103 = (f32[1024]{0:T(1024)}, f32[1024]{0:T(1024)S(1)}, u32[]{:S(2)}) copy-start(f32[1024]{0:T(1024)S(1)} %get-tuple-element.225) | copy-start | bytes 12292
  26.9 66.6 %copy-start.109 = (bf16[2,1024]{1,0:T(2,128)(2,1)}, bf16[2,1024]{1,0:T(2,128)(2,1)S(1)}, u32[]{:S(2)}) copy-start(bf16[2,1024]{1,0:T(2,128)(2,1)S(1)} %fusion.150) | copy-start | bytes 12292
  94.1 58.1 %copy-start.105 = (f32[1,1,256]{2,0,1:T(1,128)}, f32[1,1,256]{2,0,1:T(1,128)S(1)}, u32[]{:S(2)}) copy-start(f32[1,1,256]{2,0,1:T(1,128)S(1)} %get-tuple-element.218) | copy-start | bytes 3076
  94.1 58.1 %copy-start.107 = (f32[1,1,256]{2,0,1:T(1,128)}, f32[1,1,256]{2,0,1:T(1,128)S(1)}, u32[]{:S(2)}) copy-start(f32[1,1,256]{2,0,1:T(1,128)S(1)} %get-tuple-element.213) | copy-start | bytes 3076
  95.8 100.6 %all-gather.19.cloned.1.call-start = ((), (), s32[]{:S(2)}) async-start(), calls=%async_computation.15 | async-start | bytes 2621440 | tf_op jit(solution)/shard_map/all_gather | solution.py:105
  97.8 181.3 %reduce-scatter.14.cloned.1.call-start = ((), (), s32[]{:S(2)}) async-start(), calls=%async_computation.16 | async-start | bytes 2621440 | tf_op jit(solution)/shard_map/reduce_scatter | solution.py:63
  99.5 114.2 %copy-start.71 = (f32[1024,32]{0,1:T(8,128)}, f32[1024,32]{0,1:T(8,128)S(1)}, u32[]{:S(2)}) copy-start(f32[1024,32]{0,1:T(8,128)S(1)} %get-tuple-element.234) | copy-start | bytes 393220
  175.4 21.0 %copy-start.80 = (bf16[1024,1,256]{0,2,1:T(8,128)(2,1)S(1)}, bf16[1024,1,256]{0,2,1:T(8,128)(2,1)}, u32[]{:S(2)}) copy-start(bf16[1024,1,256]{0,2,1:T(8,128)(2,1)} %copy.67) | copy-start | bytes 1572868
  175.5 92.9 %copy-start.21 = (bf16[1024,1,256]{0,2,1:T(8,128)(2,1)}, bf16[1024,1,256]{0,2,1:T(8,128)(2,1)S(1)}, u32[]{:S(2)}) copy-start(bf16[1024,1,256]{0,2,1:T(8,128)(2,1)S(1)} %slice.800) | copy-start | bytes 1572868
  247.5 66.2 %reduce-scatter.10.cloned.1.call-start = ((), (), s32[]{:S(2)}) async-start(), calls=%async_computation.12 | async-start | bytes 2621440 | tf_op jit(solution)/shard_map/reduce_scatter | solution.py:63
  273.4 79.9 %all-gather.21.cloned.1.call-start = ((), (), s32[]{:S(2)}) async-start(), calls=%async_computation.17 | async-start | bytes 2621440 | tf_op jit(solution)/shard_map/all_gather | solution.py:105
  329.2 49.0 %all-gather.27.cloned.1.call-start = ((), (), s32[]{:S(2)}) async-start(), calls=%async_computation.23 | async-start | bytes 2621440 | tf_op jit(solution)/shard_map/all_gather | solution.py:69
  332.4 70.8 %all-gather.17.cloned.1.call-start = ((), (), s32[]{:S(2)}) async-start(), calls=%async_computation.13 | async-start | bytes 2621440 | tf_op jit(solution)/shard_map/all_gather | solution.py:105
  333.1 94.4 %all-gather.23.cloned.1.call-start = ((), (), s32[]{:S(2)}) async-start(), calls=%async_computation.19 | async-start | bytes 2621440 | tf_op jit(solution)/shard_map/all_gather | solution.py:69
  333.7 127.8 %reduce-scatter.22.cloned.1.call-start = ((), (), s32[]{:S(2)}) async-start(), calls=%async_computation.24 | async-start | bytes 2621440 | tf_op jit(solution)/shard_map/reduce_scatter | solution.py:109
  344.7 92.3 %copy-start.81 = (bf16[8,128,256]{2,1,0:T(8,128)(2,1)}, bf16[8,128,256]{2,1,0:T(8,128)(2,1)S(1)}, u32[]{:S(2)}) copy-start(bf16[8,128,256]{2,1,0:T(8,128)(2,1)S(1)} %broadcast_select_fusion) | copy-start | bytes 1572868
  353.2 25.0 %copy-start.82 = (bf16[8,128,256]{2,1,0:T(8,128)(2,1)S(1)}, bf16[8,128,256]{2,1,0:T(8,128)(2,1)}, u32[]{:S(2)}) copy-start(bf16[8,128,256]{2,1,0:T(8,128)(2,1)} %broadcast_select_fusion.1) | copy-start | bytes 1572868
  387.2 108.3 %reduce-scatter.18.cloned.1.call-start = ((), (), s32[]{:S(2)}) async-start(), calls=%async_computation.20 | async-start | bytes 2621440 | tf_op jit(solution)/shard_map/reduce_scatter | solution.py:109
  436.5 93.0 %reduce-scatter.16.cloned.1.call-start = ((), (), s32[]{:S(2)}) async-start(), calls=%async_computation.18 | async-start | bytes 2621440 | tf_op jit(solution)/shard_map/reduce_scatter | solution.py:63
  441.8 53.8 %copy-start.9 = (bf16[1024,256]{1,0:T(8,128)(2,1)S(1)}, bf16[1024,256]{1,0:T(8,128)(2,1)}, u32[]{:S(2)}) copy-start(bf16[1024,256]{1,0:T(8,128)(2,1)} %reduce-scatter.14.cloned.1.call-done) | copy-start | bytes 1572868
  441.8 53.8 %copy-start.10 = (bf16[1024,256]{1,0:T(8,128)(2,1)S(1)}, bf16[1024,256]{1,0:T(8,128)(2,1)}, u32[]{:S(2)}) copy-start(bf16[1024,256]{1,0:T(8,128)(2,1)} %reduce-scatter.10.cloned.1.call-done) | copy-start | bytes 1572868
  441.8 121.7 %reduce-scatter.12.cloned.1.call-start = ((), (), s32[]{:S(2)}) async-start(), calls=%async_computation.14 | async-start | bytes 2621440 | tf_op jit(solution)/shard_map/reduce_scatter | solution.py:63
  446.6 144.1 %all-gather.29.cloned.1.call-start = ((), (), s32[]{:S(2)}) async-start(), calls=%async_computation.25 | async-start | bytes 2621440 | tf_op jit(solution)/shard_map/all_gather | solution.py:69
  454.4 113.4 %copy-start.132 = (s32[8]{0:T(128)}, s32[8]{0:T(128)S(1)}, u32[]{:S(2)}) copy-start(s32[8]{0:T(128)S(1)} %get-tuple-element.38) | copy-start | bytes 100
  458.3 40.1 %copy-start.140 = (s32[8]{0:T(128)}, s32[8]{0:T(128)S(1)}, u32[]{:S(2)}) copy-start(s32[8]{0:T(128)S(1)} %get-tuple-element.34) | copy-start | bytes 100
  567.7 64.6 %all-gather.25.cloned.1.call-start = ((), (), s32[]{:S(2)}) async-start(), calls=%async_computation.21 | async-start | bytes 2621440 | tf_op jit(solution)/shard_map/all_gather | solution.py:69
  574.1 19.8 %copy-start.24 = (bf16[1024,1,256]{0,2,1:T(8,128)(2,1)S(1)}, bf16[1024,1,256]{0,2,1:T(8,128)(2,1)}, u32[]{:S(2)}) copy-start(bf16[1024,1,256]{0,2,1:T(8,128)(2,1)} %slice.799) | copy-start | bytes 1572868
  574.1 223.6 %reduce-scatter.24.cloned.1.call-start = ((), (), s32[]{:S(2)}) async-start(), calls=%async_computation.26 | async-start | bytes 2621440 | tf_op jit(solution)/shard_map/reduce_scatter | solution.py:109
  598.4 15.8 %slice-start.5 = ((s8[8388608]{0:T(1024)(128)(4,1)}), s8[4194304]{0:T(1024)(128)(4,1)S(1)}, s32[]{:S(2)}) async-start(s8[8388608]{0:T(1024)(128)(4,1)} %bitcast.345), calls=%async_computation.33 | async-start | bytes 8388608
  598.5 17.1 %slice-start.7 = ((s8[8388608]{0:T(1024)(128)(4,1)}), s8[4194304]{0:T(1024)(128)(4,1)S(1)}, s32[]{:S(2)}) async-start(s8[8388608]{0:T(1024)(128)(4,1)} %bitcast.347), calls=%async_computation.35 | async-start | bytes 8388608
  640.1 16.4 %slice-start.3 = ((s8[8388608]{0:T(1024)(128)(4,1)}), s8[4194304]{0:T(1024)(128)(4,1)S(1)}, s32[]{:S(2)}) async-start(s8[8388608]{0:T(1024)(128)(4,1)} %bitcast.343), calls=%async_computation.31 | async-start | bytes 8388608
  734.3 65.7 %reduce-scatter.20.cloned.1.call-start = ((), (), s32[]{:S(2)}) async-start(), calls=%async_computation.22 | async-start | bytes 2621440 | tf_op jit(solution)/shard_map/reduce_scatter | solution.py:109
  767.1 275.1 %reduce-scatter.26.cloned.1.call-start = ((), (), s32[]{:S(2)}) async-start(), calls=%async_computation.27 | async-start | bytes 8257536 | tf_op jit(solution)/shard_map/reduce_scatter | solution.py:57
  789.0 23.7 %copy-start.11 = (bf16[1024,256]{1,0:T(8,128)(2,1)S(1)}, bf16[1024,256]{1,0:T(8,128)(2,1)}, u32[]{:S(2)}) copy-start(bf16[1024,256]{1,0:T(8,128)(2,1)} %reduce-scatter.10.cloned.1.call-done) | copy-start | bytes 1572868
  907.7 43.9 %copy-start.100 = (f32[13,256]{1,0:T(8,128)S(1)}, f32[13,256]{1,0:T(8,128)}, u32[]{:S(2)}) copy-start(f32[13,256]{1,0:T(8,128)} %param.29) | copy-start | bytes 39940
  907.7 43.9 %copy-start.111 = (f32[13,256]{1,0:T(8,128)S(1)}, f32[13,256]{1,0:T(8,128)}, u32[]{:S(2)}) copy-start(f32[13,256]{1,0:T(8,128)} %param.31) | copy-start | bytes 39940
  907.7 43.9 %copy-start.112 = (f32[13,256]{1,0:T(8,128)S(1)}, f32[13,256]{1,0:T(8,128)}, u32[]{:S(2)}) copy-start(f32[13,256]{1,0:T(8,128)} %param.30) | copy-start | bytes 39940
  954.3 90.2 %copy-start.64 = (f32[128,14,256]{2,0,1:T(8,128)S(1)}, f32[128,14,256]{2,0,1:T(8,128)}, u32[]{:S(2)}) copy-start(f32[128,14,256]{2,0,1:T(8,128)} %param.25) | copy-start | bytes 5505028
  (129 other events, 680.7 us)
Sparse Core Ops, SparseCore 0:
  10.9 63.1 all-gather.10
  76.3 71.9 all-gather.14
  150.5 21.1 all-gather.12
  173.6 22.8 all-gather.18
  247.7 31.4 reduce-scatter.13
  282.3 31.4 reduce-scatter.9
  329.3 23.8 all-gather.20
  355.3 22.8 all-gather.26
  380.3 22.8 all-gather.16
  404.6 22.8 all-gather.22
  430.0 31.4 reduce-scatter.21
  464.1 31.4 reduce-scatter.17
  498.1 31.4 reduce-scatter.15
  532.1 31.4 reduce-scatter.11
  567.9 22.8 all-gather.28
  592.7 22.8 all-gather.24
  734.5 31.5 reduce-scatter.23
  768.6 31.3 reduce-scatter.19
  907.7 134.3 reduce-scatter.25
where the time goes:
time: 1070 us
  waiting for transfers between devices  413 us (39%)
  matrix products  198 us (19%)
  other arithmetic  186 us (17%)
  local copies, waits for them, and re-layouts  166 us (16%)
  blocking collectives  82.9 us (8%)
  between operations  16.6 us (2%)
    reduce_scatter x4, waiting for transfers between devices, branch_total(): lax.psum_scatter(partial_rows.astype(jnp.bfloat16), 'mp', scatter_dimensi...  93.9 us
    reduce_scatter x1, waiting for transfers between devices, reduce_grads(): lax.psum_scatter(values.astype(jnp.bfloat16), 'dp', scatter_dimension=0,...  85.1 us
    all_gather x4, waiting for transfers between devices, branch_spread(): return lax.all_gather(grad_rows, 'mp', axis=1, tiled=True)  56.9 us
    all_gather x1, waiting for transfers between devices, gather_block(): whole_rows = lax.all_gather(low_weights[:, :8, :], 'dp', axis=0, tiled=True)  48.8 us
    all_gather x1, waiting for transfers between devices, body(): mod_whole = lax.all_gather(low_weights[:, 8:, :], 'dp', axis=0, tiled=True)  47.2 us
    another operation x16, other arithmetic  44.8 us
    all_gather x4, waiting for transfers between devices, modulated(): return (lax.all_gather(low_rows, 'mp', axis=1, tiled=True), normed, inverse)  43.6 us
    psum x1, blocking collectives, body(): bias_grad = lax.psum(bias_local, 'dp')  39.8 us
  transfers between devices with their start and end apart: 19, of which 17 were waited for; matrix products, arithmetic and copies ran while one was open for 25% of the time, Pallas kernels for 0%

commit v1 on v0

v1 whole, which is shorter than its diff:
```python
import functools
import math

import jax
import jax.numpy as jnp
from jax import lax
from jax.experimental import pallas as pl
from jax.experimental.pallas import tpu as pltpu
from jax.sharding import Mesh
from jax.sharding import PartitionSpec as P

D = 1024
HEAD_DIM = 64
LEN = 1024
GROUPS = 8
STEP = 10
CW = 256
TB = 256
NT = LEN // TB
BF = jnp.bfloat16
F32 = jnp.float32
LOG2E = math.log2(math.e)
LN2 = math.log(2.0)

norm_epsilon = 1e-06
soap_first = 0.95
soap_second = 0.95
soap_epsilon = 1e-08
soap_rate = 0.05
soap_decay = 0.01
vector_first = 0.9
vector_second = 0.999
vector_epsilon = 1e-08
vector_rate = 0.1
masked_score = -1e30
VMEM_LIMIT = 60 * 1024 * 1024

SWAP = [(0, 1), (1, 0)]


def params(n=1):
    return pltpu.CompilerParams(
        dimension_semantics=("arbitrary",) * n, vmem_limit_bytes=VMEM_LIMIT
    )


def nt_dot(a, b):
    return lax.dot_general(a, b, (((1,), (1,)), ((), ())), preferred_element_type=F32)


def nn_dot(a, b):
    return lax.dot_general(a, b, (((1,), (0,)), ((), ())), preferred_element_type=F32)


def whole(shape):
    return pl.BlockSpec(shape, lambda *_: (0,) * len(shape))


def rows_spec(width):
    return pl.BlockSpec((TB, width), lambda i, *_: (i, 0))


ANY = pl.BlockSpec(memory_space=pl.ANY)


def cost(flops, nbytes, trans=0):
    return pl.CostEstimate(flops=int(flops), bytes_accessed=int(nbytes), transcendentals=int(trans))


def fetch_weights(meta, rowtab, arrays, dest, sem, mats, base, start):
    n_dp, _, rows, _ = arrays[0].shape
    y = meta[0]
    for other in range(2):
        col = y if other == 0 else 1 - y
        for mat in range(mats):

            def step(slot, carry, other=other, mat=mat, col=col):
                first = pl.multiple_of(rowtab[base + mat, slot] * rows, rows)
                copy = pltpu.make_async_copy(
                    arrays[other].at[slot, base % 4 + mat],
                    dest.at[mat, col, pl.ds(first, rows), :],
                    sem,
                )
                if start:
                    copy.start()
                else:
                    copy.wait()
                return carry

            lax.fori_loop(0, n_dp, step, 0, unroll=n_dp <= 8)


def store_grads(slottab, staged, target, sem, mat, local, start):
    n_dp, _, rows, _ = target.shape

    def step(block, carry):
        copy = pltpu.make_async_copy(
            staged.at[pl.ds(pl.multiple_of(block * rows, rows), rows), :],
            target.at[slottab[mat, block], local],
            sem,
        )
        if start:
            copy.start()
        else:
            copy.wait()
        return carry

    lax.fori_loop(0, n_dp, step, 0, unroll=n_dp <= 8)


def layer_norm(x):
    mean = jnp.mean(x, axis=1, keepdims=True)
    centre = x - mean
    var = jnp.mean(centre * centre, axis=1, keepdims=True)
    inv = lax.rsqrt(var + norm_epsilon)
    return centre * inv, inv


def prep_kernel(w_ref, cond_ref, wp_ref, mod_ref):
    for k in range(8):
        wp_ref[k] = w_ref[:, k, :].astype(BF)
    for c in range(6):
        mod_ref[c] = nn_dot(cond_ref[c], w_ref[:, 8 + c, :].astype(BF))


def prep(weights, condk):
    rows = weights.shape[0]
    return pl.pallas_call(
        prep_kernel,
        out_shape=(
            jax.ShapeDtypeStruct((8, rows, CW), BF),
            jax.ShapeDtypeStruct((6, GROUPS, CW), F32),
        ),
        grid=(1,),
        in_specs=[whole(weights.shape), whole(condk.shape)],
        out_specs=(whole((8, rows, CW)), whole((6, GROUPS, CW))),
        compiler_params=params(),
        cost_estimate=cost(2e6, weights.size * 6),
        name="prep",
    )(weights, condk)


def rope(x, ct, s1, s2, sign):
    width = x.shape[1]
    up = pltpu.roll(x, 1, 1)
    down = pltpu.roll(x, width - 1, 1)
    reps = width // 128
    ct = jnp.concatenate([ct] * reps, axis=1) if reps > 1 else ct
    s1 = jnp.concatenate([s1] * reps, axis=1) if reps > 1 else s1
    s2 = jnp.concatenate([s2] * reps, axis=1) if reps > 1 else s2
    turn = up * s1 + down * s2
    return x * ct + turn if sign > 0 else x * ct - turn


def qkv_kernel(meta, rowtab, x_ref, vec_ref, ct_ref, s1_ref, s2_ref, wa, wb, h1_ref, q_ref, k_ref, v_ref, wsc, sem):
    @pl.when(pl.program_id(0) == 0)
    def _():
        fetch_weights(meta, rowtab, (wa, wb), wsc, sem, 3, 0, True)

    n1, _ = layer_norm(x_ref[...].astype(F32))
    h1 = (n1 * (1.0 + vec_ref[8:9, :]) + vec_ref[7:8, :]).astype(BF)
    h1_ref[...] = h1

    @pl.when(pl.program_id(0) == 0)
    def _():
        fetch_weights(meta, rowtab, (wa, wb), wsc, sem, 3, 0, False)

    c = meta[1]
    ct, s1, s2 = ct_ref[...], s1_ref[...], s2_ref[...]
    for col in range(2):
        off = pl.multiple_of((col * 2 + c) * CW, CW)
        for k, out in ((0, q_ref), (1, k_ref), (2, v_ref)):
            acc = nn_dot(h1, wsc[k, col]) + vec_ref[k : k + 1, pl.ds(off, CW)]
            if k < 2:
                acc = rope(acc, ct, s1, s2, 1.0)
            if k == 0:
                acc = acc * (LOG2E * HEAD_DIM**-0.5)
            out[:, col * CW : (col + 1) * CW] = acc.astype(BF)


def qkv(meta, rowtab, x, vec, tables, wa, wb):
    half = 2 * CW
    return pl.pallas_call(
        qkv_kernel,
        out_shape=(jax.ShapeDtypeStruct((LEN, D), BF),) + (jax.ShapeDtypeStruct((LEN, half), BF),) * 3,
        grid_spec=pltpu.PrefetchScalarGridSpec(
            num_scalar_prefetch=2,
            grid=(NT,),
            in_specs=[rows_spec(D), whole(vec.shape)] + [rows_spec(128)] * 3 + [ANY, ANY],
            out_specs=(rows_spec(D),) + (rows_spec(half),) * 3,
            scratch_shapes=[pltpu.VMEM((3, 2, D, CW), BF), pltpu.SemaphoreType.DMA(())],
        ),
        compiler_params=params(),
        cost_estimate=cost(2 * LEN * D * 3 * half, 12e6),
        name="qkv",
    )(meta, rowtab, x, vec, *tables, wa, wb)


def lane_iota(rows):
    return lax.broadcasted_iota(jnp.int32, (rows, 128), 1)


def split3(v):
    hi = v.astype(BF).astype(F32)
    mid = (v - hi).astype(BF).astype(F32)
    return hi, mid, v - hi - mid


def attend_kernel(meta, rowtab, q_ref, k_ref, v_ref, kaug_ref, wa, wb, o_ref, qaug_ref, pa_ref, wsc, osc, sem):
    @pl.when(pl.program_id(0) == 0)
    def _():
        fetch_weights(meta, rowtab, (wa, wb), wsc, sem, 1, 3, True)

    lane = lane_iota(TB)
    first = lane < HEAD_DIM
    mask_one = jnp.where(lane == 3, 1.0, 0.0).astype(BF)
    ones = jnp.ones((LEN, 128), BF)
    kaug = kaug_ref[...]

    def pair(p, carry):
        off = pl.multiple_of(p * 128, 128)
        q2 = q_ref[:, pl.ds(off, 128)]
        kcat = jnp.concatenate([k_ref[:, pl.ds(off, 128)], kaug], axis=1)
        vcat = jnp.concatenate([v_ref[:, pl.ds(off, 128)], ones], axis=1)
        outs = []
        for head in range(2):
            mine = first if head == 0 else jnp.logical_not(first)
            qm = jnp.where(mine, q2.astype(F32), 0.0).astype(BF)
            s = nt_dot(jnp.concatenate([qm, mask_one], axis=1), kcat)
            top = jnp.max(s, axis=1, keepdims=True)
            probs = jnp.exp2(s - top).astype(BF)
            acc = nn_dot(probs, vcat)
            total = acc[:, 128:256]
            outs.append(acc[:, :128] / total)
            lse = jnp.broadcast_to(top, (TB, 128)) + jnp.log(total) * LOG2E
            hi, mid, lo = split3(-lse)
            aug = jnp.where(lane == 0, hi, jnp.where(lane == 1, mid, jnp.where(lane == 2, lo, jnp.where(lane == 3, 1.0, 0.0))))
            qaug_ref[2 * p + head] = aug.astype(BF)
        osc[:, pl.ds(off, 128)] = jnp.where(first, outs[0], outs[1]).astype(BF)
        return carry

    lax.fori_loop(0, 4, pair, 0)
    o_ref[...] = osc[...]

    @pl.when(pl.program_id(0) == 0)
    def _():
        fetch_weights(meta, rowtab, (wa, wb), wsc, sem, 1, 3, False)

    pa = nt_dot(osc[:, :CW], wsc[0, 0]) + nt_dot(osc[:, CW:], wsc[0, 1])
    pa_ref[...] = pa.astype(BF)


def attend(meta, rowtab, q, k, v, kaug, wa, wb):
    half = 2 * CW
    return pl.pallas_call(
        attend_kernel,
        out_shape=(
            jax.ShapeDtypeStruct((LEN, half), BF),
            jax.ShapeDtypeStruct((8, LEN, 128), BF),
            jax.ShapeDtypeStruct((LEN, D), BF),
        ),
        grid_spec=pltpu.PrefetchScalarGridSpec(
            num_scalar_prefetch=2,
            grid=(NT,),
            in_specs=[rows_spec(half), whole((LEN, half)), whole((LEN, half)), whole((LEN, 128)), ANY, ANY],
            out_specs=(rows_spec(half), pl.BlockSpec((8, TB, 128), lambda i, *_: (0, i, 0)), rows_spec(D)),
            scratch_shapes=[
                pltpu.VMEM((1, 2, D, CW), BF),
                pltpu.VMEM((TB, half), BF),
                pltpu.SemaphoreType.DMA(()),
            ],
        ),
        compiler_params=params(),
        cost_estimate=cost(12e9, 10e6, 8e6),
        name="attend",
    )(meta, rowtab, q, k, v, kaug, wa, wb)


def middle_rows(x, pa, pb, vec, valid):
    a = (pa.astype(F32) + pb.astype(F32) + vec[3:4, :]) * valid
    return a, x.astype(F32) + vec[9:10, :] * a


def valid_rows(start, rows, length):
    return (start + lax.broadcasted_iota(jnp.int32, (rows, 1), 0) < length).astype(F32)


def gelu_parts(v):
    c0 = math.sqrt(2.0 / math.pi)
    sq = v * v
    t = jnp.tanh(v * (c0 + (c0 * 0.044715) * sq))
    half = 0.5 * (1.0 + t)
    slope = half + (0.5 * v) * (1.0 - t * t) * (c0 + (3.0 * c0 * 0.044715) * sq)
    return v * half, slope


def feed_kernel(
    meta, rowtab, slottab, x_ref, pa_ref, pb_ref, g_ref, vec_ref, wa, wb,
    pf_ref, pg_ref, gb_ref, keep_ref, send_ref,
    wsc, h2, gf, h2t, gft, facc, gacc, zsc, ghsc, stage, sem, gsem,
):
    y, c, length = meta[0], meta[1], meta[2]
    step = pl.program_id(0)
    other = jnp.where(step < 2, 1, 0)
    half = step % 2
    col = jnp.bitwise_xor(other, y)

    @pl.when(step == 0)
    def _():
        fetch_weights(meta, rowtab, (wa, wb), wsc, sem, 4, 4, True)
        gb_ref[...] = jnp.zeros_like(gb_ref)

        def rows(i, carry):
            at = pl.ds(pl.multiple_of(i * TB, TB), TB)
            _, x1 = middle_rows(x_ref[at, :], pa_ref[at, :], pb_ref[at, :], vec_ref, valid_rows(i * TB, TB, length))
            n2, _ = layer_norm(x1)
            hh = (n2 * (1.0 + vec_ref[11:12, :]) + vec_ref[10:11, :]).astype(BF)
            gg = (vec_ref[12:13, :] * g_ref[at, :].astype(F32)).astype(BF)
            h2[at, :] = hh
            gf[at, :] = gg
            h2t[:, at] = hh.T
            gft[:, at] = gg.T
            gb_ref[2:3, :] += jnp.sum(gg.astype(F32), axis=0, keepdims=True)
            return carry

        lax.fori_loop(0, NT, rows, 0)
        fetch_weights(meta, rowtab, (wa, wb), wsc, sem, 4, 4, False)

    off = pl.multiple_of((col * 2 + c) * CW, CW)
    w_in = wsc.at[half, col]
    w_out = wsc.at[2 + half, col]
    bias = vec_ref[pl.ds(4 + half, 1), pl.ds(off, CW)]

    def rows(i, total):
        at = pl.ds(pl.multiple_of(i * TB, TB), TB)
        z, slope = gelu_parts(nn_dot(h2[at, :], w_in[...]) + bias)
        zb = z.astype(BF)
        gh = nn_dot(gf[at, :], w_out[...]) * slope
        ghb = gh.astype(BF)
        zsc[at, :] = zb
        ghsc[at, :] = ghb
        fpart = nt_dot(zb, w_out[...])
        gpart = nt_dot(ghb, w_in[...])

        @pl.when(step == 0)
        def _():
            facc[at, :] = fpart
            gacc[at, :] = gpart

        @pl.when(step > 0)
        def _():
            facc[at, :] += fpart
            gacc[at, :] += gpart

        return total + jnp.sum(ghb.astype(F32), axis=0, keepdims=True)

    total = lax.fori_loop(0, NT, rows, jnp.zeros((1, CW), F32))
    gb_ref[pl.ds(half, 1), pl.ds(off, CW)] = total

    def copies(which, start):
        local = half + 2 * which

        @pl.when(other == 0)
        def _():
            store_grads(slottab, stage.at[which], keep_ref, gsem, 4 + local, local, start)

        @pl.when(other == 1)
        def _():
            store_grads(slottab, stage.at[which], send_ref, gsem, 4 + local, local, start)

    @pl.when(step > 0)
    def _():
        for which in range(2):
            store_grads(slottab, stage.at[which], keep_ref, gsem, 4, 0, False)

    for which, (lhs, rhs) in enumerate(((h2t, ghsc), (gft, zsc))):
        for r in range(NT):
            stage[which, r * TB : (r + 1) * TB, :] = nn_dot(lhs[r * TB : (r + 1) * TB, :], rhs[...]).astype(BF)
        copies(which, True)

    @pl.when(step == 3)
    def _():
        for which in range(2):
            store_grads(slottab, stage.at[which], keep_ref, gsem, 4, 0, False)
        pf_ref[...] = facc[...].astype(BF)
        pg_ref[...] = gacc[...].astype(BF)


def feed(meta, rowtab, slottab, x, pa, pb, g, vec, wa, wb):
    grads = jax.ShapeDtypeStruct(wa.shape[:1] + (4,) + wa.shape[2:], BF)
    return pl.pallas_call(
        feed_kernel,
        out_shape=(
            jax.ShapeDtypeStruct((LEN, D), BF),
            jax.ShapeDtypeStruct((LEN, D), BF),
            jax.ShapeDtypeStruct((8, D), F32),
            grads,
            grads,
        ),
        grid_spec=pltpu.PrefetchScalarGridSpec(
            num_scalar_prefetch=3,
            grid=(4,),
            in_specs=[whole((LEN, D))] * 4 + [whole(vec.shape), ANY, ANY],
            out_specs=(whole((LEN, D)), whole((LEN, D)), whole((8, D)), ANY, ANY),
            scratch_shapes=[
                pltpu.VMEM((4, 2, D, CW), BF),
                pltpu.VMEM((LEN, D), BF),
                pltpu.VMEM((LEN, D), BF),
                pltpu.VMEM((D, LEN), BF),
                pltpu.VMEM((D, LEN), BF),
                pltpu.VMEM((LEN, D), F32),
                pltpu.VMEM((LEN, D), F32),
                pltpu.VMEM((LEN, CW), BF),
                pltpu.VMEM((LEN, CW), BF),
                pltpu.VMEM((2, D, CW), BF),
                pltpu.SemaphoreType.DMA(()),
                pltpu.SemaphoreType.DMA(()),
            ],
        ),
        compiler_params=params(),
        cost_estimate=cost(2 * LEN * D * D * 6, 24e6, 1e6),
        name="feed",
    )(meta, rowtab, slottab, x, pa, pb, g, vec, wa, wb)


def proj_back_kernel(
    meta, rowtab, slottab, x_ref, pa_ref, pb_ref, g_ref, ga_ref, gb_ref, o_ref, vec_ref, wa, wb,
    gx_ref, go_ref, sums_ref, keep_ref, send_ref, wsc, wacc, stage, sem, gsem,
):
    y, length = meta[0], meta[2]
    step = pl.program_id(0)

    @pl.when(step == 0)
    def _():
        fetch_weights(meta, rowtab, (wa, wb), wsc, sem, 1, 3, True)
        sums_ref[...] = jnp.zeros_like(sums_ref)

    a, x1 = middle_rows(x_ref[...], pa_ref[...], pb_ref[...], vec_ref, valid_rows(step * TB, TB, length))
    n2, inv = layer_norm(x1)
    gh2 = ga_ref[...].astype(F32) + gb_ref[...].astype(F32)
    gn = gh2 * (1.0 + vec_ref[11:12, :])
    m0 = jnp.mean(gn, axis=1, keepdims=True)
    m1 = jnp.mean(gn * n2, axis=1, keepdims=True)
    gx = g_ref[...].astype(F32) + (gn - m0 - n2 * m1) * inv
    gx_ref[...] = gx
    gatt = (vec_ref[9:10, :] * gx * valid_rows(step * TB, TB, length)).astype(BF)
    sums_ref[0:1, :] += jnp.sum(gx * a, axis=0, keepdims=True)
    sums_ref[1:2, :] += jnp.sum(gh2, axis=0, keepdims=True)
    sums_ref[2:3, :] += jnp.sum(gh2 * n2, axis=0, keepdims=True)
    sums_ref[3:4, :] += jnp.sum(gatt.astype(F32), axis=0, keepdims=True)

    @pl.when(step == 0)
    def _():
        fetch_weights(meta, rowtab, (wa, wb), wsc, sem, 1, 3, False)

    go_ref[:, :CW] = nn_dot(gatt, wsc[0, 0]).astype(BF)
    go_ref[:, CW:] = nn_dot(gatt, wsc[0, 1]).astype(BF)
    part = nn_dot(gatt.T, o_ref[...])

    @pl.when(step == 0)
    def _():
        wacc[...] = part

    @pl.when(step > 0)
    def _():
        wacc[...] += part

    @pl.when(step == NT - 1)
    def _():
        for col in range(2):
            stage[col] = wacc[:, col * CW : (col + 1) * CW].astype(BF)
        store_grads(slottab, stage.at[y], keep_ref, gsem, 3, 0, True)
        store_grads(slottab, stage.at[1 - y], send_ref, gsem, 3, 0, True)
        store_grads(slottab, stage.at[y], keep_ref, gsem, 3, 0, False)
        store_grads(slottab, stage.at[1 - y], send_ref, gsem, 3, 0, False)


def proj_back(meta, rowtab, slottab, x, pa, pb, g, ga, gb, o, vec, wa, wb):
    grads = jax.ShapeDtypeStruct(wa.shape[:1] + (1,) + wa.shape[2:], BF)
    half = 2 * CW
    return pl.pallas_call(
        proj_back_kernel,
        out_shape=(
            jax.ShapeDtypeStruct((LEN, D), F32),
            jax.ShapeDtypeStruct((LEN, half), BF),
            jax.ShapeDtypeStruct((8, D), F32),
            grads,
            grads,
        ),
        grid_spec=pltpu.PrefetchScalarGridSpec(
            num_scalar_prefetch=3,
            grid=(NT,),
            in_specs=[rows_spec(D)] * 6 + [rows_spec(half), whole(vec.shape), ANY, ANY],
            out_specs=(rows_spec(D), rows_spec(half), whole((8, D)), ANY, ANY),
            scratch_shapes=[
                pltpu.VMEM((1, 2, D, CW), BF),
                pltpu.VMEM((D, half), F32),
                pltpu.VMEM((2, D, CW), BF),
                pltpu.SemaphoreType.DMA(()),
                pltpu.SemaphoreType.DMA(()),
            ],
        ),
        compiler_params=params(),
        cost_estimate=cost(2 * LEN * D * half * 2, 20e6),
        name="proj_back",
    )(meta, rowtab, slottab, x, pa, pb, g, ga, gb, o, vec, wa, wb)


def attend_back_kernel(
    q_ref, k_ref, v_ref, go_ref, o_ref, qaug_ref, kaug_ref, ct_ref, s1_ref, s2_ref,
    gq_ref, gk_ref, gv_ref, gb_ref, qcat, gocat, kt, gqt,
):
    lane = lane_iota(LEN)
    first = lane < HEAD_DIM
    lane_kb = lane_iota(TB)
    first_kb = lane_kb < HEAD_DIM
    vaug = jnp.where(lane_kb < 3, 1.0, 0.0).astype(BF)
    go2 = go_ref[...].astype(F32)
    q2 = q_ref[...].astype(F32)
    dots = go2 * o_ref[...].astype(F32)
    for head in range(2):
        mine = first if head == 0 else jnp.logical_not(first)
        qcat[head, :, :128] = jnp.where(mine, q2, 0.0).astype(BF)
        qcat[head, :, 128:] = qaug_ref[head]
        gocat[head, :, :128] = jnp.where(mine, go2, 0.0).astype(BF)
        inner = jnp.sum(jnp.where(mine, dots, 0.0), axis=1, keepdims=True)
        hi, mid, lo = split3(-jnp.broadcast_to(inner, (LEN, 128)))
        aug = jnp.where(lane == 0, hi, jnp.where(lane == 1, mid, jnp.where(lane == 2, lo, 0.0)))
        gocat[head, :, 128:] = aug.astype(BF)
    kt[...] = k_ref[...].T
    gqt[...] = jnp.zeros_like(gqt)
    gb_ref[...] = jnp.zeros_like(gb_ref)

    for kb in range(NT):
        at = slice(kb * TB, (kb + 1) * TB)
        kcat = jnp.concatenate([k_ref[at, :], kaug_ref[at, :]], axis=1)
        vcat = jnp.concatenate([v_ref[at, :], vaug], axis=1)
        gvs, gks = [], []
        for head in range(2):
            pt = jnp.exp2(nt_dot(kcat, qcat[head]))
            gpt = nt_dot(vcat, gocat[head])
            gst = (pt * gpt).astype(BF)
            gvs.append(nn_dot(pt.astype(BF), go_ref[...]))
            gks.append(nn_dot(gst, q_ref[...]))
            rows = slice(head * HEAD_DIM, (head + 1) * HEAD_DIM)
            gqt[rows, :] += nn_dot(kt[rows, at], gst)
        gv = jnp.where(first_kb, gvs[0], gvs[1]).astype(BF)
        gk = jnp.where(first_kb, gks[0], gks[1]) * LN2
        gk = rope(gk, ct_ref[at, :], s1_ref[at, :], s2_ref[at, :], -1.0).astype(BF)
        gv_ref[at, :] = gv
        gk_ref[at, :] = gk
        gb_ref[1:2, :] += jnp.sum(gk.astype(F32), axis=0, keepdims=True)
        gb_ref[2:3, :] += jnp.sum(gv.astype(F32), axis=0, keepdims=True)
    gq = gqt[...].T * (HEAD_DIM**-0.5)
    gq = rope(gq, ct_ref[...], s1_ref[...], s2_ref[...], -1.0).astype(BF)
    gq_ref[...] = gq
    gb_ref[0:1, :] += jnp.sum(gq.astype(F32), axis=0, keepdims=True)


def attend_back(q, k, v, go, o, qaug, kaug, tables):
    half = 2 * CW
    pair = pl.BlockSpec((LEN, 128), lambda i: (0, i))
    return pl.pallas_call(
        attend_back_kernel,
        out_shape=(jax.ShapeDtypeStruct((LEN, half), BF),) * 3 + (jax.ShapeDtypeStruct((8, half), F32),),
        grid=(4,),
        in_specs=[pair] * 5
        + [pl.BlockSpec((2, LEN, 128), lambda i: (i, 0, 0))]
        + [whole((LEN, 128))] * 4,
        out_specs=(pair,) * 3 + (pl.BlockSpec((8, 128), lambda i: (0, i)),),
        scratch_shapes=[
            pltpu.VMEM((2, LEN, 256), BF),
            pltpu.VMEM((2, LEN, 256), BF),
            pltpu.VMEM((128, LEN), BF),
            pltpu.VMEM((128, LEN), F32),
        ],
        compiler_params=params(),
        cost_estimate=cost(30e9, 12e6, 8e6),
        name="attend_back",
    )(q, k, v, go, o, qaug, kaug, *tables)


def qkv_back_kernel(
    meta, rowtab, slottab, h1_ref, gq_ref, gk_ref, gv_ref, wa, wb, pg_ref, keep_ref, send_ref,
    wsc, h1t, stage, sem, gsem,
):
    y = meta[0]
    fetch_weights(meta, rowtab, (wa, wb), wsc, sem, 3, 0, True)

    def turn(i, carry):
        at = pl.ds(pl.multiple_of(i * TB, TB), TB)
        h1t[:, at] = h1_ref[at, :].T
        return carry

    lax.fori_loop(0, NT, turn, 0)
    for yr in (1, 0):
        col = jnp.bitwise_xor(y, yr)
        off = pl.multiple_of(col * CW, CW)
        target = send_ref if yr == 1 else keep_ref
        for k, src in enumerate((gq_ref, gk_ref, gv_ref)):
            rhs = src[:, pl.ds(off, CW)]

            def rows(i, carry, k=k, rhs=rhs, yr=yr):
                at = pl.ds(pl.multiple_of(i * TB, TB), TB)
                stage[yr, k, at, :] = nn_dot(h1t[at, :], rhs).astype(BF)
                return carry

            lax.fori_loop(0, NT, rows, 0)
            store_grads(slottab, stage.at[yr, k], target, gsem, k, k, True)
    fetch_weights(meta, rowtab, (wa, wb), wsc, sem, 3, 0, False)

    def rows(i, carry):
        at = pl.ds(pl.multiple_of(i * TB, TB), TB)
        acc = jnp.zeros((TB, D), F32)
        for k, src in enumerate((gq_ref, gk_ref, gv_ref)):
            for col in range(2):
                acc += nt_dot(src[at, col * CW : (col + 1) * CW], wsc[k, col])
        pg_ref[at, :] = acc.astype(BF)
        return carry

    lax.fori_loop(0, NT, rows, 0)
    for yr in (1, 0):
        target = send_ref if yr == 1 else keep_ref
        for k in range(3):
            store_grads(slottab, stage.at[yr, k], target, gsem, k, k, False)


def qkv_back(meta, rowtab, slottab, h1, gq, gk, gv, wa, wb):
    grads = jax.ShapeDtypeStruct(wa.shape[:1] + (3,) + wa.shape[2:], BF)
    half = 2 * CW
    return pl.pallas_call(
        qkv_back_kernel,
        out_shape=(jax.ShapeDtypeStruct((LEN, D), BF), grads, grads),
        grid_spec=pltpu.PrefetchScalarGridSpec(
            num_scalar_prefetch=3,
            grid=(1,),
            in_specs=[whole((LEN, D))] + [whole((LEN, half))] * 3 + [ANY, ANY],
            out_specs=(whole((LEN, D)), ANY, ANY),
            scratch_shapes=[
                pltpu.VMEM((3, 2, D, CW), BF),
                pltpu.VMEM((D, LEN), BF),
                pltpu.VMEM((2, 3, D, CW), BF),
                pltpu.SemaphoreType.DMA(()),
                pltpu.SemaphoreType.DMA(()),
            ],
        ),
        compiler_params=params(),
        cost_estimate=cost(2 * LEN * D * half * 6, 16e6),
        name="qkv_back",
    )(meta, rowtab, slottab, h1, gq, gk, gv, wa, wb)


def final_kernel(
    meta, x_ref, pa_ref, pb_ref, g_ref, fa_ref, fb_ref, ga_ref, gb_ref, gx_ref, vec_ref,
    outk_ref, outs_ref, gink_ref, gins_ref, sums_ref, osc, isc,
):
    y, c, length = meta[0], meta[1], meta[2]
    step = pl.program_id(0)

    @pl.when(step == 0)
    def _():
        sums_ref[...] = jnp.zeros_like(sums_ref)

    _, x1 = middle_rows(x_ref[...], pa_ref[...], pb_ref[...], vec_ref, valid_rows(step * TB, TB, length))
    f = fa_ref[...].astype(F32) + fb_ref[...].astype(F32) + vec_ref[6:7, :]
    osc[...] = x1 + vec_ref[12:13, :] * f
    n1, inv = layer_norm(x_ref[...].astype(F32))
    gh1 = ga_ref[...].astype(F32) + gb_ref[...].astype(F32)
    gn = gh1 * (1.0 + vec_ref[8:9, :])
    m0 = jnp.mean(gn, axis=1, keepdims=True)
    m1 = jnp.mean(gn * n1, axis=1, keepdims=True)
    isc[...] = gx_ref[...] + (gn - m0 - n1 * m1) * inv
    sums_ref[0:1, :] += jnp.sum(gh1, axis=0, keepdims=True)
    sums_ref[1:2, :] += jnp.sum(gh1 * n1, axis=0, keepdims=True)
    sums_ref[2:3, :] += jnp.sum(g_ref[...].astype(F32) * f, axis=0, keepdims=True)
    mine = pl.ds(pl.multiple_of((y * 2 + c) * CW, CW), CW)
    theirs = pl.ds(pl.multiple_of(((1 - y) * 2 + c) * CW, CW), CW)
    outk_ref[...] = osc[:, mine].astype(BF)
    outs_ref[...] = osc[:, theirs].astype(BF)
    gink_ref[...] = isc[:, mine]
    gins_ref[...] = isc[:, theirs].astype(BF)


def final(meta, x, pa, pb, g, fa, fb, ga, gb, gx, vec):
    return pl.pallas_call(
        final_kernel,
        out_shape=(
            jax.ShapeDtypeStruct((LEN, CW), BF),
            jax.ShapeDtypeStruct((LEN, CW), BF),
            jax.ShapeDtypeStruct((LEN, CW), F32),
            jax.ShapeDtypeStruct((LEN, CW), BF),
            jax.ShapeDtypeStruct((8, D), F32),
        ),
        grid_spec=pltpu.PrefetchScalarGridSpec(
            num_scalar_prefetch=1,
            grid=(NT,),
            in_specs=[rows_spec(D)] * 9 + [whole(vec.shape)],
            out_specs=(rows_spec(CW),) * 4 + (whole((8, D)),),
            scratch_shapes=[pltpu.VMEM((TB, D), F32), pltpu.VMEM((TB, D), F32)],
        ),
        compiler_params=params(),
        cost_estimate=cost(1e8, 22e6),
        name="final",
    )(meta, x, pa, pb, g, fa, fb, ga, gb, gx, vec)


def xor_pairs(size, step):
    return [(i, i ^ step) for i in range(size)]


def swap(v, axis):
    return lax.ppermute(v, axis, SWAP)


def true_blocks(mine, other_y, y, c):
    cm, cy = swap(mine, "c"), swap(other_y, "c")
    flip_c = c == 1
    own0, own1 = jnp.where(flip_c, cm, mine), jnp.where(flip_c, mine, cm)
    oth0, oth1 = jnp.where(flip_c, cy, other_y), jnp.where(flip_c, other_y, cy)
    flip_y = y == 1
    return (
        jnp.where(flip_y, oth0, own0),
        jnp.where(flip_y, oth1, own1),
        jnp.where(flip_y, own0, oth0),
        jnp.where(flip_y, own1, oth1),
    )


def rotary_tables():
    half_dim = HEAD_DIM // 2
    places = jnp.arange(LEN, dtype=F32)
    frequencies = 10000.0 ** (-(jnp.arange(half_dim, dtype=F32) * 2.0 / HEAD_DIM))
    angles = places[:, None] * frequencies[None, :]
    pairs = jnp.tile(jnp.repeat(angles, 2, axis=1), (1, 2))
    odd = (jnp.arange(128) % 2 == 1)[None, :]
    cos, sin = jnp.cos(pairs), jnp.sin(pairs)
    return cos, jnp.where(odd, sin, 0.0), jnp.where(odd, 0.0, -sin)


def body(fast, block_in, out_grad, lengths, group_ids, time_embed, weights, first_moments, second_moments,
         owners, left_basis, right_basis, biases, bias_first, bias_second):
    highest = lax.Precision.HIGHEST
    rows = weights.shape[0]
    n_dp = owners.shape[1]
    z, x, y, c = (lax.axis_index(name) for name in ("z", "x", "y", "c"))
    dp = z * 2 + x
    slots = jnp.arange(n_dp, dtype=jnp.int32)
    if fast:
        blocks_of = jnp.bitwise_xor(slots % 4, z) * 2 + jnp.bitwise_xor(slots // 4, x)
        slot_of = jnp.bitwise_xor(slots // 2, z) + 4 * jnp.bitwise_xor(slots % 2, x)
    else:
        blocks_of = slots
        slot_of = slots
    hits = owners[:, :, None] == blocks_of[None, None, :]
    rowtab = jnp.sum(jnp.where(hits, slots[None, :, None], 0), axis=1).astype(jnp.int32)
    slottab = jnp.sum(
        jnp.where(owners[:, :, None] == slots[None, None, :], slot_of[None, None, :], 0), axis=2
    ).astype(jnp.int32)
    meta = jnp.stack([y, c, lengths[y]]).astype(jnp.int32)

    cond = jax.nn.silu(time_embed).astype(BF)
    own_rows = (owners[8:] == dp).astype(F32)
    condk = jnp.sum(
        own_rows[:, None, :, None] * cond.astype(F32).reshape(1, GROUPS, n_dp, rows), axis=2
    ).astype(BF)
    own_weights, mod_part = prep(weights, condk)

    def to_chip(v):
        mine = lax.dynamic_slice_in_dim(v, y * LEN, LEN, 0)
        other = lax.dynamic_slice_in_dim(v, (1 - y) * LEN, LEN, 0)
        return jnp.concatenate(true_blocks(mine, swap(other, "y"), y, c), axis=1)

    def gather(piece):
        piece = piece[None]
        if fast:
            parts = [piece] + [lax.ppermute(piece, "z", xor_pairs(4, s)) for s in (1, 2, 3)]
            four = jnp.concatenate(parts, axis=0)
            own = jnp.concatenate([four, swap(four, "x")], axis=0)
        else:
            own = lax.all_gather(piece, ("z", "x"), axis=0, tiled=True)
        return own, swap(own, "y")

    xs = to_chip(block_in)
    w_attn = gather(own_weights[:4])
    w_feed = gather(own_weights[4:])
    gs = to_chip(out_grad)

    if fast:
        mod_all = mod_part
        for axis, size, step in (("x", 2, 1), ("z", 4, 1), ("z", 4, 2)):
            mod_all = mod_all + lax.ppermute(mod_all, axis, xor_pairs(size, step))
    else:
        mod_all = lax.psum(mod_part, ("z", "x"))

    def utterance_rows(index):
        hit = (jnp.arange(GROUPS) == group_ids[index]).astype(F32)
        mods = jnp.sum(mod_all * hit[None, :, None], axis=1) + biases[7:]
        return jnp.concatenate([biases[:7], mods, jnp.zeros((3, CW), F32)], axis=0)

    vec = jnp.concatenate(
        true_blocks(utterance_rows(y), swap(utterance_rows(1 - y), "y"), y, c), axis=1
    )
    tables = rotary_tables()
    lane = jnp.arange(128)[None, :]
    padded = (jnp.arange(LEN, dtype=jnp.int32) >= meta[2])[:, None]
    kaug = jnp.where(lane < 3, 1.0, jnp.where((lane == 3) & padded, masked_score, 0.0)).astype(BF)

    h1, q, k, v = qkv(meta, rowtab, xs, vec, tables, *w_attn)
    o, qaug, pa = attend(meta, rowtab, q, k, v, kaug, *w_attn)
    pb = swap(pa, "c")
    fa, g2a, gb_feed, keep_feed, send_feed = feed(meta, rowtab, slottab, xs, pa, pb, gs, vec, *w_feed)
    g2b = swap(g2a, "c")
    fb = swap(fa, "c")

    def scatter(keep, send):
        got = swap(send, "y")
        if fast:
            total = keep.astype(F32) + got.astype(F32)
            low = total[4:].astype(BF)
            four = total[:4] + swap(low, "x").astype(F32)
            own = four[0]
            for s in (1, 2, 3):
                own = own + lax.ppermute(four[s].astype(BF), "z", xor_pairs(4, s)).astype(F32)
            return own
        total = (keep.astype(F32) + got.astype(F32)).astype(BF)
        return lax.psum_scatter(total, ("z", "x"), scatter_dimension=0, tiled=True)[0].astype(F32)

    grads_feed = scatter(keep_feed, send_feed)
    gx, go, sums_mid, keep_proj, send_proj = proj_back(
        meta, rowtab, slottab, xs, pa, pb, gs, g2a, g2b, o, vec, *w_attn
    )
    grads_proj = scatter(keep_proj, send_proj)
    gq, gk, gv, gb_qkv = attend_back(q, k, v, go, o, qaug, kaug, tables)
    g1a, keep_qkv, send_qkv = qkv_back(meta, rowtab, slottab, h1, gq, gk, gv, *w_attn)
    g1b = swap(g1a, "c")
    grads_qkv = scatter(keep_qkv, send_qkv)
    out_keep, out_send, gin_keep, gin_send, sums_end = final(
        meta, xs, pa, pb, gs, fa, fb, g1a, g1b, gx, vec
    )
    out_got = swap(out_send, "y")
    gin_got = swap(gin_send, "y").astype(F32)

    def both(mine, other):
        return jnp.where(
            y == 0, jnp.concatenate([mine, other], axis=0), jnp.concatenate([other, mine], axis=0)
        )

    block_out = both(out_keep, out_got)
    input_grad = both(gin_keep, gin_got)

    local = jnp.stack(
        [
            jnp.concatenate(
                [
                    gb_qkv[:3, col * CW : (col + 1) * CW],
                    lax.dynamic_slice_in_dim(
                        jnp.concatenate(
                            [sums_mid[3:4], gb_feed[:3], sums_end[:2], sums_mid[:3], sums_end[2:3]], axis=0
                        ),
                        (col * 2 + c) * CW,
                        CW,
                        1,
                    ),
                ],
                axis=0,
            )
            for col in range(2)
        ]
    )
    hot = (jnp.arange(CW) == group_ids[y]).astype(F32)
    local = jnp.concatenate([local, jnp.broadcast_to(hot[None, None], (2, 3, CW))], axis=1)
    mine = jnp.where(y == 0, local[0], local[1])
    other = jnp.where(y == 0, local[1], local[0])
    vecs = jnp.stack([mine, swap(other, "y")])
    if fast:
        everything = [vecs]
        for zs in range(4):
            for xstep in range(2):
                if zs or xstep:
                    everything.append(
                        lax.ppermute(
                            vecs,
                            ("z", "x"),
                            [(i * 2 + j, (i ^ zs) * 2 + (j ^ xstep)) for i in range(4) for j in range(2)],
                        )
                    )
        everything = jnp.concatenate(everything, axis=0)
    else:
        everything = lax.all_gather(vecs, ("z", "x"), axis=0, tiled=True)
    bias_grad = jnp.sum(everything[:, :13], axis=0)
    grouped = jnp.einsum("ug,ukc->kgc", everything[:, 13, :GROUPS], everything[:, 7:13], precision=highest)
    grads_mod = jnp.einsum("kgr,kgc->krc", condk.astype(F32), grouped, precision=highest)
    reduced = jnp.concatenate([grads_qkv, grads_proj, grads_feed, grads_mod], axis=0)

    turned = jnp.einsum("kij,kic->kjc", left_basis, reduced, precision=highest)
    turned = jnp.einsum("kjc,kce->kje", turned, right_basis, precision=highest)
    first_old = jnp.transpose(first_moments, (1, 0, 2))
    second_old = jnp.transpose(second_moments, (1, 0, 2))
    first_new = soap_first * first_old + (1.0 - soap_first) * turned
    second_new = soap_second * second_old + (1.0 - soap_second) * turned * turned
    direction = (
        first_new
        / (1.0 - soap_first**STEP)
        / (jnp.sqrt(second_new / (1.0 - soap_second**STEP)) + soap_epsilon)
    )
    rotated_back = jnp.einsum("kij,kje->kie", left_basis, direction, precision=highest)
    rotated_back = jnp.einsum("kie,kce->ikc", rotated_back, right_basis, precision=highest)
    new_weights = weights - soap_rate * (rotated_back + soap_decay * weights)
    bias_first_new = vector_first * bias_first + (1.0 - vector_first) * bias_grad
    bias_second_new = vector_second * bias_second + (1.0 - vector_second) * bias_grad * bias_grad
    new_biases = biases - vector_rate * (bias_first_new / (1.0 - vector_first**STEP)) / (
        jnp.sqrt(bias_second_new / (1.0 - vector_second**STEP)) + vector_epsilon
    )
    back = lambda v: jnp.transpose(v, (1, 0, 2))
    return (
        block_out,
        input_grad,
        back(reduced),
        back(first_new),
        back(second_new),
        new_weights,
        new_weights.astype(BF),
        bias_first_new,
        bias_second_new,
        new_biases,
    )


def solution(mesh):
    n_dp = mesh.shape["dp"]
    fine = Mesh(mesh.devices.reshape(n_dp // 2, 2, 2, 2), ("z", "x", "y", "c"))
    dp, mp = ("z", "x"), ("y", "c")
    return jax.shard_map(
        functools.partial(body, n_dp == 8),
        mesh=fine,
        in_specs=(
            P(dp, mp),
            P(dp, mp),
            P(dp),
            P(dp),
            P(),
            P(dp, None, mp),
            P(dp, None, mp),
            P(dp, None, mp),
            P(),
            P(None, dp, None),
            P(None, mp, None),
            P(None, mp),
            P(None, mp),
            P(None, mp),
        ),
        out_specs=(
            P(dp, mp),
            P(dp, mp),
            P(dp, None, mp),
            P(dp, None, mp),
            P(dp, None, mp),
            P(dp, None, mp),
            P(dp, None, mp),
            P(None, mp),
            P(None, mp),
            P(None, mp),
        ),
        check_vma=False,
    )
```

time: 1070 us -> 531 us (0.50)
  waiting for transfers between devices: 413 us -> 213 us
  matrix products: 198 us -> 16 us
  Pallas kernels: 0 us -> 150 us
  other arithmetic: 186 us -> 42 us
  local copies, waits for them, and re-layouts: 166 us -> 47.9 us
  blocking collectives: 82.9 us -> 0 us
  starting transfers between devices: 1.87 us -> 50 us
  between operations: 16.6 us -> 1.91 us
    reduce_scatter x9 -> x0, waiting for transfers between devices: 215 us -> none  [the longest x4 93.9 us: branch_total(): lax.psum_scatter(partial_rows.astype(jnp.bfloat16), 'mp', scatter_dimensi...]
    ppermute x0 -> x51, waiting for transfers between devices: none -> 213 us  [the longest x26 121 us: swap(): return lax.ppermute(v, axis, SWAP)]
    all_gather x10 -> x0, waiting for transfers between devices: 197 us -> none  [the longest x4 56.9 us: branch_spread(): return lax.all_gather(grad_rows, 'mp', axis=1, tiled=True)]
    dot_general x55 -> x6, matrix products: 198 us -> 16 us  [the longest x1 5.62 us: body(): jnp.einsum('kie,kce->ikc', rotated_back, right_basis, precision=highest)]
    pallas_call x0 -> x8, Pallas kernels: none -> 150 us  [the longest x1 34.2 us: feed(): pl.pallas_call(feed_kernel, out_shape=(jax.ShapeDtypeStruct((LEN, D), BF)...]
    psum x5 -> x0, blocking collectives: 82.9 us -> none  [the longest x1 39.8 us: body(): bias_grad = lax.psum(bias_local, 'dp')]
    another operation x24 -> x7, other arithmetic: 67.4 us -> 4.69 us
    gather x28 -> x0, local copies, waits for them, and re-layouts: 59.3 us -> none  [the longest x14 32.5 us: stored_order(): jnp.take(blocks[:, :, slot_index, :], jnp.argsort(owners[slot_index]), ax...]
  transfers between devices with their start and end apart: 19 -> 51, of which waited for: 17 -> 22; matrix products, arithmetic and copies ran while one was open for 25% -> 17% of each run, Pallas kernels for 0% -> 21%
where the time goes in v1:
time: 531 us; the launch traced here: 522 us
  waiting for transfers between devices  213 us (40%)
  Pallas kernels  150 us (28%)
  starting transfers between devices  50 us (9%)
  local copies, waits for them, and re-layouts  47.9 us (9%)
  other arithmetic  42 us (8%)
  matrix products  16 us (3%)
    ppermute x26, waiting for transfers between devices, swap(): return lax.ppermute(v, axis, SWAP)  121 us
    ppermute x7, waiting for transfers between devices, body(): lax.ppermute(vecs, ('z', 'x'), [(i * 2 + j, (i ^ zs) * 2 + (j ^ xstep)) f...  36.5 us
    ppermute x9, waiting for transfers between devices, scatter(): lax.ppermute(four[s].astype(BF), 'z', xor_pairs(4, s)).astype(F32)  35.8 us
    pallas_call x1, Pallas kernels, feed(): pl.pallas_call(feed_kernel, out_shape=(jax.ShapeDtypeStruct((LEN, D), BF)...  34.2 us
    pallas_call x1, Pallas kernels, attend_back(): pl.pallas_call(attend_back_kernel, out_shape=(jax.ShapeDtypeStruct((LEN,...  28.9 us
    pallas_call x1, Pallas kernels, attend(): pl.pallas_call(attend_kernel, out_shape=(jax.ShapeDtypeStruct((LEN, half)...  25.1 us
    ppermute x26, starting transfers between devices, swap(): return lax.ppermute(v, axis, SWAP)  20.4 us
    ppermute x3, waiting for transfers between devices, body(): mod_all = mod_all + lax.ppermute(mod_all, axis, xor_pairs(size, step))  20.1 us
  transfers between devices with their start and end apart: 51, of which 22 were waited for; matrix products, arithmetic and copies ran while one was open for 17% of the time, Pallas kernels for 21%

profile of v1, /device:TPU:0, one launch (start us, length us, event | category | flops | bytes accessed | tf_op | source)
XLA Modules:
  0.0 521.6 jit_solution(18074608450759985292)
XLA Ops:
  2.4 3.9 copy.40.w_ref
  7.0 5.6 %prep.1 = (bf16[8,128,256]{2,1,0:T(8,128)(2,1)}, f32[6,8,256]{2,1,0:T(8,128)}) custom-call(f32[128,14,256]{2,1,0:T(8,128)} %copy.40.w_ref, bf16[6,8,128]{2,1,0:T(8,128)(2,1)} %multiply_reduce_fusion.cond_ref), custom_call_target="tpu_custom_call" | custom-call | flops 2000000 | bytes 2752512 | tf_op jit(solution)/shard_map/prep/pallas_call | solution.py:128
  12.6 1.9 slice_bitcast_fusion.5
  14.4 5.0 collective-permute-start.11
  21.8 3.6 collective-permute-start.20
  40.6 8.1 %collective-permute-done.4 = f32[6,8,256]{2,1,0:T(8,128)S(1)} collective-permute-done((f32[6,8,256]{2,1,0:T(8,128)S(1)}, f32[6,8,256]{2,1,0:T(8,128)S(1)}, u32[]{:S(2)}, u32[]{:S(2)}) %collective-permute-start.4) | collective-permute-done | bytes 49184 | tf_op jit(solution)/shard_map/ppermute | solution.py:791
  49.0 2.7 collective-permute-start.5
  54.6 12.1 %collective-permute-done.5 = f32[6,8,256]{2,1,0:T(8,128)S(1)} collective-permute-done((f32[6,8,256]{2,1,0:T(8,128)S(1)}, f32[6,8,256]{2,1,0:T(8,128)S(1)}, u32[]{:S(2)}, u32[]{:S(2)}) %collective-permute-start.5) | collective-permute-done | bytes 49184 | tf_op jit(solution)/shard_map/ppermute | solution.py:791
  73.6 4.1 collective-permute-done.12
  87.9 1.8 cos.14
  91.5 2.0 copy.44.ct_ref
  94.7 43.1 %collective-permute-done = bf16[1024,256]{1,0:T(8,128)(2,1)} collective-permute-done((bf16[1024,256]{1,0:T(8,128)(2,1)}, bf16[1024,256]{1,0:T(8,128)(2,1)}, u32[]{:S(2)}, u32[]{:S(2)}) %collective-permute-start) | collective-permute-done | bytes 524320 | tf_op jit(solution)/shard_map/ppermute | solution.py:712
  137.7 8.8 %collective-permute-done.15 = bf16[1024,256]{1,0:T(8,128)(2,1)} collective-permute-done((bf16[1024,256]{1,0:T(8,128)(2,1)}, bf16[1024,256]{1,0:T(8,128)(2,1)}, u32[]{:S(2)}, u32[]{:S(2)}) %collective-permute-start.15) | collective-permute-done | bytes 524320 | tf_op jit(solution)/shard_map/ppermute | solution.py:712
  155.1 3.2 broadcast_select_fusion.11
  159.9 13.6 %collective-permute-done.21 = bf16[4,4,128,256]{3,2,1,0:T(8,128)(2,1)S(1)} collective-permute-done((bf16[4,4,128,256]{3,2,1,0:T(8,128)(2,1)S(1)}, bf16[4,4,128,256]{3,2,1,0:T(8,128)(2,1)S(1)}, u32[]{:S(2)}, u32[]{:S(2)}) %collective-permute-start.21) | collective-permute-done | bytes 1048608 | tf_op jit(solution)/shard_map/ppermute | solution.py:712
  176.1 11.1 %qkv.1 = (bf16[1024,1024]{1,0:T(8,128)(2,1)}, bf16[1024,512]{1,0:T(8,128)(2,1)}, bf16[1024,512]{1,0:T(8,128)(2,1)}, bf16[1024,512]{1,0:T(8,128)(2,1)}) custom-call(s32[3]{0:T(128)} %pad_add_fusion.meta, s32[14,8]{1,0:T(8,128)} %copy.45.rowtab, bf16[1024,1024]{1,0:T(8,128)(2,1)} %pad_maximum_fusion.x_ref, f32[16,1024]{1,0:T(8,128)} %pad_maximum_fusion.6.vec_ref, ...), custom_call_target="tpu_custom_call" | custom-call | flops 3221225472 | bytes 12000000 | tf_op jit(solution)/shard_map/qkv/pallas_call | solution.py:183
  187.2 25.1 %attend.1 = (bf16[1024,512]{1,0:T(8,128)(2,1)}, bf16[8,1024,128]{2,1,0:T(8,128)(2,1)}, bf16[1024,1024]{1,0:T(8,128)(2,1)}) custom-call(s32[3]{0:T(128)} %pad_add_fusion.meta, s32[14,8]{1,0:T(8,128)} %copy.45.rowtab, bf16[1024,512]{1,0:T(8,128)(2,1)} %get-tuple-element.43.q_ref, bf16[1024,512]{1,0:T(8,128)(2,1)} %get-tuple-element.44.k_ref, ...), custom_call_target="tpu_custom_call" | custom-call | flops 12000000000 | bytes 10000000 | tf_op jit(solution)/shard_map/attend/pallas_call | solution.py:255
  213.8 3.0 pad_maximum_fusion.1.g_ref
  216.8 5.3 %collective-permute-done.22.wb = bf16[8,4,128,256]{3,2,1,0:T(8,128)(2,1)} collective-permute-done((bf16[8,4,128,256]{3,2,1,0:T(8,128)(2,1)}, bf16[8,4,128,256]{3,2,1,0:T(8,128)(2,1)}, u32[]{:S(2)}, u32[]{:S(2)}) %collective-permute-start.22) | collective-permute-done | bytes 2097184 | tf_op jit(solution)/shard_map/ppermute | solution.py:712
  223.5 34.2 %feed.1 = (bf16[1024,1024]{1,0:T(8,128)(2,1)}, bf16[1024,1024]{1,0:T(8,128)(2,1)}, f32[8,1024]{1,0:T(8,128)}, bf16[8,4,128,256]{3,2,1,0:T(8,128)(2,1)}, bf16[8,4,128,256]{3,2,1,0:T(8,128)(2,1)}) custom-call(s32[3]{0:T(128)} %pad_add_fusion.meta, s32[14,8]{1,0:T(8,128)} %copy.45.rowtab, s32[14,8]{1,0:T(8,128)} %copy.47.slottab, ...), custom_call_target="tpu_custom_call" | custom-call | flops 12884901888 | bytes 24000000 | tf_op jit(solution)/shard_map/feed/pallas_call | solution.py:391
  259.8 44.5 %collective-permute-done.38 = bf16[8,4,128,256]{3,2,1,0:T(8,128)(2,1)S(1)} collective-permute-done((bf16[8,4,128,256]{3,2,1,0:T(8,128)(2,1)}, bf16[8,4,128,256]{3,2,1,0:T(8,128)(2,1)S(1)}, u32[]{:S(2)}, u32[]{:S(2)}) %collective-permute-start.38) | collective-permute-done | bytes 2097184 | tf_op jit(solution)/shard_map/ppermute | solution.py:712
  304.3 2.3 convert_add_fusion
  306.6 2.0 copy-done.2
  311.6 14.9 %proj_back.1 = (f32[1024,1024]{1,0:T(8,128)}, bf16[1024,512]{1,0:T(8,128)(2,1)}, f32[8,1024]{1,0:T(8,128)}, bf16[8,1,128,256]{3,2,1,0:T(8,128)(2,1)}, bf16[8,1,128,256]{3,2,1,0:T(8,128)(2,1)}) custom-call(s32[3]{0:T(128)} %pad_add_fusion.meta, s32[14,8]{1,0:T(8,128)} %copy.45.rowtab, s32[14,8]{1,0:T(8,128)} %copy.47.slottab, ...), custom_call_target="tpu_custom_call" | custom-call | flops 2147483648 | bytes 20000000 | tf_op jit(solution)/shard_map/proj_back/pallas_call | solution.py:481
  328.1 28.9 %attend_back.1 = (bf16[1024,512]{1,0:T(8,128)(2,1)}, bf16[1024,512]{1,0:T(8,128)(2,1)}, bf16[1024,512]{1,0:T(8,128)(2,1)}, f32[8,512]{1,0:T(8,128)}) custom-call(bf16[1024,512]{1,0:T(8,128)(2,1)} %get-tuple-element.43.q_ref, bf16[1024,512]{1,0:T(8,128)(2,1)} %get-tuple-element.44.k_ref, bf16[1024,512]{1,0:T(8,128)(2,1)} %get-tuple-element.45.v_ref, ...), custom_call_target="tpu_custom_call" | custom-call | flops 30000001024 | bytes 12000000 | tf_op jit(solution)/shard_map/attend_back/pallas_call | solution.py:563
  357.8 17.3 %qkv_back.1 = (bf16[1024,1024]{1,0:T(8,128)(2,1)}, bf16[8,3,128,256]{3,2,1,0:T(8,128)(2,1)}, bf16[8,3,128,256]{3,2,1,0:T(8,128)(2,1)}) custom-call(s32[3]{0:T(128)} %pad_add_fusion.meta, s32[14,8]{1,0:T(8,128)} %copy.45.rowtab, s32[14,8]{1,0:T(8,128)} %copy.47.slottab, bf16[1024,1024]{1,0:T(8,128)(2,1)} %get-tuple-element.48.h1_ref, ...), custom_call_target="tpu_custom_call" | custom-call | flops 6442450944 | bytes 16000000 | tf_op jit(solution)/shard_map/qkv_back/pallas_call | solution.py:631
  376.1 2.3 fusion.56
  381.9 2.2 collective-permute-start.37
  384.1 5.5 %collective-permute-done.35 = bf16[1,128,256]{2,1,0:T(8,128)(2,1)} collective-permute-done((bf16[1,128,256]{2,1,0:T(8,128)(2,1)S(1)}, bf16[1,128,256]{2,1,0:T(8,128)(2,1)}, u32[]{:S(2)}, u32[]{:S(2)}) %collective-permute-start.35) | collective-permute-done | bytes 65568 | tf_op jit(solution)/shard_map/ppermute | solution.py:823
  394.0 3.2 collective-permute-done.36
  397.2 1.9 collective-permute-start.42
  404.9 3.6 collective-permute-done.42
  408.5 12.5 %collective-permute-done.41 = bf16[4,128,256]{2,1,0:T(8,128)(2,1)S(1)} collective-permute-done((bf16[4,128,256]{2,1,0:T(8,128)(2,1)S(1)}, bf16[4,128,256]{2,1,0:T(8,128)(2,1)S(1)}, u32[]{:S(2)}, u32[]{:S(2)}) %collective-permute-start.41) | collective-permute-done | bytes 262176 | tf_op jit(solution)/shard_map/ppermute | solution.py:823
  422.1 13.4 %final.1 = (bf16[1024,256]{1,0:T(8,128)(2,1)}, bf16[1024,256]{1,0:T(8,128)(2,1)}, f32[1024,256]{1,0:T(8,128)}, bf16[1024,256]{1,0:T(8,128)(2,1)}, f32[8,1024]{1,0:T(8,128)}) custom-call(s32[3]{0:T(128)} %pad_add_fusion.meta, bf16[1024,1024]{1,0:T(8,128)(2,1)} %pad_maximum_fusion.x_ref, bf16[1024,1024]{1,0:T(8,128)(2,1)} %get-tuple-element.46.pa_ref, ...), custom_call_target="tpu_custom_call" | custom-call | flops 100000000 | bytes 22000000 | tf_op jit(solution)/shard_map/final/pallas_call | solution.py:685
  437.7 1.9 convert_add_fusion.1
  443.3 2.2 collective-permute-start.50
  446.4 13.3 %collective-permute-done.44 = f32[2,16,256]{2,1,0:T(8,128)S(1)} collective-permute-done((f32[2,16,256]{2,1,0:T(8,128)S(1)}, f32[2,16,256]{2,1,0:T(8,128)S(1)}, u32[]{:S(2)}, u32[]{:S(2)}) %collective-permute-start.44) | collective-permute-done | bytes 32800 | tf_op jit(solution)/shard_map/ppermute | solution.py:881
  459.7 4.2 collective-permute-done.45
  463.9 4.9 collective-permute-done.46
  468.9 4.8 collective-permute-done.47
  474.4 4.9 collective-permute-done.48
  481.1 4.5 collective-permute-done.49
  491.0 5.4 %collective-permute-done.30 = bf16[3,128,256]{2,1,0:T(8,128)(2,1)S(1)} collective-permute-done((bf16[3,128,256]{2,1,0:T(8,128)(2,1)S(1)}, bf16[3,128,256]{2,1,0:T(8,128)(2,1)S(1)}, u32[]{:S(2)}, u32[]{:S(2)}) %collective-permute-start.30) | collective-permute-done | bytes 196640 | tf_op jit(solution)/shard_map/ppermute | solution.py:823
  496.4 4.3 collective-permute-done.31
  500.8 1.8 fusion.16
  503.3 4.7 fusion
  507.9 3.1 fusion.3
  511.1 5.6 %fusion.59 = (bf16[128,14,256]{2,0,1:T(8,128)(2,1)}, f32[128,14,256]{2,0,1:T(8,128)}) fusion(f32[128,14,256]{2,0,1:T(8,128)S(1)} %copy-done.4, f32[14,256,128]{1,2,0:T(8,128)S(1)} %fusion.3, f32[14,256,256]{2,1,0:T(8,128)S(1)} %copy-done.1), kind=kOutput, calls=%fused_computation.185 | convolution fusion | flops 1411579904 | bytes 10092544 | tf_op jit(solution)/shard_map/kie,kce->ikc/dot_general | solution.py:907
  (245 shorter events, 101.4 us)
Async XLA Ops:
  14.4 34.5 %collective-permute-start.11 = (bf16[1,4,128,256]{3,2,1,0:T(8,128)(2,1)}, bf16[1,4,128,256]{3,2,1,0:T(8,128)(2,1)}, u32[]{:S(2)}, u32[]{:S(2)}) collective-permute-start(bf16[1,4,128,256]{3,2,1,0:T(8,128)(2,1)} %get-tuple-element.110), channel_id=1, source_target_pairs={{0,24},{8,16},{16,8},{24,0},{1,25},{9,17},{17,9},{25,1},{2,26},{10... | collective-permute-start | bytes 786440 | tf_op jit(solution)/shard_map/ppermute | solution.py:776
  19.5 32.2 %collective-permute-start.10 = (bf16[1,4,128,256]{3,2,1,0:T(8,128)(2,1)}, bf16[1,4,128,256]{3,2,1,0:T(8,128)(2,1)}, u32[]{:S(2)}, u32[]{:S(2)}) collective-permute-start(bf16[1,4,128,256]{3,2,1,0:T(8,128)(2,1)} %get-tuple-element.110), channel_id=1, source_target_pairs={{0,16},{8,24},{16,0},{24,8},{1,17},{9,25},{17,1},{25,9},{2,18},{10... | collective-permute-start | bytes 786440 | tf_op jit(solution)/shard_map/ppermute | solution.py:776
  19.5 32.2 %collective-permute-start.9 = (bf16[1,4,128,256]{3,2,1,0:T(8,128)(2,1)}, bf16[1,4,128,256]{3,2,1,0:T(8,128)(2,1)}, u32[]{:S(2)}, u32[]{:S(2)}) collective-permute-start(bf16[1,4,128,256]{3,2,1,0:T(8,128)(2,1)} %get-tuple-element.110), channel_id=1, source_target_pairs={{0,8},{8,0},{16,24},{24,16},{1,9},{9,1},{17,25},{25,17},{2,10},{10... | collective-permute-start | bytes 786440 | tf_op jit(solution)/shard_map/ppermute | solution.py:776
  20.1 18.3 %collective-permute-start.3 = (f32[6,8,256]{2,1,0:T(8,128)}, f32[6,8,256]{2,1,0:T(8,128)}, u32[]{:S(2)}, u32[]{:S(2)}) collective-permute-start(f32[6,8,256]{2,1,0:T(8,128)} %get-tuple-element.41), channel_id=1, source_target_pairs={{0,4},{4,0},{1,5},{5,1},{2,6},{6,2},{3,7},{7,3},{8,12},{12,8},{9,1... | collective-permute-start | bytes 147464 | tf_op jit(solution)/shard_map/ppermute | solution.py:791
  21.8 60.7 %collective-permute-start.20 = (bf16[1,4,128,256]{3,2,1,0:T(8,128)(2,1)}, bf16[1,4,128,256]{3,2,1,0:T(8,128)(2,1)}, u32[]{:S(2)}, u32[]{:S(2)}) collective-permute-start(bf16[1,4,128,256]{3,2,1,0:T(8,128)(2,1)} %get-tuple-element.109), channel_id=1, source_target_pairs={{0,24},{8,16},{16,8},{24,0},{1,25},{9,17},{17,9},{25,1},{2,26},{10... | collective-permute-start | bytes 786440 | tf_op jit(solution)/shard_map/ppermute | solution.py:776
  39.2 9.5 %collective-permute-start.4 = (f32[6,8,256]{2,1,0:T(8,128)S(1)}, f32[6,8,256]{2,1,0:T(8,128)S(1)}, u32[]{:S(2)}, u32[]{:S(2)}) collective-permute-start(f32[6,8,256]{2,1,0:T(8,128)S(1)} %add.191), channel_id=1, source_target_pairs={{0,8},{8,0},{16,24},{24,16},{1,9},{9,1},{17,25},{25,17},{2,10},{10... | collective-permute-start | bytes 147464 | tf_op jit(solution)/shard_map/ppermute | solution.py:791
  48.7 34.6 %collective-permute-start.19 = (bf16[1,4,128,256]{3,2,1,0:T(8,128)(2,1)}, bf16[1,4,128,256]{3,2,1,0:T(8,128)(2,1)}, u32[]{:S(2)}, u32[]{:S(2)}) collective-permute-start(bf16[1,4,128,256]{3,2,1,0:T(8,128)(2,1)} %get-tuple-element.109), channel_id=1, source_target_pairs={{0,16},{8,24},{16,0},{24,8},{1,17},{9,25},{17,1},{25,9},{2,18},{10... | collective-permute-start | bytes 786440 | tf_op jit(solution)/shard_map/ppermute | solution.py:776
  49.0 17.7 %collective-permute-start.5 = (f32[6,8,256]{2,1,0:T(8,128)S(1)}, f32[6,8,256]{2,1,0:T(8,128)S(1)}, u32[]{:S(2)}, u32[]{:S(2)}) collective-permute-start(f32[6,8,256]{2,1,0:T(8,128)S(1)} %add.192), channel_id=1, source_target_pairs={{0,16},{8,24},{16,0},{24,8},{1,17},{9,25},{17,1},{25,9},{2,18},{10... | collective-permute-start | bytes 147464 | tf_op jit(solution)/shard_map/ppermute | solution.py:791
  53.0 24.6 %collective-permute-start.12 = (bf16[4,4,128,256]{3,2,1,0:T(8,128)(2,1)S(1)}, bf16[4,4,128,256]{3,2,1,0:T(8,128)(2,1)S(1)}, u32[]{:S(2)}, u32[]{:S(2)}) collective-permute-start(bf16[4,4,128,256]{3,2,1,0:T(8,128)(2,1)S(1)} %pad_maximum_fusion.4), channel_id=1, source_target_pairs={{0,4},{4,0},{1,5},{5,1},{2,6},{6,2},{3,7},{7,3},{8,12},{12,8},{9,1... | collective-permute-start | bytes 3145736 | tf_op jit(solution)/shard_map/ppermute | solution.py:712
  69.3 11.1 %collective-permute-start.8 = (f32[16,256]{1,0:T(8,128)S(1)}, f32[16,256]{1,0:T(8,128)S(1)}, u32[]{:S(2)}, u32[]{:S(2)}) collective-permute-start(f32[16,256]{1,0:T(8,128)S(1)} %get-tuple-element.127), channel_id=1, source_target_pairs={{0,1},{1,0},{2,3},{3,2},{4,5},{5,4},{6,7},{7,6},{8,9},{9,8},{10,11... | collective-permute-start | bytes 49160 | tf_op jit(solution)/shard_map/ppermute | solution.py:712
  70.6 10.4 %collective-permute-start.7 = (f32[16,256]{1,0:T(8,128)S(1)}, f32[16,256]{1,0:T(8,128)S(1)}, u32[]{:S(2)}, u32[]{:S(2)}) collective-permute-start(f32[16,256]{1,0:T(8,128)S(1)} %collective-permute-done.6), channel_id=1, source_target_pairs={{0,1},{1,0},{2,3},{3,2},{4,5},{5,4},{6,7},{7,6},{8,9},{9,8},{10,11... | collective-permute-start | bytes 49160 | tf_op jit(solution)/shard_map/ppermute | solution.py:712
  77.8 98.3 %collective-permute-start.13 = (bf16[8,4,128,256]{3,2,1,0:T(8,128)(2,1)S(1)}, bf16[8,4,128,256]{3,2,1,0:T(8,128)(2,1)}, u32[]{:S(2)}, u32[]{:S(2)}) collective-permute-start(bf16[8,4,128,256]{3,2,1,0:T(8,128)(2,1)S(1)} %constant_dynamic-update-slice_fusion.wa), channel_id=1, source_target_pairs={{0,2},{2,0},{1,3},{3,1},{4,6},{6,4},{5,7},{7,5},{8,10},{10,8},{9,1... | collective-permute-start | bytes 6291464 | tf_op jit(solution)/shard_map/ppermute | solution.py:712
  80.4 57.3 %collective-permute-start = (bf16[1024,256]{1,0:T(8,128)(2,1)}, bf16[1024,256]{1,0:T(8,128)(2,1)}, u32[]{:S(2)}, u32[]{:S(2)}) collective-permute-start(bf16[1024,256]{1,0:T(8,128)(2,1)} %get-tuple-element.103), channel_id=1, source_target_pairs={{0,2},{2,0},{1,3},{3,1},{4,6},{6,4},{5,7},{7,5},{8,10},{10,8},{9,1... | collective-permute-start | bytes 1572872 | tf_op jit(solution)/shard_map/ppermute | solution.py:712
  81.0 65.5 %collective-permute-start.15 = (bf16[1024,256]{1,0:T(8,128)(2,1)}, bf16[1024,256]{1,0:T(8,128)(2,1)}, u32[]{:S(2)}, u32[]{:S(2)}) collective-permute-start(bf16[1024,256]{1,0:T(8,128)(2,1)} %get-tuple-element.101), channel_id=1, source_target_pairs={{0,2},{2,0},{1,3},{3,1},{4,6},{6,4},{5,7},{7,5},{8,10},{10,8},{9,1... | collective-permute-start | bytes 1572872 | tf_op jit(solution)/shard_map/ppermute | solution.py:712
  82.5 65.3 %collective-permute-start.2 = (bf16[1024,256]{1,0:T(8,128)(2,1)S(1)}, bf16[1024,256]{1,0:T(8,128)(2,1)}, u32[]{:S(2)}, u32[]{:S(2)}) collective-permute-start(bf16[1024,256]{1,0:T(8,128)(2,1)S(1)} %get-tuple-element.102), channel_id=1, source_target_pairs={{0,1},{1,0},{2,3},{3,2},{4,5},{5,4},{6,7},{7,6},{8,9},{9,8},{10,11... | collective-permute-start | bytes 1572872 | tf_op jit(solution)/shard_map/ppermute | solution.py:712
  83.3 11.1 %collective-permute-start.18 = (bf16[1,4,128,256]{3,2,1,0:T(8,128)(2,1)}, bf16[1,4,128,256]{3,2,1,0:T(8,128)(2,1)}, u32[]{:S(2)}, u32[]{:S(2)}) collective-permute-start(bf16[1,4,128,256]{3,2,1,0:T(8,128)(2,1)} %get-tuple-element.109), channel_id=1, source_target_pairs={{0,8},{8,0},{16,24},{24,16},{1,9},{9,1},{17,25},{25,17},{2,10},{10... | collective-permute-start | bytes 786440 | tf_op jit(solution)/shard_map/ppermute | solution.py:776
  94.4 60.7 %collective-permute-start.17 = (bf16[1024,256]{1,0:T(8,128)(2,1)}, bf16[1024,256]{1,0:T(8,128)(2,1)S(1)}, u32[]{:S(2)}, u32[]{:S(2)}) collective-permute-start(bf16[1024,256]{1,0:T(8,128)(2,1)} %get-tuple-element.100), channel_id=1, source_target_pairs={{0,1},{1,0},{2,3},{3,2},{4,5},{5,4},{6,7},{7,6},{8,9},{9,8},{10,11... | collective-permute-start | bytes 1572872 | tf_op jit(solution)/shard_map/ppermute | solution.py:712
  137.7 17.3 %collective-permute-start.1 = (bf16[1024,256]{1,0:T(8,128)(2,1)}, bf16[1024,256]{1,0:T(8,128)(2,1)S(1)}, u32[]{:S(2)}, u32[]{:S(2)}) collective-permute-start(bf16[1024,256]{1,0:T(8,128)(2,1)} %collective-permute-done), channel_id=1, source_target_pairs={{0,1},{1,0},{2,3},{3,2},{4,5},{5,4},{6,7},{7,6},{8,9},{9,8},{10,11... | collective-permute-start | bytes 1572872 | tf_op jit(solution)/shard_map/ppermute | solution.py:712
  146.5 8.5 %collective-permute-start.16 = (bf16[1024,256]{1,0:T(8,128)(2,1)}, bf16[1024,256]{1,0:T(8,128)(2,1)S(1)}, u32[]{:S(2)}, u32[]{:S(2)}) collective-permute-start(bf16[1024,256]{1,0:T(8,128)(2,1)} %collective-permute-done.15), channel_id=1, source_target_pairs={{0,1},{1,0},{2,3},{3,2},{4,5},{5,4},{6,7},{7,6},{8,9},{9,8},{10,11... | collective-permute-start | bytes 1572872 | tf_op jit(solution)/shard_map/ppermute | solution.py:712
  147.9 25.6 %collective-permute-start.21 = (bf16[4,4,128,256]{3,2,1,0:T(8,128)(2,1)S(1)}, bf16[4,4,128,256]{3,2,1,0:T(8,128)(2,1)S(1)}, u32[]{:S(2)}, u32[]{:S(2)}) collective-permute-start(bf16[4,4,128,256]{3,2,1,0:T(8,128)(2,1)S(1)} %pad_maximum_fusion.5), channel_id=1, source_target_pairs={{0,4},{4,0},{1,5},{5,1},{2,6},{6,2},{3,7},{7,3},{8,12},{12,8},{9,1... | collective-permute-start | bytes 3145736 | tf_op jit(solution)/shard_map/ppermute | solution.py:712
  174.6 47.6 %collective-permute-start.22 = (bf16[8,4,128,256]{3,2,1,0:T(8,128)(2,1)}, bf16[8,4,128,256]{3,2,1,0:T(8,128)(2,1)}, u32[]{:S(2)}, u32[]{:S(2)}) collective-permute-start(bf16[8,4,128,256]{3,2,1,0:T(8,128)(2,1)} %constant_dynamic-update-slice_fusion.5.wa), channel_id=1, source_target_pairs={{0,2},{2,0},{1,3},{3,1},{4,6},{6,4},{5,7},{7,5},{8,10},{10,8},{9,1... | collective-permute-start | bytes 6291464 | tf_op jit(solution)/shard_map/ppermute | solution.py:712
  212.4 9.8 %collective-permute-start.14 = (bf16[1024,1024]{1,0:T(8,128)(2,1)}, bf16[1024,1024]{1,0:T(8,128)(2,1)S(1)}, u32[]{:S(2)}, u32[]{:S(2)}) collective-permute-start(bf16[1024,1024]{1,0:T(8,128)(2,1)} %get-tuple-element.46.pa_ref), channel_id=1, source_target_pairs={{0,1},{1,0},{2,3},{3,2},{4,5},{5,4},{6,7},{7,6},{8,9},{9,8},{10,11... | collective-permute-start | bytes 6291464 | tf_op jit(solution)/shard_map/ppermute | solution.py:712
  257.7 46.6 %collective-permute-start.38 = (bf16[8,4,128,256]{3,2,1,0:T(8,128)(2,1)}, bf16[8,4,128,256]{3,2,1,0:T(8,128)(2,1)S(1)}, u32[]{:S(2)}, u32[]{:S(2)}) collective-permute-start(bf16[8,4,128,256]{3,2,1,0:T(8,128)(2,1)} %get-tuple-element.67), channel_id=1, source_target_pairs={{0,2},{2,0},{1,3},{3,1},{4,6},{6,4},{5,7},{7,5},{8,10},{10,8},{9,1... | collective-permute-start | bytes 6291464 | tf_op jit(solution)/shard_map/ppermute | solution.py:712
  259.2 51.0 %collective-permute-start.24 = (bf16[1024,1024]{1,0:T(8,128)(2,1)}, bf16[1024,1024]{1,0:T(8,128)(2,1)S(1)}, u32[]{:S(2)}, u32[]{:S(2)}) collective-permute-start(bf16[1024,1024]{1,0:T(8,128)(2,1)} %get-tuple-element.49.ga_ref), channel_id=1, source_target_pairs={{0,1},{1,0},{2,3},{3,2},{4,5},{5,4},{6,7},{7,6},{8,9},{9,8},{10,11... | collective-permute-start | bytes 6291464 | tf_op jit(solution)/shard_map/ppermute | solution.py:712
  259.2 162.8 %collective-permute-start.23 = (bf16[1024,1024]{1,0:T(8,128)(2,1)}, bf16[1024,1024]{1,0:T(8,128)(2,1)}, u32[]{:S(2)}, u32[]{:S(2)}) collective-permute-start(bf16[1024,1024]{1,0:T(8,128)(2,1)} %get-tuple-element.47.fa_ref), channel_id=1, source_target_pairs={{0,1},{1,0},{2,3},{3,2},{4,5},{5,4},{6,7},{7,6},{8,9},{9,8},{10,11... | collective-permute-start | bytes 6291464 | tf_op jit(solution)/shard_map/ppermute | solution.py:712
  308.7 67.3 %collective-permute-start.39 = (bf16[4,4,128,256]{3,2,1,0:T(8,128)(2,1)S(1)}, bf16[4,4,128,256]{3,2,1,0:T(8,128)(2,1)}, u32[]{:S(2)}, u32[]{:S(2)}) collective-permute-start(bf16[4,4,128,256]{3,2,1,0:T(8,128)(2,1)S(1)} %slice.236), channel_id=1, source_target_pairs={{0,4},{4,0},{1,5},{5,1},{2,6},{6,2},{3,7},{7,3},{8,12},{12,8},{9,1... | collective-permute-start | bytes 3145736 | tf_op jit(solution)/shard_map/ppermute | solution.py:712
  326.5 30.5 %collective-permute-start.33 = (bf16[8,1,128,256]{3,2,1,0:T(8,128)(2,1)}, bf16[8,1,128,256]{3,2,1,0:T(8,128)(2,1)S(1)}, u32[]{:S(2)}, u32[]{:S(2)}) collective-permute-start(bf16[8,1,128,256]{3,2,1,0:T(8,128)(2,1)} %get-tuple-element.65), channel_id=1, source_target_pairs={{0,2},{2,0},{1,3},{3,1},{4,6},{6,4},{5,7},{7,5},{8,10},{10,8},{9,1... | collective-permute-start | bytes 1572872 | tf_op jit(solution)/shard_map/ppermute | solution.py:712
  357.2 18.0 %collective-permute-start.34 = (bf16[4,1,128,256]{3,2,1,0:T(8,128)(2,1)S(1)}, bf16[4,1,128,256]{3,2,1,0:T(8,128)(2,1)S(1)}, u32[]{:S(2)}, u32[]{:S(2)}) collective-permute-start(bf16[4,1,128,256]{3,2,1,0:T(8,128)(2,1)S(1)} %slice.238), channel_id=1, source_target_pairs={{0,4},{4,0},{1,5},{5,1},{2,6},{6,2},{3,7},{7,3},{8,12},{12,8},{9,1... | collective-permute-start | bytes 786440 | tf_op jit(solution)/shard_map/ppermute | solution.py:712
  375.1 46.9 %collective-permute-start.25 = (bf16[1024,1024]{1,0:T(8,128)(2,1)}, bf16[1024,1024]{1,0:T(8,128)(2,1)}, u32[]{:S(2)}, u32[]{:S(2)}) collective-permute-start(bf16[1024,1024]{1,0:T(8,128)(2,1)} %get-tuple-element.56.ga_ref), channel_id=1, source_target_pairs={{0,1},{1,0},{2,3},{3,2},{4,5},{5,4},{6,7},{7,6},{8,9},{9,8},{10,11... | collective-permute-start | bytes 6291464 | tf_op jit(solution)/shard_map/ppermute | solution.py:712
  379.2 19.9 %collective-permute-start.40 = (bf16[4,128,256]{2,1,0:T(8,128)(2,1)}, bf16[4,128,256]{2,1,0:T(8,128)(2,1)S(1)}, u32[]{:S(2)}, u32[]{:S(2)}) collective-permute-start(bf16[4,128,256]{2,1,0:T(8,128)(2,1)} %get-tuple-element.97), channel_id=1, source_target_pairs={{0,8},{8,0},{16,24},{24,16},{1,9},{9,1},{17,25},{25,17},{2,10},{10... | collective-permute-start | bytes 786440 | tf_op jit(solution)/shard_map/ppermute | solution.py:823
  380.3 9.3 %collective-permute-start.35 = (bf16[1,128,256]{2,1,0:T(8,128)(2,1)S(1)}, bf16[1,128,256]{2,1,0:T(8,128)(2,1)}, u32[]{:S(2)}, u32[]{:S(2)}) collective-permute-start(bf16[1,128,256]{2,1,0:T(8,128)(2,1)S(1)} %get-tuple-element.113), channel_id=1, source_target_pairs={{0,8},{8,0},{16,24},{24,16},{1,9},{9,1},{17,25},{25,17},{2,10},{10... | collective-permute-start | bytes 196616 | tf_op jit(solution)/shard_map/ppermute | solution.py:823
  381.9 9.6 %collective-permute-start.37 = (bf16[1,128,256]{2,1,0:T(8,128)(2,1)}, bf16[1,128,256]{2,1,0:T(8,128)(2,1)}, u32[]{:S(2)}, u32[]{:S(2)}) collective-permute-start(bf16[1,128,256]{2,1,0:T(8,128)(2,1)} %get-tuple-element.114), channel_id=1, source_target_pairs={{0,24},{8,16},{16,8},{24,0},{1,25},{9,17},{17,9},{25,1},{2,26},{10... | collective-permute-start | bytes 196616 | tf_op jit(solution)/shard_map/ppermute | solution.py:823
  389.6 48.1 %collective-permute-start.28 = (bf16[8,3,128,256]{3,2,1,0:T(8,128)(2,1)}, bf16[8,3,128,256]{3,2,1,0:T(8,128)(2,1)}, u32[]{:S(2)}, u32[]{:S(2)}) collective-permute-start(bf16[8,3,128,256]{3,2,1,0:T(8,128)(2,1)} %get-tuple-element.63), channel_id=1, source_target_pairs={{0,2},{2,0},{1,3},{3,1},{4,6},{6,4},{5,7},{7,5},{8,10},{10,8},{9,1... | collective-permute-start | bytes 4718600 | tf_op jit(solution)/shard_map/ppermute | solution.py:712
  391.5 5.7 %collective-permute-start.36 = (bf16[1,128,256]{2,1,0:T(8,128)(2,1)}, bf16[1,128,256]{2,1,0:T(8,128)(2,1)S(1)}, u32[]{:S(2)}, u32[]{:S(2)}) collective-permute-start(bf16[1,128,256]{2,1,0:T(8,128)(2,1)} %get-tuple-element.115), channel_id=1, source_target_pairs={{0,16},{8,24},{16,0},{24,8},{1,17},{9,25},{17,1},{25,9},{2,18},{10... | collective-permute-start | bytes 196616 | tf_op jit(solution)/shard_map/ppermute | solution.py:823
  397.2 11.3 %collective-permute-start.42 = (bf16[4,128,256]{2,1,0:T(8,128)(2,1)}, bf16[4,128,256]{2,1,0:T(8,128)(2,1)S(1)}, u32[]{:S(2)}, u32[]{:S(2)}) collective-permute-start(bf16[4,128,256]{2,1,0:T(8,128)(2,1)} %get-tuple-element.98), channel_id=1, source_target_pairs={{0,24},{8,16},{16,8},{24,0},{1,25},{9,17},{17,9},{25,1},{2,26},{10... | collective-permute-start | bytes 786440 | tf_op jit(solution)/shard_map/ppermute | solution.py:823
  399.1 21.8 %collective-permute-start.41 = (bf16[4,128,256]{2,1,0:T(8,128)(2,1)S(1)}, bf16[4,128,256]{2,1,0:T(8,128)(2,1)S(1)}, u32[]{:S(2)}, u32[]{:S(2)}) collective-permute-start(bf16[4,128,256]{2,1,0:T(8,128)(2,1)S(1)} %get-tuple-element.99), channel_id=1, source_target_pairs={{0,16},{8,24},{16,0},{24,8},{1,17},{9,25},{17,1},{25,9},{2,18},{10... | collective-permute-start | bytes 786440 | tf_op jit(solution)/shard_map/ppermute | solution.py:823
  437.6 5.7 %collective-permute-start.43 = (f32[16,256]{1,0:T(8,128)S(1)}, f32[16,256]{1,0:T(8,128)S(1)}, u32[]{:S(2)}, u32[]{:S(2)}) collective-permute-start(f32[16,256]{1,0:T(8,128)S(1)} %get-tuple-element.122), channel_id=1, source_target_pairs={{0,2},{2,0},{1,3},{3,1},{4,6},{6,4},{5,7},{7,5},{8,10},{10,8},{9,1... | collective-permute-start | bytes 49160 | tf_op jit(solution)/shard_map/ppermute | solution.py:712
  439.8 46.7 %collective-permute-start.29 = (bf16[4,3,128,256]{3,2,1,0:T(8,128)(2,1)S(1)}, bf16[4,3,128,256]{3,2,1,0:T(8,128)(2,1)S(1)}, u32[]{:S(2)}, u32[]{:S(2)}) collective-permute-start(bf16[4,3,128,256]{3,2,1,0:T(8,128)(2,1)S(1)} %slice.237), channel_id=1, source_target_pairs={{0,4},{4,0},{1,5},{5,1},{2,6},{6,2},{3,7},{7,3},{8,12},{12,8},{9,1... | collective-permute-start | bytes 2359304 | tf_op jit(solution)/shard_map/ppermute | solution.py:712
  441.3 78.6 %collective-permute-start.26 = (bf16[1024,256]{1,0:T(8,128)(2,1)S(1)}, bf16[1024,256]{1,0:T(8,128)(2,1)S(1)}, u32[]{:S(2)}, u32[]{:S(2)}) collective-permute-start(bf16[1024,256]{1,0:T(8,128)(2,1)S(1)} %copy-done.34), channel_id=1, source_target_pairs={{0,2},{2,0},{1,3},{3,1},{4,6},{6,4},{5,7},{7,5},{8,10},{10,8},{9,1... | collective-permute-start | bytes 1572872 | tf_op jit(solution)/shard_map/ppermute | solution.py:712
  442.8 75.2 %collective-permute-start.27 = (bf16[1024,256]{1,0:T(8,128)(2,1)S(1)}, bf16[1024,256]{1,0:T(8,128)(2,1)S(1)}, u32[]{:S(2)}, u32[]{:S(2)}) collective-permute-start(bf16[1024,256]{1,0:T(8,128)(2,1)S(1)} %copy-done.35), channel_id=1, source_target_pairs={{0,2},{2,0},{1,3},{3,1},{4,6},{6,4},{5,7},{7,5},{8,10},{10,8},{9,1... | collective-permute-start | bytes 1572872 | tf_op jit(solution)/shard_map/ppermute | solution.py:712
  443.3 42.2 %collective-permute-start.50 = (f32[2,16,256]{2,1,0:T(8,128)S(1)}, f32[2,16,256]{2,1,0:T(8,128)S(1)}, u32[]{:S(2)}, u32[]{:S(2)}) collective-permute-start(f32[2,16,256]{2,1,0:T(8,128)S(1)} %pad_maximum_fusion.8), channel_id=1, source_target_pairs={{0,28},{4,24},{8,20},{12,16},{16,12},{20,8},{24,4},{28,0},{1,29},{... | collective-permute-start | bytes 98312 | tf_op jit(solution)/shard_map/ppermute | solution.py:881
  445.6 14.1 %collective-permute-start.44 = (f32[2,16,256]{2,1,0:T(8,128)S(1)}, f32[2,16,256]{2,1,0:T(8,128)S(1)}, u32[]{:S(2)}, u32[]{:S(2)}) collective-permute-start(f32[2,16,256]{2,1,0:T(8,128)S(1)} %pad_maximum_fusion.8), channel_id=1, source_target_pairs={{0,4},{4,0},{8,12},{12,8},{16,20},{20,16},{24,28},{28,24},{1,5},{5... | collective-permute-start | bytes 98312 | tf_op jit(solution)/shard_map/ppermute | solution.py:881
  463.8 5.0 collective-permute-start.46
  473.6 5.7 %collective-permute-start.48 = (f32[2,16,256]{2,1,0:T(8,128)S(1)}, f32[2,16,256]{2,1,0:T(8,128)S(1)}, u32[]{:S(2)}, u32[]{:S(2)}) collective-permute-start(f32[2,16,256]{2,1,0:T(8,128)S(1)} %pad_maximum_fusion.8), channel_id=1, source_target_pairs={{0,20},{4,16},{8,28},{12,24},{16,4},{20,0},{24,12},{28,8},{1,21},{... | collective-permute-start | bytes 98312 | tf_op jit(solution)/shard_map/ppermute | solution.py:881
  479.4 6.2 %collective-permute-start.49 = (f32[2,16,256]{2,1,0:T(8,128)S(1)}, f32[2,16,256]{2,1,0:T(8,128)S(1)}, u32[]{:S(2)}, u32[]{:S(2)}) collective-permute-start(f32[2,16,256]{2,1,0:T(8,128)S(1)} %pad_maximum_fusion.8), channel_id=1, source_target_pairs={{0,24},{4,28},{8,16},{12,20},{16,8},{20,12},{24,0},{28,4},{1,25},{... | collective-permute-start | bytes 98312 | tf_op jit(solution)/shard_map/ppermute | solution.py:881
  486.8 9.6 %collective-permute-start.30 = (bf16[3,128,256]{2,1,0:T(8,128)(2,1)S(1)}, bf16[3,128,256]{2,1,0:T(8,128)(2,1)S(1)}, u32[]{:S(2)}, u32[]{:S(2)}) collective-permute-start(bf16[3,128,256]{2,1,0:T(8,128)(2,1)S(1)} %get-tuple-element.104), channel_id=1, source_target_pairs={{0,8},{8,0},{16,24},{24,16},{1,9},{9,1},{17,25},{25,17},{2,10},{10... | collective-permute-start | bytes 589832 | tf_op jit(solution)/shard_map/ppermute | solution.py:823
  486.9 9.5 %collective-permute-start.32 = (bf16[3,128,256]{2,1,0:T(8,128)(2,1)S(1)}, bf16[3,128,256]{2,1,0:T(8,128)(2,1)S(1)}, u32[]{:S(2)}, u32[]{:S(2)}) collective-permute-start(bf16[3,128,256]{2,1,0:T(8,128)(2,1)S(1)} %get-tuple-element.105), channel_id=1, source_target_pairs={{0,24},{8,16},{16,8},{24,0},{1,25},{9,17},{17,9},{25,1},{2,26},{10... | collective-permute-start | bytes 589832 | tf_op jit(solution)/shard_map/ppermute | solution.py:823
  488.7 12.0 %collective-permute-start.31 = (bf16[3,128,256]{2,1,0:T(8,128)(2,1)S(1)}, bf16[3,128,256]{2,1,0:T(8,128)(2,1)S(1)}, u32[]{:S(2)}, u32[]{:S(2)}) collective-permute-start(bf16[3,128,256]{2,1,0:T(8,128)(2,1)S(1)} %get-tuple-element.106), channel_id=1, source_target_pairs={{0,16},{8,24},{16,0},{24,8},{1,17},{9,25},{17,1},{25,9},{2,18},{10... | collective-permute-start | bytes 589832 | tf_op jit(solution)/shard_map/ppermute | solution.py:823
  (41 other events, 1039.8 us)

commit v2 on v1

--- a/solution.py
+++ b/solution.py
@@ -67,19 +67,16 @@
     return pl.CostEstimate(flops=int(flops), bytes_accessed=int(nbytes), transcendentals=int(trans))
 
 
-def fetch_weights(meta, rowtab, arrays, dest, sem, mats, base, start):
-    n_dp, _, rows, _ = arrays[0].shape
-    y = meta[0]
-    for other in range(2):
-        col = y if other == 0 else 1 - y
-        for mat in range(mats):
-
-            def step(slot, carry, other=other, mat=mat, col=col):
-                first = pl.multiple_of(rowtab[base + mat, slot] * rows, rows)
+def fetch_weights(rowcol, sources, dest, sem, start):
+    for at, (mat, arrays, index) in enumerate(sources):
+        n_dp, _, rows, _ = arrays[0].shape
+        for side in range(2):
+
+            def step(slot, carry, at=at, mat=mat, index=index, side=side, array=arrays[side], n_dp=n_dp, rows=rows):
+                code = rowcol[mat, side * n_dp + slot]
+                first = pl.multiple_of((code // 2) * rows, rows)
                 copy = pltpu.make_async_copy(
-                    arrays[other].at[slot, base % 4 + mat],
-                    dest.at[mat, col, pl.ds(first, rows), :],
-                    sem,
+                    array.at[slot, index], dest.at[at, code % 2, pl.ds(first, rows), :], sem
                 )
                 if start:
                     copy.start()
@@ -90,19 +87,24 @@
             lax.fori_loop(0, n_dp, step, 0, unroll=n_dp <= 8)
 
 
-def store_grads(slottab, staged, target, sem, mat, local, start):
-    n_dp, _, rows, _ = target.shape
+def store_grads(slottab, mat, col, staged, targets, index, sem, start):
+    n_dp, _, rows, _ = targets[0].shape
 
     def step(block, carry):
-        copy = pltpu.make_async_copy(
-            staged.at[pl.ds(pl.multiple_of(block * rows, rows), rows), :],
-            target.at[slottab[mat, block], local],
-            sem,
-        )
-        if start:
-            copy.start()
-        else:
-            copy.wait()
+        source = staged.at[pl.ds(pl.multiple_of(block * rows, rows), rows), :]
+        if not start:
+            pltpu.make_async_copy(source, targets[0].at[0, index], sem).wait()
+            return carry
+        code = slottab[mat, block * 2 + col]
+
+        @pl.when(code < n_dp)
+        def _():
+            pltpu.make_async_copy(source, targets[0].at[code, index], sem).start()
+
+        @pl.when(code >= n_dp)
+        def _():
+            pltpu.make_async_copy(source, targets[1].at[code - n_dp, index], sem).start()
+
         return carry
 
     lax.fori_loop(0, n_dp, step, 0, unroll=n_dp <= 8)
@@ -118,13 +120,13 @@
 
 def prep_kernel(w_ref, cond_ref, wp_ref, mod_ref):
     for k in range(8):
-        wp_ref[k] = w_ref[:, k, :].astype(BF)
+        wp_ref[k] = w_ref[k].astype(BF)
     for c in range(6):
-        mod_ref[c] = nn_dot(cond_ref[c], w_ref[:, 8 + c, :].astype(BF))
+        mod_ref[c] = nn_dot(cond_ref[c], w_ref[8 + c].astype(BF))
 
 
 def prep(weights, condk):
-    rows = weights.shape[0]
+    rows = weights.shape[1]
     return pl.pallas_call(
         prep_kernel,
         out_shape=(
@@ -152,10 +154,16 @@
     return x * ct + turn if sign > 0 else x * ct - turn
 
 
-def qkv_kernel(meta, rowtab, x_ref, vec_ref, ct_ref, s1_ref, s2_ref, wa, wb, h1_ref, q_ref, k_ref, v_ref, wsc, sem):
+def qkv_sources(a0, a1, b0, b1):
+    return ((0, (a0, a1), 0), (1, (a0, a1), 1), (2, (b0, b1), 0))
+
+
+def qkv_kernel(
+    meta, rowtab, x_ref, vec_ref, ct_ref, s1_ref, s2_ref, a0, a1, b0, b1, h1_ref, q_ref, k_ref, v_ref, wsc, sem
+):
     @pl.when(pl.program_id(0) == 0)
     def _():
-        fetch_weights(meta, rowtab, (wa, wb), wsc, sem, 3, 0, True)
+        fetch_weights(rowtab, qkv_sources(a0, a1, b0, b1), wsc, sem, True)
 
     n1, _ = layer_norm(x_ref[...].astype(F32))
     h1 = (n1 * (1.0 + vec_ref[8:9, :]) + vec_ref[7:8, :]).astype(BF)
@@ -163,7 +171,7 @@
 
     @pl.when(pl.program_id(0) == 0)
     def _():
-        fetch_weights(meta, rowtab, (wa, wb), wsc, sem, 3, 0, False)
+        fetch_weights(rowtab, qkv_sources(a0, a1, b0, b1), wsc, sem, False)
 
     c = meta[1]
     ct, s1, s2 = ct_ref[...], s1_ref[...], s2_ref[...]
@@ -178,7 +186,7 @@
             out[:, col * CW : (col + 1) * CW] = acc.astype(BF)
 
 
-def qkv(meta, rowtab, x, vec, tables, wa, wb):
+def qkv(meta, rowtab, x, vec, tables, w_attn):
     half = 2 * CW
     return pl.pallas_call(
         qkv_kernel,
@@ -186,14 +194,14 @@
         grid_spec=pltpu.PrefetchScalarGridSpec(
             num_scalar_prefetch=2,
             grid=(NT,),
-            in_specs=[rows_spec(D), whole(vec.shape)] + [rows_spec(128)] * 3 + [ANY, ANY],
+            in_specs=[rows_spec(D), whole(vec.shape)] + [rows_spec(128)] * 3 + [ANY] * 4,
             out_specs=(rows_spec(D),) + (rows_spec(half),) * 3,
             scratch_shapes=[pltpu.VMEM((3, 2, D, CW), BF), pltpu.SemaphoreType.DMA(())],
         ),
         compiler_params=params(),
         cost_estimate=cost(2 * LEN * D * 3 * half, 12e6),
         name="qkv",
-    )(meta, rowtab, x, vec, *tables, wa, wb)
+    )(meta, rowtab, x, vec, *tables, *w_attn)
 
 
 def lane_iota(rows):
@@ -209,7 +217,7 @@
 def attend_kernel(meta, rowtab, q_ref, k_ref, v_ref, kaug_ref, wa, wb, o_ref, qaug_ref, pa_ref, wsc, osc, sem):
     @pl.when(pl.program_id(0) == 0)
     def _():
-        fetch_weights(meta, rowtab, (wa, wb), wsc, sem, 1, 3, True)
+        fetch_weights(rowtab, ((3, (wa, wb), 1),), wsc, sem, True)
 
     lane = lane_iota(TB)
     first = lane < HEAD_DIM
@@ -244,7 +252,7 @@
 
     @pl.when(pl.program_id(0) == 0)
     def _():
-        fetch_weights(meta, rowtab, (wa, wb), wsc, sem, 1, 3, False)
+        fetch_weights(rowtab, ((3, (wa, wb), 1),), wsc, sem, False)
 
     pa = nt_dot(osc[:, :CW], wsc[0, 0]) + nt_dot(osc[:, CW:], wsc[0, 1])
     pa_ref[...] = pa.astype(BF)
@@ -295,19 +303,19 @@
 
 
 def feed_kernel(
-    meta, rowtab, slottab, x_ref, pa_ref, pb_ref, g_ref, vec_ref, wa, wb,
-    pf_ref, pg_ref, gb_ref, keep_ref, send_ref,
+    meta, rowtab, slottab, x_ref, pa_ref, pb_ref, g_ref, vec_ref, c0, c1, d0, d1,
+    pfk_ref, pfs_ref, pg_ref, gb_ref, gck_ref, gcs_ref, gdk_ref, gds_ref,
     wsc, h2, gf, h2t, gft, facc, gacc, zsc, ghsc, stage, sem, gsem,
 ):
-    y, c, length = meta[0], meta[1], meta[2]
+    c, length = meta[1], meta[2]
     step = pl.program_id(0)
-    other = jnp.where(step < 2, 1, 0)
     half = step % 2
-    col = jnp.bitwise_xor(other, y)
+    col = step // 2
+    sources = ((4, (c0, c1), 0), (5, (c0, c1), 1), (6, (d0, d1), 0), (7, (d0, d1), 1))
 
     @pl.when(step == 0)
     def _():
-        fetch_weights(meta, rowtab, (wa, wb), wsc, sem, 4, 4, True)
+        fetch_weights(rowtab, sources, wsc, sem, True)
         gb_ref[...] = jnp.zeros_like(gb_ref)
 
         def rows(i, carry):
@@ -324,7 +332,7 @@
             return carry
 
         lax.fori_loop(0, NT, rows, 0)
-        fetch_weights(meta, rowtab, (wa, wb), wsc, sem, 4, 4, False)
+        fetch_weights(rowtab, sources, wsc, sem, False)
 
     off = pl.multiple_of((col * 2 + c) * CW, CW)
     w_in = wsc.at[half, col]
@@ -357,51 +365,41 @@
     total = lax.fori_loop(0, NT, rows, jnp.zeros((1, CW), F32))
     gb_ref[pl.ds(half, 1), pl.ds(off, CW)] = total
 
-    def copies(which, start):
-        local = half + 2 * which
-
-        @pl.when(other == 0)
-        def _():
-            store_grads(slottab, stage.at[which], keep_ref, gsem, 4 + local, local, start)
-
-        @pl.when(other == 1)
-        def _():
-            store_grads(slottab, stage.at[which], send_ref, gsem, 4 + local, local, start)
+    targets = ((gck_ref, gcs_ref), (gdk_ref, gds_ref))
 
     @pl.when(step > 0)
     def _():
         for which in range(2):
-            store_grads(slottab, stage.at[which], keep_ref, gsem, 4, 0, False)
+            store_grads(slottab, 4, 0, stage.at[which], targets[0], 0, gsem, False)
 
     for which, (lhs, rhs) in enumerate(((h2t, ghsc), (gft, zsc))):
         for r in range(NT):
             stage[which, r * TB : (r + 1) * TB, :] = nn_dot(lhs[r * TB : (r + 1) * TB, :], rhs[...]).astype(BF)
-        copies(which, True)
+        store_grads(slottab, 4 + 2 * which + half, col, stage.at[which], targets[which], half, gsem, True)
 
     @pl.when(step == 3)
     def _():
         for which in range(2):
-            store_grads(slottab, stage.at[which], keep_ref, gsem, 4, 0, False)
-        pf_ref[...] = facc[...].astype(BF)
+            store_grads(slottab, 4, 0, stage.at[which], targets[0], 0, gsem, False)
+        for block in range(2):
+            mine = pl.ds(pl.multiple_of((block * 2 + c) * CW, CW), CW)
+            theirs = pl.ds(pl.multiple_of((block * 2 + 1 - c) * CW, CW), CW)
+            pfk_ref[:, block * CW : (block + 1) * CW] = facc[:, mine].astype(BF)
+            pfs_ref[:, block * CW : (block + 1) * CW] = facc[:, theirs].astype(BF)
         pg_ref[...] = gacc[...].astype(BF)
 
 
-def feed(meta, rowtab, slottab, x, pa, pb, g, vec, wa, wb):
-    grads = jax.ShapeDtypeStruct(wa.shape[:1] + (4,) + wa.shape[2:], BF)
+def feed(meta, rowtab, slottab, x, pa, pb, g, vec, w_feed):
+    grads = jax.ShapeDtypeStruct(w_feed[0].shape, BF)
+    part = jax.ShapeDtypeStruct((LEN, 2 * CW), BF)
     return pl.pallas_call(
         feed_kernel,
-        out_shape=(
-            jax.ShapeDtypeStruct((LEN, D), BF),
-            jax.ShapeDtypeStruct((LEN, D), BF),
-            jax.ShapeDtypeStruct((8, D), F32),
-            grads,
-            grads,
-        ),
+        out_shape=(part, part, jax.ShapeDtypeStruct((LEN, D), BF), jax.ShapeDtypeStruct((8, D), F32)) + (grads,) * 4,
         grid_spec=pltpu.PrefetchScalarGridSpec(
             num_scalar_prefetch=3,
             grid=(4,),
-            in_specs=[whole((LEN, D))] * 4 + [whole(vec.shape), ANY, ANY],
-            out_specs=(whole((LEN, D)), whole((LEN, D)), whole((8, D)), ANY, ANY),
+            in_specs=[whole((LEN, D))] * 4 + [whole(vec.shape)] + [ANY] * 4,
+            out_specs=(whole((LEN, 2 * CW)), whole((LEN, 2 * CW)), whole((LEN, D)), whole((8, D))) + (ANY,) * 4,
             scratch_shapes=[
                 pltpu.VMEM((4, 2, D, CW), BF),
                 pltpu.VMEM((LEN, D), BF),
@@ -420,19 +418,19 @@
         compiler_params=params(),
         cost_estimate=cost(2 * LEN * D * D * 6, 24e6, 1e6),
         name="feed",
-    )(meta, rowtab, slottab, x, pa, pb, g, vec, wa, wb)
+    )(meta, rowtab, slottab, x, pa, pb, g, vec, *w_feed)
 
 
 def proj_back_kernel(
     meta, rowtab, slottab, x_ref, pa_ref, pb_ref, g_ref, ga_ref, gb_ref, o_ref, vec_ref, wa, wb,
     gx_ref, go_ref, sums_ref, keep_ref, send_ref, wsc, wacc, stage, sem, gsem,
 ):
-    y, length = meta[0], meta[2]
+    length = meta[2]
     step = pl.program_id(0)
 
     @pl.when(step == 0)
     def _():
-        fetch_weights(meta, rowtab, (wa, wb), wsc, sem, 1, 3, True)
+        fetch_weights(rowtab, ((3, (wa, wb), 1),), wsc, sem, True)
         sums_ref[...] = jnp.zeros_like(sums_ref)
 
     a, x1 = middle_rows(x_ref[...], pa_ref[...], pb_ref[...], vec_ref, valid_rows(step * TB, TB, length))
@@ -451,7 +449,7 @@
 
     @pl.when(step == 0)
     def _():
-        fetch_weights(meta, rowtab, (wa, wb), wsc, sem, 1, 3, False)
+        fetch_weights(rowtab, ((3, (wa, wb), 1),), wsc, sem, False)
 
     go_ref[:, :CW] = nn_dot(gatt, wsc[0, 0]).astype(BF)
     go_ref[:, CW:] = nn_dot(gatt, wsc[0, 1]).astype(BF)
@@ -469,10 +467,9 @@
     def _():
         for col in range(2):
             stage[col] = wacc[:, col * CW : (col + 1) * CW].astype(BF)
-        store_grads(slottab, stage.at[y], keep_ref, gsem, 3, 0, True)
-        store_grads(slottab, stage.at[1 - y], send_ref, gsem, 3, 0, True)
-        store_grads(slottab, stage.at[y], keep_ref, gsem, 3, 0, False)
-        store_grads(slottab, stage.at[1 - y], send_ref, gsem, 3, 0, False)
+            store_grads(slottab, 3, col, stage.at[col], (keep_ref, send_ref), 0, gsem, True)
+        for col in range(2):
+            store_grads(slottab, 3, col, stage.at[col], (keep_ref, send_ref), 0, gsem, False)
 
 
 def proj_back(meta, rowtab, slottab, x, pa, pb, g, ga, gb, o, vec, wa, wb):
@@ -581,11 +578,10 @@
 
 
 def qkv_back_kernel(
-    meta, rowtab, slottab, h1_ref, gq_ref, gk_ref, gv_ref, wa, wb, pg_ref, keep_ref, send_ref,
-    wsc, h1t, stage, sem, gsem,
+    meta, rowtab, slottab, h1_ref, gq_ref, gk_ref, gv_ref, a0, a1, b0, b1,
+    pg_ref, gak_ref, gas_ref, gbk_ref, gbs_ref, wsc, h1t, stage, sem, gsem,
 ):
-    y = meta[0]
-    fetch_weights(meta, rowtab, (wa, wb), wsc, sem, 3, 0, True)
+    fetch_weights(rowtab, qkv_sources(a0, a1, b0, b1), wsc, sem, True)
 
     def turn(i, carry):
         at = pl.ds(pl.multiple_of(i * TB, TB), TB)
@@ -593,53 +589,54 @@
         return carry
 
     lax.fori_loop(0, NT, turn, 0)
-    for yr in (1, 0):
-        col = jnp.bitwise_xor(y, yr)
-        off = pl.multiple_of(col * CW, CW)
-        target = send_ref if yr == 1 else keep_ref
-        for k, src in enumerate((gq_ref, gk_ref, gv_ref)):
-            rhs = src[:, pl.ds(off, CW)]
-
-            def rows(i, carry, k=k, rhs=rhs, yr=yr):
-                at = pl.ds(pl.multiple_of(i * TB, TB), TB)
-                stage[yr, k, at, :] = nn_dot(h1t[at, :], rhs).astype(BF)
-                return carry
-
-            lax.fori_loop(0, NT, rows, 0)
-            store_grads(slottab, stage.at[yr, k], target, gsem, k, k, True)
-    fetch_weights(meta, rowtab, (wa, wb), wsc, sem, 3, 0, False)
+    targets = ((gak_ref, gas_ref), (gak_ref, gas_ref), (gbk_ref, gbs_ref))
+    sources = (gq_ref, gk_ref, gv_ref)
+    for k in range(3):
+
+        def rows(i, carry, k=k):
+            at = pl.ds(pl.multiple_of(i * TB, TB), TB)
+            part = nn_dot(h1t[at, :], sources[k][...]).astype(BF)
+            stage[k, 0, at, :] = part[:, :CW]
+            stage[k, 1, at, :] = part[:, CW:]
+            return carry
+
+        lax.fori_loop(0, NT, rows, 0)
+        for col in range(2):
+            store_grads(slottab, k, col, stage.at[k, col], targets[k], k % 2, gsem, True)
+    fetch_weights(rowtab, qkv_sources(a0, a1, b0, b1), wsc, sem, False)
 
     def rows(i, carry):
         at = pl.ds(pl.multiple_of(i * TB, TB), TB)
         acc = jnp.zeros((TB, D), F32)
-        for k, src in enumerate((gq_ref, gk_ref, gv_ref)):
+        for k in range(3):
             for col in range(2):
-                acc += nt_dot(src[at, col * CW : (col + 1) * CW], wsc[k, col])
+                acc += nt_dot(sources[k][at, col * CW : (col + 1) * CW], wsc[k, col])
         pg_ref[at, :] = acc.astype(BF)
         return carry
 
     lax.fori_loop(0, NT, rows, 0)
-    for yr in (1, 0):
-        target = send_ref if yr == 1 else keep_ref
-        for k in range(3):
-            store_grads(slottab, stage.at[yr, k], target, gsem, k, k, False)
-
-
-def qkv_back(meta, rowtab, slottab, h1, gq, gk, gv, wa, wb):
-    grads = jax.ShapeDtypeStruct(wa.shape[:1] + (3,) + wa.shape[2:], BF)
+    for k in range(3):
+        for col in range(2):
+            store_grads(slottab, k, col, stage.at[k, col], targets[k], k % 2, gsem, False)
+
+
+def qkv_back(meta, rowtab, slottab, h1, gq, gk, gv, w_attn):
+    n_dp, _, rows, _ = w_attn[0].shape
+    two = jax.ShapeDtypeStruct((n_dp, 2, rows, CW), BF)
+    one = jax.ShapeDtypeStruct((n_dp, 1, rows, CW), BF)
     half = 2 * CW
     return pl.pallas_call(
         qkv_back_kernel,
-        out_shape=(jax.ShapeDtypeStruct((LEN, D), BF), grads, grads),
+        out_shape=(jax.ShapeDtypeStruct((LEN, D), BF), two, two, one, one),
         grid_spec=pltpu.PrefetchScalarGridSpec(
             num_scalar_prefetch=3,
             grid=(1,),
-            in_specs=[whole((LEN, D))] + [whole((LEN, half))] * 3 + [ANY, ANY],
-            out_specs=(whole((LEN, D)), ANY, ANY),
+            in_specs=[whole((LEN, D))] + [whole((LEN, half))] * 3 + [ANY] * 4,
+            out_specs=(whole((LEN, D)),) + (ANY,) * 4,
             scratch_shapes=[
                 pltpu.VMEM((3, 2, D, CW), BF),
                 pltpu.VMEM((D, LEN), BF),
-                pltpu.VMEM((2, 3, D, CW), BF),
+                pltpu.VMEM((3, 2, D, CW), BF),
                 pltpu.SemaphoreType.DMA(()),
                 pltpu.SemaphoreType.DMA(()),
             ],
@@ -647,13 +644,10 @@
         compiler_params=params(),
         cost_estimate=cost(2 * LEN * D * half * 6, 16e6),
         name="qkv_back",
-    )(meta, rowtab, slottab, h1, gq, gk, gv, wa, wb)
-
-
-def final_kernel(
-    meta, x_ref, pa_ref, pb_ref, g_ref, fa_ref, fb_ref, ga_ref, gb_ref, gx_ref, vec_ref,
-    outk_ref, outs_ref, gink_ref, gins_ref, sums_ref, osc, isc,
-):
+    )(meta, rowtab, slottab, h1, gq, gk, gv, *w_attn)
+
+
+def emit_kernel(meta, x0, x1, pa0, pa1, pb0, pb1, g0, g1, fk_ref, fr_ref, vec_ref, outk_ref, outs_ref, sums_ref):
     y, c, length = meta[0], meta[1], meta[2]
     step = pl.program_id(0)
 
@@ -661,32 +655,65 @@
     def _():
         sums_ref[...] = jnp.zeros_like(sums_ref)
 
-    _, x1 = middle_rows(x_ref[...], pa_ref[...], pb_ref[...], vec_ref, valid_rows(step * TB, TB, length))
-    f = fa_ref[...].astype(F32) + fb_ref[...].astype(F32) + vec_ref[6:7, :]
-    osc[...] = x1 + vec_ref[12:13, :] * f
+    valid = valid_rows(step * TB, TB, length)
+    outs = []
+    for col, (x, pa, pb, g) in enumerate(((x0, pa0, pb0, g0), (x1, pa1, pb1, g1))):
+        off = pl.ds(pl.multiple_of((col * 2 + c) * CW, CW), CW)
+        here = slice(col * CW, (col + 1) * CW)
+        a = (pa[...].astype(F32) + pb[...].astype(F32) + vec_ref[3:4, off]) * valid
+        middle = x[...].astype(F32) + vec_ref[9:10, off] * a
+        f = fk_ref[:, here].astype(F32) + fr_ref[:, here].astype(F32) + vec_ref[6:7, off]
+        outs.append((middle + vec_ref[12:13, off] * f).astype(BF))
+        sums_ref[0:1, here] += jnp.sum(g[...].astype(F32) * f, axis=0, keepdims=True)
+    outk_ref[...] = jnp.where(y == 0, outs[0].astype(F32), outs[1].astype(F32)).astype(BF)
+    outs_ref[...] = jnp.where(y == 0, outs[1].astype(F32), outs[0].astype(F32)).astype(BF)
+
+
+def column_specs():
+    return [pl.BlockSpec((TB, CW), lambda i, meta, col=col: (i, 2 * col + meta[1])) for col in range(2)]
+
+
+def emit(meta, x, pa, pb, g, fk, fr, vec):
+    return pl.pallas_call(
+        emit_kernel,
+        out_shape=(jax.ShapeDtypeStruct((LEN, CW), BF),) * 2 + (jax.ShapeDtypeStruct((8, 2 * CW), F32),),
+        grid_spec=pltpu.PrefetchScalarGridSpec(
+            num_scalar_prefetch=1,
+            grid=(NT,),
+            in_specs=column_specs() * 4 + [rows_spec(2 * CW)] * 2 + [whole(vec.shape)],
+            out_specs=(rows_spec(CW),) * 2 + (whole((8, 2 * CW)),),
+        ),
+        compiler_params=params(),
+        cost_estimate=cost(1e7, 8e6),
+        name="emit",
+    )(meta, x, x, pa, pa, pb, pb, g, g, fk, fr, vec)
+
+
+def final_kernel(meta, x_ref, ga_ref, gb_ref, gx0, gx1, vec_ref, gink_ref, gins_ref, sums_ref, isc):
+    y, c = meta[0], meta[1]
+    step = pl.program_id(0)
+
+    @pl.when(step == 0)
+    def _():
+        sums_ref[...] = jnp.zeros_like(sums_ref)
+
     n1, inv = layer_norm(x_ref[...].astype(F32))
     gh1 = ga_ref[...].astype(F32) + gb_ref[...].astype(F32)
     gn = gh1 * (1.0 + vec_ref[8:9, :])
     m0 = jnp.mean(gn, axis=1, keepdims=True)
     m1 = jnp.mean(gn * n1, axis=1, keepdims=True)
-    isc[...] = gx_ref[...] + (gn - m0 - n1 * m1) * inv
+    isc[...] = (gn - m0 - n1 * m1) * inv
     sums_ref[0:1, :] += jnp.sum(gh1, axis=0, keepdims=True)
     sums_ref[1:2, :] += jnp.sum(gh1 * n1, axis=0, keepdims=True)
-    sums_ref[2:3, :] += jnp.sum(g_ref[...].astype(F32) * f, axis=0, keepdims=True)
-    mine = pl.ds(pl.multiple_of((y * 2 + c) * CW, CW), CW)
-    theirs = pl.ds(pl.multiple_of(((1 - y) * 2 + c) * CW, CW), CW)
-    outk_ref[...] = osc[:, mine].astype(BF)
-    outs_ref[...] = osc[:, theirs].astype(BF)
-    gink_ref[...] = isc[:, mine]
-    gins_ref[...] = isc[:, theirs].astype(BF)
-
-
-def final(meta, x, pa, pb, g, fa, fb, ga, gb, gx, vec):
+    grads = [gx[...] + isc[:, pl.ds(pl.multiple_of((col * 2 + c) * CW, CW), CW)] for col, gx in ((0, gx0), (1, gx1))]
+    gink_ref[...] = jnp.where(y == 0, grads[0], grads[1])
+    gins_ref[...] = jnp.where(y == 0, grads[1], grads[0]).astype(BF)
+
+
+def final(meta, x, ga, gb, gx, vec):
     return pl.pallas_call(
         final_kernel,
         out_shape=(
-            jax.ShapeDtypeStruct((LEN, CW), BF),
-            jax.ShapeDtypeStruct((LEN, CW), BF),
             jax.ShapeDtypeStruct((LEN, CW), F32),
             jax.ShapeDtypeStruct((LEN, CW), BF),
             jax.ShapeDtypeStruct((8, D), F32),
@@ -694,14 +721,67 @@
         grid_spec=pltpu.PrefetchScalarGridSpec(
             num_scalar_prefetch=1,
             grid=(NT,),
-            in_specs=[rows_spec(D)] * 9 + [whole(vec.shape)],
-            out_specs=(rows_spec(CW),) * 4 + (whole((8, D)),),
-            scratch_shapes=[pltpu.VMEM((TB, D), F32), pltpu.VMEM((TB, D), F32)],
+            in_specs=[rows_spec(D)] * 3 + column_specs() + [whole(vec.shape)],
+            out_specs=(rows_spec(CW),) * 2 + (whole((8, D)),),
+            scratch_shapes=[pltpu.VMEM((TB, D), F32)],
         ),
         compiler_params=params(),
-        cost_estimate=cost(1e8, 22e6),
+        cost_estimate=cost(1e8, 12e6),
         name="final",
-    )(meta, x, pa, pb, g, fa, fb, ga, gb, gx, vec)
+    )(meta, x, ga, gb, gx, gx, vec)
+
+
+def turn(a, b, contract):
+    return lax.dot_general(
+        a.astype(BF), b.astype(BF), ((contract[:1], contract[1:]), ((), ())), preferred_element_type=F32
+    )
+
+
+def soap_kernel(parts, chained, *refs):
+    grads_in, (w, m1, m2, lb, rb), outs = refs[:parts], refs[parts : parts + 5], refs[parts + 5 + chained :]
+    grad = grads_in[0][0].astype(F32)
+    for extra in grads_in[1:]:
+        grad = grad + extra[0].astype(F32)
+    left, right = lb[0], rb[0]
+    turned = turn(turn(left, grad, (0, 0)), right, (1, 0))
+    first = soap_first * m1[0] + (1.0 - soap_first) * turned
+    second = soap_second * m2[0] + (1.0 - soap_second) * turned * turned
+    direction = first * (1.0 / (1.0 - soap_first**STEP)) / (
+        jnp.sqrt(second * (1.0 / (1.0 - soap_second**STEP))) + soap_epsilon
+    )
+    back = turn(turn(left, direction, (1, 0)), right, (1, 1))
+    new = w[0] - soap_rate * (back + soap_decay * w[0])
+    outs[0][0] = grad
+    outs[1][0] = first
+    outs[2][0] = second
+    outs[3][0] = new
+    outs[4][0] = new.astype(BF)
+
+
+def soap(base, grads, state, chain):
+    count, rows, _ = grads[0].shape
+    total = state[0].shape[0]
+    parts = len(grads)
+    own = pl.BlockSpec((1, rows, CW), lambda i: (i, 0, 0))
+    place = pl.BlockSpec((1, rows, CW), lambda i: (base + i, 0, 0))
+    shape = jax.ShapeDtypeStruct((total, rows, CW), F32)
+    return pl.pallas_call(
+        functools.partial(soap_kernel, parts, len(chain)),
+        out_shape=(shape,) * 4 + (jax.ShapeDtypeStruct((total, rows, CW), BF),),
+        grid=(count,),
+        in_specs=[own] * parts
+        + [place] * 3
+        + [
+            pl.BlockSpec((1, rows, rows), lambda i: (base + i, 0, 0)),
+            pl.BlockSpec((1, CW, CW), lambda i: (base + i, 0, 0)),
+        ]
+        + [ANY] * len(chain),
+        out_specs=(place,) * 5,
+        input_output_aliases={parts + 5 + i: i for i in range(len(chain))},
+        compiler_params=params(),
+        cost_estimate=cost(count * rows * CW * (rows + CW) * 24, count * rows * CW * 34),
+        name="soap",
+    )(*grads, *state, *chain)
 
 
 def xor_pairs(size, step):
@@ -712,18 +792,18 @@
     return lax.ppermute(v, axis, SWAP)
 
 
-def true_blocks(mine, other_y, y, c):
-    cm, cy = swap(mine, "c"), swap(other_y, "c")
-    flip_c = c == 1
-    own0, own1 = jnp.where(flip_c, cm, mine), jnp.where(flip_c, mine, cm)
-    oth0, oth1 = jnp.where(flip_c, cy, other_y), jnp.where(flip_c, other_y, cy)
-    flip_y = y == 1
-    return (
-        jnp.where(flip_y, oth0, own0),
-        jnp.where(flip_y, oth1, own1),
-        jnp.where(flip_y, own0, oth0),
-        jnp.where(flip_y, own1, oth1),
-    )
+def after(value, *deps):
+    return lax.optimization_barrier((value,) + deps)[0]
+
+
+def true_blocks(own, got, y, c):
+    blocks = jnp.stack([own, got], axis=1)
+    blocks = jnp.where(c == 1, blocks[:, ::-1], blocks)
+    return jnp.where(y == 1, blocks[::-1], blocks)
+
+
+def side_by_side(blocks):
+    return jnp.concatenate([blocks[0, 0], blocks[0, 1], blocks[1, 0], blocks[1, 1]], axis=-1)
 
 
 def rotary_tables():
@@ -737,24 +817,33 @@
     return cos, jnp.where(odd, sin, 0.0), jnp.where(odd, 0.0, -sin)
 
 
+LAST = ("x", "x", "y", "y", "x", "x", "y", "y")
+
+
 def body(fast, block_in, out_grad, lengths, group_ids, time_embed, weights, first_moments, second_moments,
          owners, left_basis, right_basis, biases, bias_first, bias_second):
     highest = lax.Precision.HIGHEST
-    rows = weights.shape[0]
     n_dp = owners.shape[1]
     z, x, y, c = (lax.axis_index(name) for name in ("z", "x", "y", "c"))
     dp = z * 2 + x
-    slots = jnp.arange(n_dp, dtype=jnp.int32)
+    by_matrix = lambda v: jnp.transpose(v, (1, 0, 2))
+    weights, first_moments, second_moments = map(by_matrix, (weights, first_moments, second_moments))
+    rows = weights.shape[1]
+
+    columns = jnp.arange(2, dtype=jnp.int32)[None, None, :]
+    holder = owners[:, :, None]
+    yr = jnp.bitwise_xor(columns, y)
     if fast:
-        blocks_of = jnp.bitwise_xor(slots % 4, z) * 2 + jnp.bitwise_xor(slots // 4, x)
-        slot_of = jnp.bitwise_xor(slots // 2, z) + 4 * jnp.bitwise_xor(slots % 2, x)
+        zr = jnp.bitwise_xor(holder // 2, z)
+        xr = jnp.bitwise_xor(holder % 2, x)
+        x_last = jnp.array([name == "x" for name in LAST] + [False] * 6)[:, None, None]
+        slottab = jnp.where(x_last, xr * 8 + yr * 4, yr * 8 + xr * 4) + zr
     else:
-        blocks_of = slots
-        slot_of = slots
-    hits = owners[:, :, None] == blocks_of[None, None, :]
-    rowtab = jnp.sum(jnp.where(hits, slots[None, :, None], 0), axis=1).astype(jnp.int32)
-    slottab = jnp.sum(
-        jnp.where(owners[:, :, None] == slots[None, None, :], slot_of[None, None, :], 0), axis=2
+        slottab = yr * n_dp + holder
+    slottab = slottab.reshape(owners.shape[0], 2 * n_dp).astype(jnp.int32)
+    codes = jnp.arange(2 * n_dp, dtype=jnp.int32)
+    rowtab = jnp.sum(
+        jnp.where(slottab[:, :, None] == codes[None, None, :], codes[None, :, None], 0), axis=1
     ).astype(jnp.int32)
     meta = jnp.stack([y, c, lengths[y]]).astype(jnp.int32)
 
@@ -765,165 +854,168 @@
     ).astype(BF)
     own_weights, mod_part = prep(weights, condk)
 
-    def to_chip(v):
-        mine = lax.dynamic_slice_in_dim(v, y * LEN, LEN, 0)
-        other = lax.dynamic_slice_in_dim(v, (1 - y) * LEN, LEN, 0)
-        return jnp.concatenate(true_blocks(mine, swap(other, "y"), y, c), axis=1)
-
-    def gather(piece):
-        piece = piece[None]
-        if fast:
-            parts = [piece] + [lax.ppermute(piece, "z", xor_pairs(4, s)) for s in (1, 2, 3)]
-            four = jnp.concatenate(parts, axis=0)
-            own = jnp.concatenate([four, swap(four, "x")], axis=0)
-        else:
-            own = lax.all_gather(piece, ("z", "x"), axis=0, tiled=True)
-        return own, swap(own, "y")
-
-    xs = to_chip(block_in)
-    w_attn = gather(own_weights[:4])
-    w_feed = gather(own_weights[4:])
-    gs = to_chip(out_grad)
-
-    if fast:
-        mod_all = mod_part
-        for axis, size, step in (("x", 2, 1), ("z", 4, 1), ("z", 4, 2)):
-            mod_all = mod_all + lax.ppermute(mod_all, axis, xor_pairs(size, step))
-    else:
-        mod_all = lax.psum(mod_part, ("z", "x"))
+    def part(v, index):
+        return lax.dynamic_slice_in_dim(v, index * LEN, LEN, 0)
+
+    def z_stage(pieces):
+        return [lax.ppermute(piece, "z", xor_pairs(4, s + 1)) for s, piece in enumerate(pieces)]
 
     def utterance_rows(index):
         hit = (jnp.arange(GROUPS) == group_ids[index]).astype(F32)
         mods = jnp.sum(mod_all * hit[None, :, None], axis=1) + biases[7:]
         return jnp.concatenate([biases[:7], mods, jnp.zeros((3, CW), F32)], axis=0)
 
-    vec = jnp.concatenate(
-        true_blocks(utterance_rows(y), swap(utterance_rows(1 - y), "y"), y, c), axis=1
-    )
+    both_in = jnp.stack([block_in, out_grad])
+    pair = lambda index: lax.dynamic_slice_in_dim(both_in, index * LEN, LEN, 1)
+    rows_own = jnp.stack([pair(y), swap(pair(1 - y), "y")])
+    if fast:
+        piece = own_weights[None, :4]
+        z_attn = [piece] + z_stage([piece] * 3)
+        mod_all = mod_part + swap(mod_part, "x")
+        for step in (1, 2):
+            mod_all = mod_all + lax.ppermute(mod_all, "z", xor_pairs(4, step))
+    else:
+        mod_all = lax.psum(mod_part, ("z", "x"))
+    vec_own = jnp.stack([utterance_rows(y), swap(utterance_rows(1 - y), "y")])
+    vec_got = swap(vec_own, "c")
+    if fast:
+        four = jnp.concatenate(z_attn, axis=0)
+        four, rows_own, vec_got = lax.optimization_barrier((four, rows_own, vec_got))
+    rows_got = swap(rows_own, "c")
+    if fast:
+        a_got, b_got = swap(four[:, :2], "y"), swap(four[:, 2:], "x")
+        piece = after(own_weights[None, 4:], four)
+        z_feed = [piece] + z_stage([piece] * 3)
+        a_got, b_got, rows_got = lax.optimization_barrier((a_got, b_got, rows_got))
+        eight_a = jnp.concatenate([four[:, :2], a_got], axis=0)
+        eight_b = jnp.concatenate([four[:, 2:], b_got], axis=0)
+        w_attn = (eight_a, swap(eight_a, "x"), eight_b, swap(eight_b, "y"))
+        z_feed, w_attn = lax.optimization_barrier((z_feed, w_attn))
+        four = jnp.concatenate(z_feed, axis=0)
+    else:
+        gathered = [
+            lax.all_gather(own_weights[None, 2 * i : 2 * i + 2], ("z", "x"), axis=0, tiled=True) for i in range(4)
+        ]
+        w_attn = (gathered[0], swap(gathered[0], "y"), gathered[1], swap(gathered[1], "y"))
+
+    rows_both = true_blocks(rows_own, rows_got, y, c)
+    xs = side_by_side(rows_both[:, :, 0])
+    gs = side_by_side(rows_both[:, :, 1])
+    vec = side_by_side(true_blocks(vec_own, vec_got, y, c))
     tables = rotary_tables()
     lane = jnp.arange(128)[None, :]
     padded = (jnp.arange(LEN, dtype=jnp.int32) >= meta[2])[:, None]
     kaug = jnp.where(lane < 3, 1.0, jnp.where((lane == 3) & padded, masked_score, 0.0)).astype(BF)
 
-    h1, q, k, v = qkv(meta, rowtab, xs, vec, tables, *w_attn)
-    o, qaug, pa = attend(meta, rowtab, q, k, v, kaug, *w_attn)
+    if fast:
+        c_got, d_got = swap(four[:, :2], "y"), swap(four[:, 2:], "x")
+    h1, q, k, v = qkv(meta, rowtab, xs, vec, tables, w_attn)
+    if fast:
+        q, c_got, d_got = lax.optimization_barrier((q, c_got, d_got))
+        eight_c = jnp.concatenate([four[:, :2], c_got], axis=0)
+        eight_d = jnp.concatenate([four[:, 2:], d_got], axis=0)
+        w_feed = (eight_c, swap(eight_c, "x"), eight_d, swap(eight_d, "y"))
+    else:
+        w_feed = (gathered[2], swap(gathered[2], "y"), gathered[3], swap(gathered[3], "y"))
+    o, qaug, pa = attend(meta, rowtab, q, k, v, kaug, *w_attn[2:])
+    pa, w_feed = lax.optimization_barrier((pa, w_feed))
     pb = swap(pa, "c")
-    fa, g2a, gb_feed, keep_feed, send_feed = feed(meta, rowtab, slottab, xs, pa, pb, gs, vec, *w_feed)
+    pfk, pfs, g2a, gb_feed, keep_c, send_c, keep_d, send_d = feed(
+        meta, rowtab, slottab, xs, pa, pb, gs, vec, w_feed
+    )
     g2b = swap(g2a, "c")
-    fb = swap(fa, "c")
-
-    def scatter(keep, send):
-        got = swap(send, "y")
-        if fast:
-            total = keep.astype(F32) + got.astype(F32)
-            low = total[4:].astype(BF)
-            four = total[:4] + swap(low, "x").astype(F32)
-            own = four[0]
-            for s in (1, 2, 3):
-                own = own + lax.ppermute(four[s].astype(BF), "z", xor_pairs(4, s)).astype(F32)
-            return own
-        total = (keep.astype(F32) + got.astype(F32)).astype(BF)
-        return lax.psum_scatter(total, ("z", "x"), scatter_dimension=0, tiled=True)[0].astype(F32)
-
-    grads_feed = scatter(keep_feed, send_feed)
-    gx, go, sums_mid, keep_proj, send_proj = proj_back(
-        meta, rowtab, slottab, xs, pa, pb, gs, g2a, g2b, o, vec, *w_attn
+
+    def second_stage(keep, got, axis):
+        total = keep.astype(F32) + got.astype(F32)
+        if not fast:
+            return lax.psum_scatter(total.astype(BF), ("z", "x"), scatter_dimension=0, tiled=True)[0], None
+        return total[:4], swap(total[4:].astype(BF), axis)
+
+    def third_stage(*states):
+        if not fast:
+            return [jnp.concatenate([state[0] for state in states], axis=0)]
+        total = jnp.concatenate([keep + got.astype(F32) for keep, got in states], axis=1)
+        low = total.astype(BF)
+        return [total[0]] + z_stage([low[1], low[2], low[3]])
+
+    first = lambda name: name if fast else "y"
+    got_c, got_d = swap(send_c, first("x")), swap(send_d, "y")
+    gx, go, sums_mid, keep_o, send_o = proj_back(
+        meta, rowtab, slottab, xs, pa, pb, gs, g2a, g2b, o, vec, *w_attn[2:]
     )
-    grads_proj = scatter(keep_proj, send_proj)
+    pfr = swap(after(pfs, g2b), "c")
+    out_keep, out_send, sums_out = emit(meta, xs, pa, pb, gs, pfk, after(pfr, go), vec)
+    go, got_c, got_d, out_send = lax.optimization_barrier((go, got_c, got_d, out_send))
+    state_c = second_stage(keep_c, got_c, "y")
+    state_d = second_stage(keep_d, got_d, "x")
+    got_o = swap(send_o, "y")
     gq, gk, gv, gb_qkv = attend_back(q, k, v, go, o, qaug, kaug, tables)
-    g1a, keep_qkv, send_qkv = qkv_back(meta, rowtab, slottab, h1, gq, gk, gv, *w_attn)
+    gq, state_c, state_d, got_o = lax.optimization_barrier((gq, state_c, state_d, got_o))
+    grads_feed = third_stage(state_c, state_d)
+    state_o = second_stage(keep_o, got_o, "x")
+    out_got = swap(out_send, "y")
+    g1a, keep_a, send_a, keep_v, send_v = qkv_back(meta, rowtab, slottab, h1, gq, gk, gv, w_attn)
+    g1a, state_o, out_got, grads_feed = lax.optimization_barrier((g1a, state_o, out_got, grads_feed))
     g1b = swap(g1a, "c")
-    grads_qkv = scatter(keep_qkv, send_qkv)
-    out_keep, out_send, gin_keep, gin_send, sums_end = final(
-        meta, xs, pa, pb, gs, fa, fb, g1a, g1b, gx, vec
-    )
-    out_got = swap(out_send, "y")
+    got_a, got_v = swap(send_a, first("x")), swap(send_v, "y")
+    gin_keep, gin_send, sums_end = final(meta, xs, g1a, g1b, gx, vec)
     gin_got = swap(gin_send, "y").astype(F32)
 
-    def both(mine, other):
-        return jnp.where(
-            y == 0, jnp.concatenate([mine, other], axis=0), jnp.concatenate([other, mine], axis=0)
-        )
-
-    block_out = both(out_keep, out_got)
-    input_grad = both(gin_keep, gin_got)
-
+    def columns_of(v, col):
+        return lax.dynamic_slice_in_dim(v, (col * 2 + c) * CW, CW, 1)
+
+    tall = jnp.concatenate([sums_mid[3:4], gb_feed[:3], sums_end[:2], sums_mid[:3]], axis=0)
+    hot = jnp.broadcast_to((jnp.arange(CW) == group_ids[y]).astype(F32)[None], (3, CW))
     local = jnp.stack(
         [
             jnp.concatenate(
                 [
                     gb_qkv[:3, col * CW : (col + 1) * CW],
-                    lax.dynamic_slice_in_dim(
-                        jnp.concatenate(
-                            [sums_mid[3:4], gb_feed[:3], sums_end[:2], sums_mid[:3], sums_end[2:3]], axis=0
-                        ),
-                        (col * 2 + c) * CW,
-                        CW,
-                        1,
-                    ),
+                    columns_of(tall, col),
+                    sums_out[:1, col * CW : (col + 1) * CW],
+                    hot,
                 ],
                 axis=0,
             )
             for col in range(2)
         ]
     )
-    hot = (jnp.arange(CW) == group_ids[y]).astype(F32)
-    local = jnp.concatenate([local, jnp.broadcast_to(hot[None, None], (2, 3, CW))], axis=1)
     mine = jnp.where(y == 0, local[0], local[1])
     other = jnp.where(y == 0, local[1], local[0])
     vecs = jnp.stack([mine, swap(other, "y")])
     if fast:
-        everything = [vecs]
-        for zs in range(4):
-            for xstep in range(2):
-                if zs or xstep:
-                    everything.append(
-                        lax.ppermute(
-                            vecs,
-                            ("z", "x"),
-                            [(i * 2 + j, (i ^ zs) * 2 + (j ^ xstep)) for i in range(4) for j in range(2)],
-                        )
-                    )
-        everything = jnp.concatenate(everything, axis=0)
+        vecs = jnp.concatenate([vecs, swap(vecs, "x")], axis=0)
+        for step in (1, 2):
+            vecs = jnp.concatenate([vecs, lax.ppermute(vecs, "z", xor_pairs(4, step))], axis=0)
     else:
-        everything = lax.all_gather(vecs, ("z", "x"), axis=0, tiled=True)
-    bias_grad = jnp.sum(everything[:, :13], axis=0)
-    grouped = jnp.einsum("ug,ukc->kgc", everything[:, 13, :GROUPS], everything[:, 7:13], precision=highest)
+        vecs = lax.all_gather(vecs, ("z", "x"), axis=0, tiled=True)
+
+    state = (weights, first_moments, second_moments, left_basis, right_basis)
+    chain = soap(4, grads_feed, state, ())
+    got_a, got_v, vecs, gin_got, chain = lax.optimization_barrier((got_a, got_v, vecs, gin_got, chain))
+    state_a = second_stage(keep_a, got_a, "y")
+    state_v = second_stage(keep_v, got_v, "x")
+    bias_grad = jnp.sum(vecs[:, :13], axis=0)
+    grouped = jnp.einsum("ug,ukc->kgc", vecs[:, 13, :GROUPS], vecs[:, 7:13], precision=highest)
     grads_mod = jnp.einsum("kgr,kgc->krc", condk.astype(F32), grouped, precision=highest)
-    reduced = jnp.concatenate([grads_qkv, grads_proj, grads_feed, grads_mod], axis=0)
-
-    turned = jnp.einsum("kij,kic->kjc", left_basis, reduced, precision=highest)
-    turned = jnp.einsum("kjc,kce->kje", turned, right_basis, precision=highest)
-    first_old = jnp.transpose(first_moments, (1, 0, 2))
-    second_old = jnp.transpose(second_moments, (1, 0, 2))
-    first_new = soap_first * first_old + (1.0 - soap_first) * turned
-    second_new = soap_second * second_old + (1.0 - soap_second) * turned * turned
-    direction = (
-        first_new
-        / (1.0 - soap_first**STEP)
-        / (jnp.sqrt(second_new / (1.0 - soap_second**STEP)) + soap_epsilon)
-    )
-    rotated_back = jnp.einsum("kij,kje->kie", left_basis, direction, precision=highest)
-    rotated_back = jnp.einsum("kie,kce->ikc", rotated_back, right_basis, precision=highest)
-    new_weights = weights - soap_rate * (rotated_back + soap_decay * weights)
+    chain = soap(8, [grads_mod], state, chain)
+    state_a, state_v, chain = lax.optimization_barrier((state_a, state_v, chain))
+    grads_attn = third_stage(state_a, state_v, state_o)
+    chain = soap(0, grads_attn, state, chain)
+
+    def both(mine, other):
+        return jnp.where(
+            y == 0, jnp.concatenate([mine, other], axis=0), jnp.concatenate([other, mine], axis=0)
+        )
+
+    block_out = both(out_keep, out_got)
+    input_grad = both(gin_keep, gin_got)
     bias_first_new = vector_first * bias_first + (1.0 - vector_first) * bias_grad
     bias_second_new = vector_second * bias_second + (1.0 - vector_second) * bias_grad * bias_grad
     new_biases = biases - vector_rate * (bias_first_new / (1.0 - vector_first**STEP)) / (
         jnp.sqrt(bias_second_new / (1.0 - vector_second**STEP)) + vector_epsilon
     )
-    back = lambda v: jnp.transpose(v, (1, 0, 2))
-    return (
-        block_out,
-        input_grad,
-        back(reduced),
-        back(first_new),
-        back(second_new),
-        new_weights,
-        new_weights.astype(BF),
-        bias_first_new,
-        bias_second_new,
-        new_biases,
-    )
+    return (block_out, input_grad) + tuple(map(by_matrix, chain)) + (bias_first_new, bias_second_new, new_biases)
 
 
 def solution(mesh):

time: 531 us -> 373 us (0.70)
  waiting for transfers between devices: 213 us -> 84.5 us
  local copies, waits for them, and re-layouts: 47.9 us -> 22.5 us
  Pallas kernels: 150 us -> 165 us
  matrix products: 16 us -> 1.65 us
    ppermute x26 -> x31, waiting for transfers between devices: 121 us -> 37.1 us  [swap(): return lax.ppermute(v, axis, SWAP)]
    ppermute x25 -> x16, waiting for transfers between devices: 92.5 us -> 47.4 us  [the longest x12 24 us: z_stage(): lax.ppermute(piece, 'z', xor_pairs(4, s + 1))]
    pallas_call x2 -> x6, Pallas kernels: 47.6 us -> 67.5 us  [the longest x1 34.5 us: feed(): pl.pallas_call(feed_kernel, out_shape=(part, part, jax.ShapeDtypeStruct((...]
    dot_general x5 -> x1, matrix products: 15.5 us -> 0.23 us  [body(): jnp.einsum('ug,ukc->kgc', vecs[:, 13, :GROUPS], vecs[:, 7:13], precision=...]
    unnamed x89 -> x88, local copies, waits for them, and re-layouts: 19.2 us -> 7.55 us
    ppermute x26 -> x31, starting transfers between devices: 20.4 us -> 30.9 us  [swap(): return lax.ppermute(v, axis, SWAP)]
    ppermute x25 -> x16, starting transfers between devices: 29.6 us -> 22.2 us  [the longest x12 18.6 us: z_stage(): lax.ppermute(piece, 'z', xor_pairs(4, s + 1))]
    add x9 -> x13, other arithmetic: 7.94 us -> 12.1 us  [the longest x5 7.59 us: second_stage(): total = keep.astype(F32) + got.astype(F32)]
  transfers between devices with their start and end apart: 51 -> 47, of which waited for: 22 -> 20; matrix products, arithmetic and copies ran while one was open for 17% -> 12% of each run, Pallas kernels for 21% -> 33%
where the time goes in v2:
time: 373 us; the launch traced here: 366 us
  Pallas kernels  165 us (44%)
  waiting for transfers between devices  84.5 us (23%)
  starting transfers between devices  53.1 us (14%)
  other arithmetic  37 us (10%)
  local copies, waits for them, and re-layouts  22.5 us (6%)
    ppermute x31, waiting for transfers between devices, swap(): return lax.ppermute(v, axis, SWAP)  37.1 us
    pallas_call x1, Pallas kernels, feed(): pl.pallas_call(feed_kernel, out_shape=(part, part, jax.ShapeDtypeStruct((...  34.5 us
    ppermute x31, starting transfers between devices, swap(): return lax.ppermute(v, axis, SWAP)  30.9 us
    pallas_call x1, Pallas kernels, attend_back(): pl.pallas_call(attend_back_kernel, out_shape=(jax.ShapeDtypeStruct((LEN,...  28.7 us
    pallas_call x1, Pallas kernels, attend(): pl.pallas_call(attend_kernel, out_shape=(jax.ShapeDtypeStruct((LEN, half)...  24.9 us
    ppermute x12, waiting for transfers between devices, z_stage(): lax.ppermute(piece, 'z', xor_pairs(4, s + 1))  24 us
    pallas_call x3, Pallas kernels, soap(): pl.pallas_call(functools.partial(soap_kernel, parts, len(chain)), out_sha...  18.7 us
    ppermute x12, starting transfers between devices, z_stage(): lax.ppermute(piece, 'z', xor_pairs(4, s + 1))  18.6 us
  transfers between devices with their start and end apart: 47, of which 20 were waited for; matrix products, arithmetic and copies ran while one was open for 12% of the time, Pallas kernels for 33%

profile of v2, /device:TPU:0, one launch (start us, length us, event | category | flops | bytes accessed | tf_op | source)
XLA Modules:
  0.0 365.5 jit_solution(16063244711302039173)
XLA Ops:
  3.2 2.4 prep.1
  5.6 1.8 slice_bitcast_fusion.17
  7.4 5.0 %collective-permute-start.2 = (bf16[1,4,128,256]{3,2,1,0:T(8,128)(2,1)}, bf16[1,4,128,256]{3,2,1,0:T(8,128)(2,1)}, u32[]{:S(2)}, u32[]{:S(2)}) collective-permute-start(bf16[1,4,128,256]{3,2,1,0:T(8,128)(2,1)} %get-tuple-element.268), channel_id=1, source_target_pairs={{0,24},{8,16},{16,8},{24,0},{1,25},{9,17},{17,9},{25,1},{2,26},{10... | collective-permute-start | bytes 786440 | tf_op jit(solution)/shard_map/ppermute | solution.py:861
  13.0 1.7 collective-permute-start.4
  15.9 1.5 collective-permute-start.3
  21.2 9.4 %collective-permute-done.5 = f32[6,8,256]{2,1,0:T(8,128)S(1)} collective-permute-done((f32[6,8,256]{2,1,0:T(8,128)S(1)}, f32[6,8,256]{2,1,0:T(8,128)S(1)}, u32[]{:S(2)}, u32[]{:S(2)}) %collective-permute-start.5) | collective-permute-done | bytes 49184 | tf_op jit(solution)/shard_map/ppermute | solution.py:876
  33.3 3.3 collective-permute-done.6
  36.8 1.5 collective-permute-start.7
  42.1 1.4 pad_maximum_fusion.2
  48.1 3.2 collective-permute-start.14
  51.3 1.5 collective-permute-start.10
  54.8 10.2 %collective-permute-done.10 = bf16[4,2,128,256]{3,2,1,0:T(8,128)(2,1)S(1)} collective-permute-done((bf16[4,2,128,256]{3,2,1,0:T(8,128)(2,1)S(1)}, bf16[4,2,128,256]{3,2,1,0:T(8,128)(2,1)S(1)}, u32[]{:S(2)}, u32[]{:S(2)}) %collective-permute-start.10) | collective-permute-done | bytes 524320 | tf_op jit(solution)/shard_map/ppermute | solution.py:792
  71.4 1.6 slice_bitcast_fusion
  74.3 3.3 collective-permute-done.12
  77.7 12.2 %collective-permute-done.16.b1.wb = bf16[8,2,128,256]{3,2,1,0:T(8,128)(2,1)S(1)} collective-permute-done((bf16[8,2,128,256]{3,2,1,0:T(8,128)(2,1)S(1)}, bf16[8,2,128,256]{3,2,1,0:T(8,128)(2,1)S(1)}, u32[]{:S(2)}, u32[]{:S(2)}) %collective-permute-start.16) | collective-permute-done | bytes 1048608 | tf_op jit(solution)/shard_map/ppermute | solution.py:792
  93.9 1.6 pad_maximum_fusion.3.x_ref.x0.x1
  95.5 11.0 %qkv.1 = (bf16[1024,1024]{1,0:T(8,128)(2,1)}, bf16[1024,512]{1,0:T(8,128)(2,1)}, bf16[1024,512]{1,0:T(8,128)(2,1)}, bf16[1024,512]{1,0:T(8,128)(2,1)}) custom-call(s32[3]{0:T(128)} %pad_add_fusion.meta, s32[14,16]{1,0:T(8,128)} %select_reduce_fusion.rowtab, bf16[1024,1024]{1,0:T(8,128)(2,1)} %pad_maximum_fusion.3.x_ref.x0.x1, ...), custom_call_target="tpu_custom_call" | custom-call | flops 3221225472 | bytes 12000000 | tf_op jit(solution)/shard_map/qkv/pallas_call | solution.py:191
  109.1 24.9 %attend.1 = (bf16[1024,512]{1,0:T(8,128)(2,1)}, bf16[8,1024,128]{2,1,0:T(8,128)(2,1)}, bf16[1024,1024]{1,0:T(8,128)(2,1)}) custom-call(s32[3]{0:T(128)} %pad_add_fusion.meta, s32[14,16]{1,0:T(8,128)} %select_reduce_fusion.rowtab, bf16[1024,512]{1,0:T(8,128)(2,1)} %get-tuple-element.141.q_ref, bf16[1024,512]{1,0:T(8,128)(2,1)} %get-tuple-element.142.k_ref, ...), custom_call_target="tpu_custom_call" | custom-call | flops 12000000000 | bytes 10000000 | tf_op jit(solution)/shard_map/attend/pallas_call | solution.py:263
  134.2 1.7 slice_bitcast_fusion.6
  135.8 1.6 pad_maximum_fusion.4.g_ref.g0.g1
  139.8 34.5 %feed.1 = (bf16[1024,512]{1,0:T(8,128)(2,1)}, bf16[1024,512]{1,0:T(8,128)(2,1)}, bf16[1024,1024]{1,0:T(8,128)(2,1)}, f32[8,1024]{1,0:T(8,128)}, bf16[8,2,128,256...) custom-call(s32[3]{0:T(128)} %pad_add_fusion.meta, ...), custom_call_target="tpu_custom_call" | custom-call | flops 12884901888 | bytes 24000000 | tf_op jit(solution)/shard_map/feed/pallas_call | solution.py:395
  174.6 4.2 %collective-permute-done.22.gb_ref = bf16[1024,1024]{1,0:T(8,128)(2,1)S(1)} collective-permute-done((bf16[1024,1024]{1,0:T(8,128)(2,1)}, bf16[1024,1024]{1,0:T(8,128)(2,1)S(1)}, u32[]{:S(2)}, u32[]{:S(2)}) %collective-permute-start.22) | collective-permute-done | bytes 2097184 | tf_op jit(solution)/shard_map/ppermute | solution.py:792
  180.9 14.9 %proj_back.1 = (f32[1024,1024]{1,0:T(8,128)}, bf16[1024,512]{1,0:T(8,128)(2,1)}, f32[8,1024]{1,0:T(8,128)}, bf16[8,1,128,256]{3,2,1,0:T(8,128)(2,1)}, bf16[8,1,128,256]{3,2,1,0:T(8,128)(2,1)}) custom-call(s32[3]{0:T(128)} %pad_add_fusion.meta, s32[14,16]{1,0:T(8,128)} %select_reduce_fusion.rowtab, s32[14,16]{1,0:T(8,128)} %copy-done.27, ...), custom_call_target="tpu_custom_call" | custom-call | flops 2147483648 | bytes 20000000 | tf_op jit(solution)/shard_map/proj_back/pallas_call | solution.py:478
  198.1 6.1 %emit.1 = (bf16[1024,256]{1,0:T(8,128)(2,1)}, bf16[1024,256]{1,0:T(8,128)(2,1)}, f32[8,512]{1,0:T(8,128)}) custom-call(s32[3]{0:T(128)} %pad_add_fusion.meta, bf16[1024,1024]{1,0:T(8,128)(2,1)} %pad_maximum_fusion.3.x_ref.x0.x1, bf16[1024,1024]{1,0:T(8,128)(2,1)} %pad_maximum_fusion.3.x_ref.x0.x1, bf16[1024,1024]{1,0:T(8,128)(2,1)} %get-tuple-element.147.pa_ref.pa0.pa1, ...), custom_call_target="tpu_custom_call" | custom-call | flops 10000000 | bytes 8000000 | tf_op jit(solution)/shard_map/emit/pallas_call | solution.py:677
  204.7 1.8 collective-permute-done.25
  206.5 1.5 convert_add_fusion.2
  208.1 1.9 copy-done.16
  210.0 1.5 convert_add_fusion.1
  214.6 28.7 %attend_back.1 = (bf16[1024,512]{1,0:T(8,128)(2,1)}, bf16[1024,512]{1,0:T(8,128)(2,1)}, bf16[1024,512]{1,0:T(8,128)(2,1)}, f32[8,512]{1,0:T(8,128)}) custom-call(bf16[1024,512]{1,0:T(8,128)(2,1)} %get-tuple-element.141.q_ref, bf16[1024,512]{1,0:T(8,128)(2,1)} %get-tuple-element.142.k_ref, bf16[1024,512]{1,0:T(8,128)(2,1)} %get-tuple-element.143.v_ref, ...), custom_call_target="tpu_custom_call" | custom-call | flops 30000001024 | bytes 12000000 | tf_op jit(solution)/shard_map/attend_back/pallas_call | solution.py:560
  243.4 1.5 convert_add_fusion.7
  249.5 3.0 collective-permute-start.33
  253.9 15.2 %qkv_back.1 = (bf16[1024,1024]{1,0:T(8,128)(2,1)}, bf16[8,2,128,256]{3,2,1,0:T(8,128)(2,1)}, bf16[8,2,128,256]{3,2,1,0:T(8,128)(2,1)}, bf16[8,1,128,256]{3,2,1,0:T(8,128)(2,1)}, bf16[8,1,128,256]{3,2,1,0:T(8,128)(2,1)}) custom-call(s32[3]{0:T(128)} %pad_add_fusion.meta, s32[14,16]{1,0:T(8,128)} %select_reduce_fusion.rowtab, s32[14,16]{1,0:T(8,128)} %copy-done.27, ...), custom_call_target="tpu_custom_call" | custom-call | flops 6442450944 | bytes 16000000 | tf_op jit(solution)/shard_map/qkv_back/pallas_call | solution.py:628
  270.0 2.7 collective-permute-done.32.refs_2_
  278.1 8.1 %final.1 = (f32[1024,256]{1,0:T(8,128)}, bf16[1024,256]{1,0:T(8,128)(2,1)}, f32[8,1024]{1,0:T(8,128)}) custom-call(s32[3]{0:T(128)} %pad_add_fusion.meta, bf16[1024,1024]{1,0:T(8,128)(2,1)} %pad_maximum_fusion.3.x_ref.x0.x1, bf16[1024,1024]{1,0:T(8,128)(2,1)} %get-tuple-element.184.ga_ref, bf16[1024,1024]{1,0:T(8,128)(2,1)} %collective-permute-done.34.gb_ref, ...), custom_call_target="tpu_custom_call" | custom-call | flops 100000000 | bytes 12000000 | tf_op jit(solution)/shard_map/final/pallas_call | solution.py:714
  288.4 2.4 collective-permute-done.37
  291.9 5.6 %soap.3 = (f32[14,128,256]{2,1,0:T(8,128)}, f32[14,128,256]{2,1,0:T(8,128)}, f32[14,128,256]{2,1,0:T(8,128)}, f32[14,128,256]{2,1,0:T(8,128)}, bf16[14,128,256]{2,1,0:T(8,128)(2,1)}) custom-call(f32[4,128,256]{2,1,0:T(8,128)} %fusion.5.refs_0_, bf16[4,128,256]{2,1,0:T(8,128)(2,1)} %collective-permute-done.31.refs_1_, ...), custom_call_target="tpu_custom_call" | custom-call | flops 1207959552 | bytes 4456448 | tf_op jit(solution)/shard_map/soap/pallas_call | solution.py:768
  298.9 2.2 collective-permute-done.38
  301.1 4.2 %collective-permute-done.39 = f32[4,16,256]{2,1,0:T(8,128)S(1)} collective-permute-done((f32[4,16,256]{2,1,0:T(8,128)S(1)}, f32[4,16,256]{2,1,0:T(8,128)S(1)}, u32[]{:S(2)}, u32[]{:S(2)}) %collective-permute-start.39) | collective-permute-done | bytes 65568 | tf_op jit(solution)/shard_map/ppermute | solution.py:989
  306.3 6.5 %collective-permute-done.40 = f32[8,16,256]{2,1,0:T(8,128)S(1)} collective-permute-done((f32[8,16,256]{2,1,0:T(8,128)S(1)}, f32[8,16,256]{2,1,0:T(8,128)S(1)}, u32[]{:S(2)}, u32[]{:S(2)}) %collective-permute-start.40) | collective-permute-done | bytes 131104 | tf_op jit(solution)/shard_map/ppermute | solution.py:989
  313.0 1.6 convert_add_fusion.4
  318.3 1.5 convert_add_fusion
  322.0 7.5 %soap.4 = (f32[14,128,256]{2,1,0:T(8,128)}, f32[14,128,256]{2,1,0:T(8,128)}, f32[14,128,256]{2,1,0:T(8,128)}, f32[14,128,256]{2,1,0:T(8,128)}, bf16[14,128,256]{2,1,0:T(8,128)(2,1)}) custom-call(f32[6,128,256]{2,1,0:T(8,128)} %fusion.33.refs_0_, ...), custom_call_target="tpu_custom_call", output_to_operand_aliasing={{0}: (6, {}), {1}: (7, {}), {2}: (8, {}), {3}: (9, {}), {4}... | custom-call | flops 1811939328 | bytes 6684672 | tf_op jit(solution)/shard_map/soap/pallas_call | solution.py:768
  330.9 1.6 maximum_select_fusion
  336.2 2.4 collective-permute-start.46
  338.7 2.0 collective-permute-start.44
  341.7 5.6 %collective-permute-done.46.refs_3_ = bf16[4,128,256]{2,1,0:T(8,128)(2,1)S(1)} collective-permute-done((bf16[4,128,256]{2,1,0:T(8,128)(2,1)S(1)}, bf16[4,128,256]{2,1,0:T(8,128)(2,1)S(1)}, u32[]{:S(2)}, u32[]{:S(2)}) %collective-permute-start.46) | collective-permute-done | bytes 262176 | tf_op jit(solution)/shard_map/ppermute | solution.py:861
  347.3 11.0 %collective-permute-done.45.refs_2_ = bf16[4,128,256]{2,1,0:T(8,128)(2,1)S(1)} collective-permute-done((bf16[4,128,256]{2,1,0:T(8,128)(2,1)S(1)}, bf16[4,128,256]{2,1,0:T(8,128)(2,1)S(1)}, u32[]{:S(2)}, u32[]{:S(2)}) %collective-permute-start.45) | collective-permute-done | bytes 262176 | tf_op jit(solution)/shard_map/ppermute | solution.py:861
  359.8 5.5 %soap.5 = (f32[14,128,256]{2,1,0:T(8,128)}, f32[14,128,256]{2,1,0:T(8,128)}, f32[14,128,256]{2,1,0:T(8,128)}, f32[14,128,256]{2,1,0:T(8,128)}, bf16[14,128,256]{2,1,0:T(8,128)(2,1)}) custom-call(f32[4,128,256]{2,1,0:T(8,128)} %slice_bitcast_fusion.2.refs_0_, ...), custom_call_target="tpu_custom_call", output_to_operand_aliasing={{0}: (9, {}), {1}: (10, {}), {2}: (11, {}), {3}: (12, {}), ... | custom-call | flops 1207959552 | bytes 4456448 | tf_op jit(solution)/shard_map/soap/pallas_call | solution.py:768
  (275 shorter events, 77.0 us)
Async XLA Ops:
  7.4 33.3 %collective-permute-start.2 = (bf16[1,4,128,256]{3,2,1,0:T(8,128)(2,1)}, bf16[1,4,128,256]{3,2,1,0:T(8,128)(2,1)}, u32[]{:S(2)}, u32[]{:S(2)}) collective-permute-start(bf16[1,4,128,256]{3,2,1,0:T(8,128)(2,1)} %get-tuple-element.268), channel_id=1, source_target_pairs={{0,24},{8,16},{16,8},{24,0},{1,25},{9,17},{17,9},{25,1},{2,26},{10... | collective-permute-start | bytes 786440 | tf_op jit(solution)/shard_map/ppermute | solution.py:861
  12.4 28.3 %collective-permute-start.1 = (bf16[1,4,128,256]{3,2,1,0:T(8,128)(2,1)}, bf16[1,4,128,256]{3,2,1,0:T(8,128)(2,1)}, u32[]{:S(2)}, u32[]{:S(2)}) collective-permute-start(bf16[1,4,128,256]{3,2,1,0:T(8,128)(2,1)} %get-tuple-element.268), channel_id=1, source_target_pairs={{0,16},{8,24},{16,0},{24,8},{1,17},{9,25},{17,1},{25,9},{2,18},{10... | collective-permute-start | bytes 786440 | tf_op jit(solution)/shard_map/ppermute | solution.py:861
  12.4 28.3 %collective-permute-start = (bf16[1,4,128,256]{3,2,1,0:T(8,128)(2,1)}, bf16[1,4,128,256]{3,2,1,0:T(8,128)(2,1)}, u32[]{:S(2)}, u32[]{:S(2)}) collective-permute-start(bf16[1,4,128,256]{3,2,1,0:T(8,128)(2,1)} %get-tuple-element.268), channel_id=1, source_target_pairs={{0,8},{8,0},{16,24},{24,16},{1,9},{9,1},{17,25},{25,17},{2,10},{10... | collective-permute-start | bytes 786440 | tf_op jit(solution)/shard_map/ppermute | solution.py:861
  13.0 5.6 %collective-permute-start.4 = (f32[6,8,256]{2,1,0:T(8,128)}, f32[6,8,256]{2,1,0:T(8,128)S(1)}, u32[]{:S(2)}, u32[]{:S(2)}) collective-permute-start(f32[6,8,256]{2,1,0:T(8,128)} %get-tuple-element.124), channel_id=1, source_target_pairs={{0,4},{4,0},{1,5},{5,1},{2,6},{6,2},{3,7},{7,3},{8,12},{12,8},{9,1... | collective-permute-start | bytes 147464 | tf_op jit(solution)/shard_map/ppermute | solution.py:792
  15.9 26.2 %collective-permute-start.3 = (bf16[2,1024,256]{2,1,0:T(8,128)(2,1)}, bf16[2,1024,256]{2,1,0:T(8,128)(2,1)}, u32[]{:S(2)}, u32[]{:S(2)}) collective-permute-start(bf16[2,1024,256]{2,1,0:T(8,128)(2,1)} %get-tuple-element.254), channel_id=1, source_target_pairs={{0,2},{2,0},{1,3},{3,1},{4,6},{6,4},{5,7},{7,5},{8,10},{10,8},{9,1... | collective-permute-start | bytes 3145736 | tf_op jit(solution)/shard_map/ppermute | solution.py:792
  18.6 12.0 %collective-permute-start.5 = (f32[6,8,256]{2,1,0:T(8,128)S(1)}, f32[6,8,256]{2,1,0:T(8,128)S(1)}, u32[]{:S(2)}, u32[]{:S(2)}) collective-permute-start(f32[6,8,256]{2,1,0:T(8,128)S(1)} %add.181), channel_id=1, source_target_pairs={{0,8},{8,0},{16,24},{24,16},{1,9},{9,1},{17,25},{25,17},{2,10},{10... | collective-permute-start | bytes 147464 | tf_op jit(solution)/shard_map/ppermute | solution.py:876
  30.6 5.9 %collective-permute-start.6 = (f32[6,8,256]{2,1,0:T(8,128)S(1)}, f32[6,8,256]{2,1,0:T(8,128)S(1)}, u32[]{:S(2)}, u32[]{:S(2)}) collective-permute-start(f32[6,8,256]{2,1,0:T(8,128)S(1)} %add.182), channel_id=1, source_target_pairs={{0,16},{8,24},{16,0},{24,8},{1,17},{9,25},{17,1},{25,9},{2,18},{10... | collective-permute-start | bytes 147464 | tf_op jit(solution)/shard_map/ppermute | solution.py:876
  36.8 3.9 %collective-permute-start.7 = (f32[16,256]{1,0:T(8,128)S(1)}, f32[16,256]{1,0:T(8,128)S(1)}, u32[]{:S(2)}, u32[]{:S(2)}) collective-permute-start(f32[16,256]{1,0:T(8,128)S(1)} %get-tuple-element.288), channel_id=1, source_target_pairs={{0,2},{2,0},{1,3},{3,1},{4,6},{6,4},{5,7},{7,5},{8,10},{10,8},{9,1... | collective-permute-start | bytes 49160 | tf_op jit(solution)/shard_map/ppermute | solution.py:792
  40.6 2.9 collective-permute-start.8
  43.5 22.5 %collective-permute-start.11 = (bf16[2,2,1024,256]{3,2,0,1:T(8,128)(2,1)S(1)}, bf16[2,2,1024,256]{3,2,0,1:T(8,128)(2,1)S(1)}, u32[]{:S(2)}, u32[]{:S(2)}) collective-permute-start(bf16[2,2,1024,256]{3,2,0,1:T(8,128)(2,1)S(1)} %pad_maximum_fusion.2), channel_id=1, source_target_pairs={{0,1},{1,0},{2,3},{3,2},{4,5},{5,4},{6,7},{7,6},{8,9},{9,8},{10,11... | collective-permute-start | bytes 6291464 | tf_op jit(solution)/shard_map/ppermute | solution.py:792
  48.1 24.9 %collective-permute-start.14 = (bf16[1,4,128,256]{3,2,1,0:T(8,128)(2,1)S(1)}, bf16[1,4,128,256]{3,2,1,0:T(8,128)(2,1)S(1)}, u32[]{:S(2)}, u32[]{:S(2)}) collective-permute-start(bf16[1,4,128,256]{3,2,1,0:T(8,128)(2,1)S(1)} %get-tuple-element.137), channel_id=1, source_target_pairs={{0,24},{8,16},{16,8},{24,0},{1,25},{9,17},{17,9},{25,1},{2,26},{10... | collective-permute-start | bytes 786440 | tf_op jit(solution)/shard_map/ppermute | solution.py:861
  51.3 23.1 %collective-permute-start.13 = (bf16[1,4,128,256]{3,2,1,0:T(8,128)(2,1)S(1)}, bf16[1,4,128,256]{3,2,1,0:T(8,128)(2,1)S(1)}, u32[]{:S(2)}, u32[]{:S(2)}) collective-permute-start(bf16[1,4,128,256]{3,2,1,0:T(8,128)(2,1)S(1)} %get-tuple-element.137), channel_id=1, source_target_pairs={{0,16},{8,24},{16,0},{24,8},{1,17},{9,25},{17,1},{25,9},{2,18},{10... | collective-permute-start | bytes 786440 | tf_op jit(solution)/shard_map/ppermute | solution.py:861
  51.3 13.6 %collective-permute-start.10 = (bf16[4,2,128,256]{3,2,1,0:T(8,128)(2,1)S(1)}, bf16[4,2,128,256]{3,2,1,0:T(8,128)(2,1)S(1)}, u32[]{:S(2)}, u32[]{:S(2)}) collective-permute-start(bf16[4,2,128,256]{3,2,1,0:T(8,128)(2,1)S(1)} %get-tuple-element.263), channel_id=1, source_target_pairs={{0,4},{4,0},{1,5},{5,1},{2,6},{6,2},{3,7},{7,3},{8,12},{12,8},{9,1... | collective-permute-start | bytes 1572872 | tf_op jit(solution)/shard_map/ppermute | solution.py:792
  52.8 13.2 %collective-permute-start.9 = (bf16[4,2,128,256]{3,2,1,0:T(8,128)(2,1)S(1)}, bf16[4,2,128,256]{3,2,1,0:T(8,128)(2,1)S(1)}, u32[]{:S(2)}, u32[]{:S(2)}) collective-permute-start(bf16[4,2,128,256]{3,2,1,0:T(8,128)(2,1)S(1)} %get-tuple-element.264), channel_id=1, source_target_pairs={{0,2},{2,0},{1,3},{3,1},{4,6},{6,4},{5,7},{7,5},{8,10},{10,8},{9,1... | collective-permute-start | bytes 1572872 | tf_op jit(solution)/shard_map/ppermute | solution.py:792
  65.0 12.7 %collective-permute-start.12 = (bf16[1,4,128,256]{3,2,1,0:T(8,128)(2,1)S(1)}, bf16[1,4,128,256]{3,2,1,0:T(8,128)(2,1)S(1)}, u32[]{:S(2)}, u32[]{:S(2)}) collective-permute-start(bf16[1,4,128,256]{3,2,1,0:T(8,128)(2,1)S(1)} %get-tuple-element.137), channel_id=1, source_target_pairs={{0,8},{8,0},{16,24},{24,16},{1,9},{9,1},{17,25},{25,17},{2,10},{10... | collective-permute-start | bytes 786440 | tf_op jit(solution)/shard_map/ppermute | solution.py:861
  66.3 23.6 %collective-permute-start.16 = (bf16[8,2,128,256]{3,2,1,0:T(8,128)(2,1)S(1)}, bf16[8,2,128,256]{3,2,1,0:T(8,128)(2,1)S(1)}, u32[]{:S(2)}, u32[]{:S(2)}) collective-permute-start(bf16[8,2,128,256]{3,2,1,0:T(8,128)(2,1)S(1)} %pad_maximum_fusion.8.b0.wa), channel_id=1, source_target_pairs={{0,2},{2,0},{1,3},{3,1},{4,6},{6,4},{5,7},{7,5},{8,10},{10,8},{9,1... | collective-permute-start | bytes 3145736 | tf_op jit(solution)/shard_map/ppermute | solution.py:792
  67.7 23.3 %collective-permute-start.15 = (bf16[8,2,128,256]{3,2,1,0:T(8,128)(2,1)S(1)}, bf16[8,2,128,256]{3,2,1,0:T(8,128)(2,1)S(1)}, u32[]{:S(2)}, u32[]{:S(2)}) collective-permute-start(bf16[8,2,128,256]{3,2,1,0:T(8,128)(2,1)S(1)} %pad_maximum_fusion.7.a0), channel_id=1, source_target_pairs={{0,4},{4,0},{1,5},{5,1},{2,6},{6,2},{3,7},{7,3},{8,12},{12,8},{9,1... | collective-permute-start | bytes 3145736 | tf_op jit(solution)/shard_map/ppermute | solution.py:792
  91.9 14.7 %collective-permute-start.18 = (bf16[4,2,128,256]{3,2,1,0:T(8,128)(2,1)S(1)}, bf16[4,2,128,256]{3,2,1,0:T(8,128)(2,1)S(1)}, u32[]{:S(2)}, u32[]{:S(2)}) collective-permute-start(bf16[4,2,128,256]{3,2,1,0:T(8,128)(2,1)S(1)} %get-tuple-element.261), channel_id=1, source_target_pairs={{0,4},{4,0},{1,5},{5,1},{2,6},{6,2},{3,7},{7,3},{8,12},{12,8},{9,1... | collective-permute-start | bytes 1572872 | tf_op jit(solution)/shard_map/ppermute | solution.py:792
  93.1 13.5 %collective-permute-start.17 = (bf16[4,2,128,256]{3,2,1,0:T(8,128)(2,1)S(1)}, bf16[4,2,128,256]{3,2,1,0:T(8,128)(2,1)S(1)}, u32[]{:S(2)}, u32[]{:S(2)}) collective-permute-start(bf16[4,2,128,256]{3,2,1,0:T(8,128)(2,1)S(1)} %get-tuple-element.262), channel_id=1, source_target_pairs={{0,2},{2,0},{1,3},{3,1},{4,6},{6,4},{5,7},{7,5},{8,10},{10,8},{9,1... | collective-permute-start | bytes 1572872 | tf_op jit(solution)/shard_map/ppermute | solution.py:792
  106.7 27.3 %copy-start.12 = (bf16[8,2,128,256]{3,2,1,0:T(8,128)(2,1)}, bf16[8,2,128,256]{3,2,1,0:T(8,128)(2,1)S(1)}, u32[]{:S(2)}) copy-start(bf16[8,2,128,256]{3,2,1,0:T(8,128)(2,1)S(1)} %pad_maximum_fusion.9.c0) | copy-start | bytes 3145732
  106.8 27.2 %collective-permute-start.20 = (bf16[8,2,128,256]{3,2,1,0:T(8,128)(2,1)S(1)}, bf16[8,2,128,256]{3,2,1,0:T(8,128)(2,1)}, u32[]{:S(2)}, u32[]{:S(2)}) collective-permute-start(bf16[8,2,128,256]{3,2,1,0:T(8,128)(2,1)S(1)} %pad_maximum_fusion.10.d0), channel_id=1, source_target_pairs={{0,2},{2,0},{1,3},{3,1},{4,6},{6,4},{5,7},{7,5},{8,10},{10,8},{9,1... | collective-permute-start | bytes 3145736 | tf_op jit(solution)/shard_map/ppermute | solution.py:792
  108.2 25.8 %collective-permute-start.19 = (bf16[8,2,128,256]{3,2,1,0:T(8,128)(2,1)S(1)}, bf16[8,2,128,256]{3,2,1,0:T(8,128)(2,1)}, u32[]{:S(2)}, u32[]{:S(2)}) collective-permute-start(bf16[8,2,128,256]{3,2,1,0:T(8,128)(2,1)S(1)} %pad_maximum_fusion.9.c0), channel_id=1, source_target_pairs={{0,4},{4,0},{1,5},{5,1},{2,6},{6,2},{3,7},{7,3},{8,12},{12,8},{9,1... | collective-permute-start | bytes 3145736 | tf_op jit(solution)/shard_map/ppermute | solution.py:792
  134.1 4.4 %collective-permute-start.21 = (bf16[1024,1024]{1,0:T(8,128)(2,1)}, bf16[1024,1024]{1,0:T(8,128)(2,1)S(1)}, u32[]{:S(2)}, u32[]{:S(2)}) collective-permute-start(bf16[1024,1024]{1,0:T(8,128)(2,1)} %get-tuple-element.147.pa_ref.pa0.pa1), channel_id=1, source_target_pairs={{0,1},{1,0},{2,3},{3,2},{4,5},{5,4},{6,7},{7,6},{8,9},{9,8},{10,11... | collective-permute-start | bytes 6291464 | tf_op jit(solution)/shard_map/ppermute | solution.py:792
  174.4 4.4 %collective-permute-start.22 = (bf16[1024,1024]{1,0:T(8,128)(2,1)}, bf16[1024,1024]{1,0:T(8,128)(2,1)S(1)}, u32[]{:S(2)}, u32[]{:S(2)}) collective-permute-start(bf16[1024,1024]{1,0:T(8,128)(2,1)} %get-tuple-element.154.ga_ref), channel_id=1, source_target_pairs={{0,1},{1,0},{2,3},{3,2},{4,5},{5,4},{6,7},{7,6},{8,9},{9,8},{10,11... | collective-permute-start | bytes 6291464 | tf_op jit(solution)/shard_map/ppermute | solution.py:792
  178.8 18.3 %collective-permute-start.23 = (bf16[1024,512]{1,0:T(8,128)(2,1)}, bf16[1024,512]{1,0:T(8,128)(2,1)S(1)}, u32[]{:S(2)}, u32[]{:S(2)}) collective-permute-start(bf16[1024,512]{1,0:T(8,128)(2,1)} %get-tuple-element.155), channel_id=1, source_target_pairs={{0,1},{1,0},{2,3},{3,2},{4,5},{5,4},{6,7},{7,6},{8,9},{9,8},{10,11... | collective-permute-start | bytes 3145736 | tf_op jit(solution)/shard_map/ppermute | solution.py:792
  179.0 25.7 %collective-permute-start.24 = (bf16[8,2,128,256]{3,2,1,0:T(8,128)(2,1)}, bf16[8,2,128,256]{3,2,1,0:T(8,128)(2,1)}, u32[]{:S(2)}, u32[]{:S(2)}) collective-permute-start(bf16[8,2,128,256]{3,2,1,0:T(8,128)(2,1)} %get-tuple-element.161), channel_id=1, source_target_pairs={{0,4},{4,0},{1,5},{5,1},{2,6},{6,2},{3,7},{7,3},{8,12},{12,8},{9,1... | collective-permute-start | bytes 3145736 | tf_op jit(solution)/shard_map/ppermute | solution.py:792
  180.2 26.3 %collective-permute-start.25 = (bf16[8,2,128,256]{3,2,1,0:T(8,128)(2,1)}, bf16[8,2,128,256]{3,2,1,0:T(8,128)(2,1)}, u32[]{:S(2)}, u32[]{:S(2)}) collective-permute-start(bf16[8,2,128,256]{3,2,1,0:T(8,128)(2,1)} %get-tuple-element.162), channel_id=1, source_target_pairs={{0,2},{2,0},{1,3},{3,1},{4,6},{6,4},{5,7},{7,5},{8,10},{10,8},{9,1... | collective-permute-start | bytes 3145736 | tf_op jit(solution)/shard_map/ppermute | solution.py:792
  195.8 47.5 %collective-permute-start.28 = (bf16[8,1,128,256]{3,2,1,0:T(8,128)(2,1)}, bf16[8,1,128,256]{3,2,1,0:T(8,128)(2,1)}, u32[]{:S(2)}, u32[]{:S(2)}) collective-permute-start(bf16[8,1,128,256]{3,2,1,0:T(8,128)(2,1)} %get-tuple-element.171), channel_id=1, source_target_pairs={{0,2},{2,0},{1,3},{3,1},{4,6},{6,4},{5,7},{7,5},{8,10},{10,8},{9,1... | collective-permute-start | bytes 1572872 | tf_op jit(solution)/shard_map/ppermute | solution.py:792
  211.6 58.4 %collective-permute-start.30 = (bf16[1024,256]{1,0:T(8,128)(2,1)}, bf16[1024,256]{1,0:T(8,128)(2,1)S(1)}, u32[]{:S(2)}, u32[]{:S(2)}) collective-permute-start(bf16[1024,256]{1,0:T(8,128)(2,1)} %get-tuple-element.178), channel_id=1, source_target_pairs={{0,2},{2,0},{1,3},{3,1},{4,6},{6,4},{5,7},{7,5},{8,10},{10,8},{9,1... | collective-permute-start | bytes 1572872 | tf_op jit(solution)/shard_map/ppermute | solution.py:792
  212.5 30.9 %collective-permute-start.26 = (bf16[4,2,128,256]{3,2,1,0:T(8,128)(2,1)S(1)}, bf16[4,2,128,256]{3,2,1,0:T(8,128)(2,1)S(1)}, u32[]{:S(2)}, u32[]{:S(2)}) collective-permute-start(bf16[4,2,128,256]{3,2,1,0:T(8,128)(2,1)S(1)} %slice.302), channel_id=1, source_target_pairs={{0,2},{2,0},{1,3},{3,1},{4,6},{6,4},{5,7},{7,5},{8,10},{10,8},{9,1... | collective-permute-start | bytes 1572872 | tf_op jit(solution)/shard_map/ppermute | solution.py:792
  213.7 29.6 %collective-permute-start.27 = (bf16[4,2,128,256]{3,2,1,0:T(8,128)(2,1)S(1)}, bf16[4,2,128,256]{3,2,1,0:T(8,128)(2,1)S(1)}, u32[]{:S(2)}, u32[]{:S(2)}) collective-permute-start(bf16[4,2,128,256]{3,2,1,0:T(8,128)(2,1)S(1)} %slice.301), channel_id=1, source_target_pairs={{0,4},{4,0},{1,5},{5,1},{2,6},{6,2},{3,7},{7,3},{8,12},{12,8},{9,1... | collective-permute-start | bytes 1572872 | tf_op jit(solution)/shard_map/ppermute | solution.py:792
  246.0 24.0 %collective-permute-start.29 = (bf16[4,1,128,256]{3,2,1,0:T(8,128)(2,1)}, bf16[4,1,128,256]{3,2,1,0:T(8,128)(2,1)}, u32[]{:S(2)}, u32[]{:S(2)}) collective-permute-start(bf16[4,1,128,256]{3,2,1,0:T(8,128)(2,1)} %slice.304), channel_id=1, source_target_pairs={{0,4},{4,0},{1,5},{5,1},{2,6},{6,2},{3,7},{7,3},{8,12},{12,8},{9,1... | collective-permute-start | bytes 786440 | tf_op jit(solution)/shard_map/ppermute | solution.py:792
  249.5 20.5 %collective-permute-start.33 = (bf16[4,128,256]{2,1,0:T(8,128)(2,1)}, bf16[4,128,256]{2,1,0:T(8,128)(2,1)S(1)}, u32[]{:S(2)}, u32[]{:S(2)}) collective-permute-start(bf16[4,128,256]{2,1,0:T(8,128)(2,1)} %get-tuple-element.258), channel_id=1, source_target_pairs={{0,24},{8,16},{16,8},{24,0},{1,25},{9,17},{17,9},{25,1},{2,26},{10... | collective-permute-start | bytes 786440 | tf_op jit(solution)/shard_map/ppermute | solution.py:861
  252.5 20.2 %collective-permute-start.32 = (bf16[4,128,256]{2,1,0:T(8,128)(2,1)}, bf16[4,128,256]{2,1,0:T(8,128)(2,1)}, u32[]{:S(2)}, u32[]{:S(2)}) collective-permute-start(bf16[4,128,256]{2,1,0:T(8,128)(2,1)} %get-tuple-element.259), channel_id=1, source_target_pairs={{0,16},{8,24},{16,0},{24,8},{1,17},{9,25},{17,1},{25,9},{2,18},{10... | collective-permute-start | bytes 786440 | tf_op jit(solution)/shard_map/ppermute | solution.py:861
  252.5 20.2 %collective-permute-start.31 = (bf16[4,128,256]{2,1,0:T(8,128)(2,1)}, bf16[4,128,256]{2,1,0:T(8,128)(2,1)}, u32[]{:S(2)}, u32[]{:S(2)}) collective-permute-start(bf16[4,128,256]{2,1,0:T(8,128)(2,1)} %get-tuple-element.260), channel_id=1, source_target_pairs={{0,8},{8,0},{16,24},{24,16},{1,9},{9,1},{17,25},{25,17},{2,10},{10... | collective-permute-start | bytes 786440 | tf_op jit(solution)/shard_map/ppermute | solution.py:861
  272.7 5.3 %collective-permute-start.34 = (bf16[1024,1024]{1,0:T(8,128)(2,1)}, bf16[1024,1024]{1,0:T(8,128)(2,1)}, u32[]{:S(2)}, u32[]{:S(2)}) collective-permute-start(bf16[1024,1024]{1,0:T(8,128)(2,1)} %get-tuple-element.184.ga_ref), channel_id=1, source_target_pairs={{0,1},{1,0},{2,3},{3,2},{4,5},{5,4},{6,7},{7,6},{8,9},{9,8},{10,11... | collective-permute-start | bytes 6291464 | tf_op jit(solution)/shard_map/ppermute | solution.py:792
  274.1 38.9 %collective-permute-start.36 = (bf16[8,1,128,256]{3,2,1,0:T(8,128)(2,1)}, bf16[8,1,128,256]{3,2,1,0:T(8,128)(2,1)}, u32[]{:S(2)}, u32[]{:S(2)}) collective-permute-start(bf16[8,1,128,256]{3,2,1,0:T(8,128)(2,1)} %get-tuple-element.188), channel_id=1, source_target_pairs={{0,2},{2,0},{1,3},{3,1},{4,6},{6,4},{5,7},{7,5},{8,10},{10,8},{9,1... | collective-permute-start | bytes 1572872 | tf_op jit(solution)/shard_map/ppermute | solution.py:792
  274.9 38.1 %collective-permute-start.35 = (bf16[8,2,128,256]{3,2,1,0:T(8,128)(2,1)}, bf16[8,2,128,256]{3,2,1,0:T(8,128)(2,1)S(1)}, u32[]{:S(2)}, u32[]{:S(2)}) collective-permute-start(bf16[8,2,128,256]{3,2,1,0:T(8,128)(2,1)} %get-tuple-element.187), channel_id=1, source_target_pairs={{0,4},{4,0},{1,5},{5,1},{2,6},{6,2},{3,7},{7,3},{8,12},{12,8},{9,1... | collective-permute-start | bytes 3145736 | tf_op jit(solution)/shard_map/ppermute | solution.py:792
  287.0 3.8 %collective-permute-start.37 = (f32[16,256]{1,0:T(8,128)S(1)}, f32[16,256]{1,0:T(8,128)S(1)}, u32[]{:S(2)}, u32[]{:S(2)}) collective-permute-start(f32[16,256]{1,0:T(8,128)S(1)} %fusion.13), channel_id=1, source_target_pairs={{0,2},{2,0},{1,3},{3,1},{4,6},{6,4},{5,7},{7,5},{8,10},{10,8},{9,1... | collective-permute-start | bytes 49160 | tf_op jit(solution)/shard_map/ppermute | solution.py:792
  290.8 10.3 %collective-permute-start.38 = (f32[2,16,256]{2,1,0:T(8,128)S(1)}, f32[2,16,256]{2,1,0:T(8,128)S(1)}, u32[]{:S(2)}, u32[]{:S(2)}) collective-permute-start(f32[2,16,256]{2,1,0:T(8,128)S(1)} %pad_maximum_fusion.17), channel_id=1, source_target_pairs={{0,4},{4,0},{1,5},{5,1},{2,6},{6,2},{3,7},{7,3},{8,12},{12,8},{9,1... | collective-permute-start | bytes 98312 | tf_op jit(solution)/shard_map/ppermute | solution.py:792
  297.6 15.3 %collective-permute-start.41 = (bf16[1024,256]{1,0:T(8,128)(2,1)S(1)}, bf16[1024,256]{1,0:T(8,128)(2,1)S(1)}, u32[]{:S(2)}, u32[]{:S(2)}) collective-permute-start(bf16[1024,256]{1,0:T(8,128)(2,1)S(1)} %copy-done.39), channel_id=1, source_target_pairs={{0,2},{2,0},{1,3},{3,1},{4,6},{6,4},{5,7},{7,5},{8,10},{10,8},{9,1... | collective-permute-start | bytes 1572872 | tf_op jit(solution)/shard_map/ppermute | solution.py:792
  301.1 4.3 %collective-permute-start.39 = (f32[4,16,256]{2,1,0:T(8,128)S(1)}, f32[4,16,256]{2,1,0:T(8,128)S(1)}, u32[]{:S(2)}, u32[]{:S(2)}) collective-permute-start(f32[4,16,256]{2,1,0:T(8,128)S(1)} %pad_maximum_fusion.15), channel_id=1, source_target_pairs={{0,8},{8,0},{16,24},{24,16},{1,9},{9,1},{17,25},{25,17},{2,10},{10... | collective-permute-start | bytes 196616 | tf_op jit(solution)/shard_map/ppermute | solution.py:989
  305.4 7.4 %collective-permute-start.40 = (f32[8,16,256]{2,1,0:T(8,128)S(1)}, f32[8,16,256]{2,1,0:T(8,128)S(1)}, u32[]{:S(2)}, u32[]{:S(2)}) collective-permute-start(f32[8,16,256]{2,1,0:T(8,128)S(1)} %pad_maximum_fusion.11), channel_id=1, source_target_pairs={{0,16},{8,24},{16,0},{24,8},{1,17},{9,25},{17,1},{25,9},{2,18},{10... | collective-permute-start | bytes 393224 | tf_op jit(solution)/shard_map/ppermute | solution.py:989
  315.4 17.0 %collective-permute-start.43 = (bf16[4,1,128,256]{3,2,1,0:T(8,128)(2,1)}, bf16[4,1,128,256]{3,2,1,0:T(8,128)(2,1)}, u32[]{:S(2)}, u32[]{:S(2)}) collective-permute-start(bf16[4,1,128,256]{3,2,1,0:T(8,128)(2,1)} %slice.303), channel_id=1, source_target_pairs={{0,4},{4,0},{1,5},{5,1},{2,6},{6,2},{3,7},{7,3},{8,12},{12,8},{9,1... | collective-permute-start | bytes 786440 | tf_op jit(solution)/shard_map/ppermute | solution.py:792
  320.7 13.1 %collective-permute-start.42 = (bf16[4,2,128,256]{3,2,1,0:T(8,128)(2,1)}, bf16[4,2,128,256]{3,2,1,0:T(8,128)(2,1)}, u32[]{:S(2)}, u32[]{:S(2)}) collective-permute-start(bf16[4,2,128,256]{3,2,1,0:T(8,128)(2,1)} %slice.300), channel_id=1, source_target_pairs={{0,2},{2,0},{1,3},{3,1},{4,6},{6,4},{5,7},{7,5},{8,10},{10,8},{9,1... | collective-permute-start | bytes 1572872 | tf_op jit(solution)/shard_map/ppermute | solution.py:792
  336.2 11.1 %collective-permute-start.46 = (bf16[4,128,256]{2,1,0:T(8,128)(2,1)S(1)}, bf16[4,128,256]{2,1,0:T(8,128)(2,1)S(1)}, u32[]{:S(2)}, u32[]{:S(2)}) collective-permute-start(bf16[4,128,256]{2,1,0:T(8,128)(2,1)S(1)} %get-tuple-element.255), channel_id=1, source_target_pairs={{0,24},{8,16},{16,8},{24,0},{1,25},{9,17},{17,9},{25,1},{2,26},{10... | collective-permute-start | bytes 786440 | tf_op jit(solution)/shard_map/ppermute | solution.py:861
  338.6 19.7 %collective-permute-start.45 = (bf16[4,128,256]{2,1,0:T(8,128)(2,1)S(1)}, bf16[4,128,256]{2,1,0:T(8,128)(2,1)S(1)}, u32[]{:S(2)}, u32[]{:S(2)}) collective-permute-start(bf16[4,128,256]{2,1,0:T(8,128)(2,1)S(1)} %get-tuple-element.256), channel_id=1, source_target_pairs={{0,16},{8,24},{16,0},{24,8},{1,17},{9,25},{17,1},{25,9},{2,18},{10... | collective-permute-start | bytes 786440 | tf_op jit(solution)/shard_map/ppermute | solution.py:861
  338.7 19.7 %collective-permute-start.44 = (bf16[4,128,256]{2,1,0:T(8,128)(2,1)S(1)}, bf16[4,128,256]{2,1,0:T(8,128)(2,1)S(1)}, u32[]{:S(2)}, u32[]{:S(2)}) collective-permute-start(bf16[4,128,256]{2,1,0:T(8,128)(2,1)S(1)} %get-tuple-element.257), channel_id=1, source_target_pairs={{0,8},{8,0},{16,24},{24,16},{1,9},{9,1},{17,25},{25,17},{2,10},{10... | collective-permute-start | bytes 786440 | tf_op jit(solution)/shard_map/ppermute | solution.py:861
  (45 other events, 276.4 us)
